TPU v7x, 32 devices: a whole 2x2x4 slice. The times are simulated.
32 devices in a mesh: energy: 2 (over x), slab: 8 (over z, y), row: 2 (over core).
Axes of the slice: x: 2, y: 2, z: 4, core: 2. Of those that a mesh axis runs over, the one named last changes fastest.
Arguments:
- green_blocks: bfloat16 [2, 12288, 768], P(None, ('energy', 'slab', 'row')), parts along dimension 1, may hold values from -3 to 3
- coupling: bfloat16 [2, 1024, 128], P(None, 'slab'), may hold values from -2 to 2
- source: bfloat16 [2, 12288, 128], P(None, ('energy', 'slab', 'row')), parts along dimension 1, may hold values from -6 to 6
- interior_count: int32 [8], P('slab'), may hold values from 256 to 512, as said below
Outputs:
- solution: float32 [2, 12288, 128], P(None, ('energy', 'slab', 'row')), parts along dimension 1
There are 2 independent parts, one for each index of `energy`. A program takes and returns all parts, laid end to end along the dimension named above; an argument that names none is the same for every part. Nothing has to cross between parts.
Inputs may be any that keep to these rules, and one draw needn't show every extreme that they name: `interior_count`: some slab has exactly 512 live interior orbitals.
All inputs are finite; a program needn't handle non-finite values.
Results may differ from a plain program's by a relative error of at most 0.0095.
Values may be sent and summed in bfloat16 or wider, within the bound.
No kernel may reach another device: no remote copies, remote signals or barrier semaphores. Data moves between devices by JAX's collectives and lax.ppermute only.
A program may use at most 128 MiB of HBM per device.

v0:
```python
import jax
import jax.numpy as jnp
from jax import lax
from jax.experimental import pallas as pl
from jax.experimental.pallas import tpu as pltpu
from jax.sharding import PartitionSpec as P


F32 = jnp.float32
BF16 = jnp.bfloat16
GROUP = 4
FF, FL, LF, LL, BN = range(5)


def contract(x, matrix, across):
    return lax.dot_general(
        x, matrix, (((1,), (1 if across else 0,)), ((), ())), preferred_element_type=F32
    )


def split(x):
    high = x.astype(BF16)
    return high, (x - high.astype(F32)).astype(BF16)


def apply(real_form, x, across=True):
    high, low = split(x)
    both = contract(jnp.concatenate([high, low], axis=0), real_form, across)
    return both[: x.shape[0]] + both[x.shape[0] :]


def apply_short(real_form, x, across=True):
    return contract(x.astype(BF16), real_form, across)


def turned(x):
    half = x.shape[1] // 2
    return jnp.concatenate([-x[:, half:], x[:, :half]], axis=1)


def stacked(x):
    return jnp.concatenate([x, turned(x)], axis=0)


def apply_computed(columns, x):
    high, low = split(stacked(columns))
    x_high, x_low = split(x)
    both = contract(jnp.concatenate([x_high, x_low], axis=0), high, False)
    return both[: x.shape[0]] + both[x.shape[0] :] + contract(x_high, low, False)


def pack_kernel(green, coupling, source, edge, pack, source_near, sems):
    row = lax.axis_index("row")
    shard_rows, width = green.shape[1:]
    surface = edge.shape[1]
    rows = pl.ds(pl.multiple_of(row * (shard_rows - surface), surface), surface)
    last = pl.ds(width - surface, surface)
    copies = [
        pltpu.make_async_copy(green.at[:, rows, pl.ds(0, surface)], pack.at[pl.ds(0, 2)], sems.at[0]),
        pltpu.make_async_copy(green.at[:, rows, last], pack.at[pl.ds(2, 2)], sems.at[1]),
        pltpu.make_async_copy(coupling.at[pl.ds(row, 1)], pack.at[pl.ds(4, 1)], sems.at[2]),
        pltpu.make_async_copy(green.at[:, rows], edge, sems.at[3]),
        pltpu.make_async_copy(source, source_near, sems.at[4]),
    ]
    for c in copies:
        c.start()
    for c in copies:
        c.wait()


def masked_source(count, own, other, surface):
    row = lax.axis_index("row")
    orbitals = 2 * own.shape[1]

    def masked(part):
        mine, theirs = own[part].astype(F32), other[part].astype(F32)
        whole = jnp.concatenate(
            [jnp.where(row == 0, mine, theirs), jnp.where(row == 0, theirs, mine)], axis=0
        )
        orbital = lax.broadcasted_iota(jnp.int32, whole.shape, 0)
        live = (orbital < surface + count[:1]) | (orbital >= orbitals - surface)
        return jnp.where(live, whole, 0.0)

    real, imag = masked(0), masked(1)
    return (
        jnp.concatenate([real, imag], axis=1).astype(BF16),
        jnp.concatenate([-imag, real], axis=1).astype(BF16),
    )


def edge_kernel(count, edge, edge_other, source_own, source_other, vectors):
    row = lax.axis_index("row")
    surface = edge.shape[1]
    columns = source_own.shape[2]
    half = columns // 2
    above, below = masked_source(count, source_own, source_other, surface)

    def surface_rows(blocks):
        x = contract(blocks[0], above, False) + contract(blocks[1], below, False)
        whole = jnp.concatenate([x[:, :columns].T, x[:, columns:].T], axis=1)
        return jnp.where(row == 0, whole[:half], whole[half:]).astype(BF16)

    own, other = surface_rows(edge), surface_rows(edge_other)

    @pl.when(row == 0)
    def _():
        vectors[:half] = own
        vectors[half:] = other

    @pl.when(row == 1)
    def _():
        vectors[:half] = other
        vectors[half:] = own


def direct_kernel(count, green, source_own, source_other, surfaces, direct):
    above, below = masked_source(count, source_own, source_other, surfaces.shape[1] // 2)
    direct[...] = contract(green[0], above, False) + contract(green[1], below, False)


def unit_columns(size):
    eye = (
        lax.broadcasted_iota(jnp.int32, (size, size), 0)
        == lax.broadcasted_iota(jnp.int32, (size, size), 1)
    ).astype(F32)
    return jnp.concatenate([eye, jnp.zeros_like(eye)], axis=1)


def solve_kernel(*refs):
    edge, edge_other, coupling = refs[:3]
    packs = refs[3 : 3 + 2 * (GROUP - 1)]
    given = refs[3 + len(packs) : 3 + len(packs) + GROUP]
    maps, send, here, after, last_term, leaving, entering, vectors, states, backs = refs[
        3 + len(packs) + GROUP :
    ]
    row = lax.axis_index("row")
    slab = lax.axis_index("slab")
    slabs = lax.axis_size("slab")
    member = slab % GROUP
    size = coupling.shape[1]
    width = edge.shape[2]
    half = vectors.shape[1] // 2

    def put(slot, name, re, im):
        maps[slot, name, :size, :size] = re
        maps[slot, name, :size, size:] = -im
        maps[slot, name, size:, :size] = im
        maps[slot, name, size:, size:] = re

    def put_coupling(slot, re, im):
        known = slab - member + slot < slabs - 1
        put(slot, BN, jnp.where(known, re, jnp.zeros_like(re)), jnp.where(known, im, jnp.zeros_like(im)))

    def fill(first_is_own):
        f, l = (edge, edge_other) if first_is_own else (edge_other, edge)
        for name, ref, start in ((FF, f, 0), (FL, f, width - size), (LF, l, 0), (LL, l, width - size)):
            put(member, name, ref[0, :, start : start + size], ref[1, :, start : start + size])
        put_coupling(member, coupling[0], coupling[1])
        for k in range(1, GROUP):
            mine, other = packs[2 * k - 2], packs[2 * k - 1]
            f, l = (mine, other) if first_is_own else (other, mine)
            slot = member ^ k
            put(slot, FF, f[0], f[1])
            put(slot, FL, f[2], f[3])
            put(slot, LF, l[0], l[1])
            put(slot, LL, l[2], l[3])
            put_coupling(slot, f[4], l[4])

    @pl.when(row == 0)
    def _():
        fill(True)

    @pl.when(row == 1)
    def _():
        fill(False)

    for k, v in enumerate(given):
        vectors[member ^ k] = v[...]
    first = [vectors[i, :half] for i in range(GROUP)]
    last = [vectors[i, half:].astype(F32) for i in range(GROUP)]
    unit = unit_columns(size)
    nothing = jnp.zeros_like(unit)

    def beside(x, below=nothing):
        return jnp.concatenate([x, below], axis=0)

    w = apply_short(maps[GROUP - 1, BN], unit)
    w = apply(maps[GROUP - 1, BN], apply_short(maps[GROUP - 1, LL], w), False)
    last_term[...] = w
    terms = [
        last[i] + apply(maps[i, LL], apply_short(maps[i, BN], first[i + 1]))
        for i in range(GROUP - 1)
    ] + [last[GROUP - 1]]
    u = beside(jnp.zeros((half, 2 * size), F32), unit)
    for i in range(GROUP):
        states[i] = u
        t = apply(maps[i, LF], u) + beside(terms[i])
        u = apply(maps[i, BN], t, False)
    leaving[...] = u
    s = apply(maps[GROUP - 1, FF], states[GROUP - 1]) + beside(first[GROUP - 1].astype(F32))
    backs[GROUP] = jnp.zeros_like(s)
    backs[GROUP - 1] = s
    for i in reversed(range(GROUP - 1)):
        e = apply(maps[i, FF], states[i]) + beside(first[i].astype(F32))
        s = e + apply(maps[i, FL], apply(maps[i, BN], s))
        backs[i] = s
    entering[...] = s
    left = slab < slabs // 2
    send[:half] = jnp.where(left, u[:half], s[:half]).astype(BF16)
    send[half : 2 * half] = first[0]
    send[2 * half :] = jnp.where(left, w, s[half:]).astype(BF16)
    here[...] = states[member]
    after[...] = backs[member + 1]


def gamma_kernel(maps, gamma, whole, backs):
    member = lax.axis_index("slab") % GROUP
    unit = unit_columns(gamma.shape[0])
    backs[GROUP] = unit
    s = apply(maps[GROUP - 1, FL], apply_short(maps[GROUP - 1, BN], unit))
    backs[GROUP - 1] = s
    for i in reversed(range(GROUP - 1)):
        s = apply(maps[i, FL], apply(maps[i, BN], s))
        backs[i] = s
    whole[...] = s
    gamma[...] = backs[member + 1]


def close_kernel(coupling, leaving, first, seen, last_term, here, after, gamma, out):
    half = first.shape[0]
    left = lax.axis_index("slab") < lax.axis_size("slab") // 2
    there = seen[:half].astype(F32)
    map_form = stacked(seen[2 * half :].astype(F32)).astype(BF16)
    b_re, b_im = coupling[0], coupling[1]
    b = jnp.concatenate(
        [jnp.concatenate([b_re, -b_im], axis=1), jnp.concatenate([b_im, b_re], axis=1)], axis=0
    )

    @pl.when(left)
    def _():
        ahead = seen[half : 2 * half].astype(F32)
        past = leaving[:half] + apply_computed(last_term[...], ahead)
        entry = there + apply(map_form, past, False)
        behind = after[:half] + apply_computed(gamma[...], entry)
        out[:half] = here[:half].astype(BF16)
        out[half:] = apply(b, behind).astype(BF16)

    @pl.when(jnp.logical_not(left))
    def _():
        before = there + apply_short(map_form, first[...], False)
        behind = after[:half] + apply_computed(after[half:], before)
        out[:half] = (here[:half] + apply_computed(here[half:], before)).astype(BF16)
        out[half:] = apply(b, behind).astype(BF16)


def final_kernel(count, green, direct, own, other, result, whole):
    row = lax.axis_index("row")
    shard_rows, width = green.shape[1:]
    half = own.shape[0] // 2
    columns = 2 * half
    surface = own.shape[1] // 2

    def place(first, second):
        for i in range(2):
            whole[i, :half] = first[i * half : (i + 1) * half]
            whole[i, half:] = second[i * half : (i + 1) * half]

    @pl.when(row == 0)
    def _():
        place(own, other)

    @pl.when(row == 1)
    def _():
        place(other, own)

    def product(start, x):
        g = jnp.concatenate(
            [green[0, :, start : start + surface], green[1, :, start : start + surface]], axis=1
        )
        x_re, x_im = x[:, :surface], x[:, surface:]
        form = jnp.concatenate(
            [jnp.concatenate([x_re, -x_im], axis=1), jnp.concatenate([x_im, x_re], axis=1)], axis=0
        )
        return contract(g, form, True)

    total = direct[...] + product(0, whole[0]) + product(width - surface, whole[1])
    orbital = row * shard_rows + lax.broadcasted_iota(jnp.int32, total.shape, 0)
    limit = jnp.concatenate([count[:1]] * (total.shape[1] // count.shape[1]), axis=1)
    live = (orbital < surface + limit) | (orbital >= width - surface)
    total = jnp.where(live, total, 0.0)
    result[0] = total[:, :columns]
    result[1] = total[:, columns:]


V, H = (pl.BlockSpec(memory_space=m) for m in (pltpu.VMEM, pltpu.HBM))


def call(kernel, specs, outs, scratch, *args, keep=False):
    args = [
        pltpu.with_memory_space_constraint(a, s.memory_space)
        for a, s in zip(args, specs, strict=True)
    ]
    kind = jax.ShapeDtypeStruct if keep else pltpu.VMEM
    return pl.pallas_call(
        kernel,
        in_specs=specs,
        out_specs=[V] * len(outs),
        out_shape=[kind(s, d) for s, d in outs],
        scratch_shapes=[pltpu.VMEM(*x) if isinstance(x, tuple) else x for x in scratch],
        compiler_params=pltpu.CompilerParams(vmem_limit_bytes=24 << 20),
    )(*args)


def compute(columns, x):
    size = columns.shape[1] // 2

    def mul(a, b):
        return jnp.dot(a, b, preferred_element_type=F32, precision=lax.Precision.HIGHEST)

    c_re, c_im = columns[:, :size], columns[:, size:]
    x_re, x_im = x[:, :size], x[:, size:]
    return jnp.concatenate([mul(x_re, c_re) - mul(x_im, c_im), mul(x_re, c_im) + mul(x_im, c_re)], axis=1)


def body(green_blocks, coupling, source, interior_count):
    shard_rows = green_blocks.shape[1]
    width = green_blocks.shape[2]
    surface = coupling.shape[1]
    columns = source.shape[2]
    half = columns // 2
    slab = lax.axis_index("slab")
    slabs = lax.axis_size("slab")

    def across(x):
        return lax.ppermute(x, "row", [(0, 1), (1, 0)])

    def partner(x, bit):
        return lax.ppermute(x, "slab", [(i, i ^ bit) for i in range(slabs)])

    square = (surface, 2 * surface)
    joint = (half + surface, 2 * surface)
    edge, pack, source_near = call(
        pack_kernel,
        [H] * 3,
        [
            ((2, surface, width), BF16),
            ((5, surface, surface), BF16),
            (source.shape, BF16),
        ],
        [pltpu.SemaphoreType.DMA((5,))],
        green_blocks,
        coupling,
        source,
    )
    count = jnp.broadcast_to(interior_count.reshape(1, 1), (8, columns))
    source_other = across(source_near)
    edge_other = across(edge)
    packs = [partner(pack, k) for k in range(1, GROUP)]
    (vectors,) = call(
        edge_kernel,
        [V] * 5,
        [((columns, 2 * surface), BF16)],
        [],
        count,
        edge,
        edge_other,
        source_near,
        source_other,
    )
    (direct,) = call(
        direct_kernel,
        [V] * 5,
        [((shard_rows, 2 * columns), F32)],
        [],
        count,
        green_blocks,
        source_near,
        source_other,
        vectors,
    )
    gathered = [partner(vectors, k) for k in range(1, GROUP)]
    both = []
    for p in packs:
        both += [p, across(p)]
    maps, send, here, after, last_term, leaving, entering = call(
        solve_kernel,
        [V] * (3 + len(both) + GROUP),
        [((GROUP, 5, 2 * surface, 2 * surface), BF16), ((columns + surface, 2 * surface), BF16)]
        + [(joint, F32)] * 2
        + [(square, F32)]
        + [(joint, F32)] * 2,
        [
            ((GROUP, columns, 2 * surface), BF16),
            ((GROUP,) + joint, F32),
            ((GROUP + 1,) + joint, F32),
        ],
        edge,
        edge_other,
        coupling,
        *both,
        vectors,
        *gathered,
    )
    gamma, back_whole = call(
        gamma_kernel, [V], [(square, F32), (square, F32)], [((GROUP + 1,) + square, F32)], maps
    )
    first = send[half:columns]
    bit = GROUP
    if 2 * bit < slabs:
        first = first.astype(F32)
        leave, a_map = leaving[:half], leaving[half:]
        back, d_map = entering[:half], entering[half:]
        pi, alpha, sigma, delta = here[:half], here[half:], after[:half], after[half:]
        c_map = back_whole
    while 2 * bit < slabs:
        right = (slab // bit) % 2 == 1

        def sides(own):
            seen = partner(own, bit)
            return jnp.where(right, seen, own), jnp.where(right, own, seen)

        (ax, ay), (cx, cy), (dx, dy) = sides(a_map), sides(c_map), sides(d_map)
        (wx, wy), (fx, fy) = sides(last_term), sides(first)
        (px, py), (qx, qy) = sides(leave), sides(back)
        middle = px + compute(wx, fy)
        entry = qy + compute(dy, middle)
        through = compute(dy, ax)
        pi = pi + jnp.where(right, compute(alpha, middle), 0.0)
        sigma = sigma + jnp.where(right, compute(delta, middle), compute(gamma, entry))
        delta = jnp.where(right, compute(delta, ax), delta + compute(gamma, through))
        alpha = jnp.where(right, compute(alpha, ax), alpha)
        gamma = jnp.where(right, gamma, compute(gamma, cy))
        leave, back = py + compute(ay, middle), qx + compute(cx, entry)
        a_map, c_map, d_map = compute(ay, ax), compute(cx, cy), dx + compute(cx, through)
        last_term, first = wy, fx
        bit *= 2
        if 2 * bit == slabs:
            left = slab < slabs // 2
            parts = [jnp.where(left, leave, back), first, jnp.where(left, last_term, d_map)]
            send = jnp.concatenate(parts, axis=0).astype(BF16)
            first = first.astype(BF16)
            leaving = jnp.concatenate([leave, a_map], axis=0)
            here = jnp.concatenate([pi, alpha], axis=0)
            after = jnp.concatenate([sigma, delta], axis=0)
    seen = partner(send, slabs // 2)
    (closed,) = call(
        close_kernel,
        [V] * 8,
        [((columns, 2 * surface), BF16)],
        [],
        coupling,
        leaving,
        first,
        seen,
        last_term,
        here,
        after,
        gamma,
    )
    (result,) = call(
        final_kernel,
        [V] * 5,
        [((2, shard_rows, columns), F32)],
        [((2, columns, 2 * surface), BF16)],
        count,
        green_blocks,
        direct,
        closed,
        across(closed),
        keep=True,
    )
    return result


def solution(mesh):
    placed = (
        P(None, ("energy", "slab", "row"), None),
        P(None, "slab", None),
        P(None, ("energy", "slab", "row"), None),
        P("slab"),
    )
    return jax.shard_map(
        body,
        mesh=mesh,
        in_specs=placed,
        out_specs=P(None, ("energy", "slab", "row"), None),
        check_vma=False,
    )
```

profile of v0, /device:TPU:0, one launch (start us, length us, event | category | flops | bytes accessed | tf_op | source)
XLA Modules:
  0.0 38.0 jit_solution(6177663108226292275)
XLA Ops:
  0.0 1.2 %shard_map.46 = (bf16[2,128,768]{2,1,0:T(8,128)(2,1)S(1)}, bf16[5,128,128]{2,1,0:T(8,128)(2,1)S(1)}, bf16[2,384,128]{2,1,0:T(8,128)(2,1)S(1)}) custom-call(bf16[2,384,768]{2,1,0:T(8,128)(2,1)} %green.5, bf16[2,128,128]{2,1,0:T(8,128)(2,1)} %coupling.3, bf16[2,384,128]{2,1,0:T(8,128)(2,1)} %source.1), custom_call_target="tpu_custom_call" | custom-call | tf_op jit(solution)/shard_map/pallas_call | solution.py:304
  1.2 0.6 %collective-permute-start.1 = (bf16[2,128,768]{2,1,0:T(8,128)(2,1)S(1)}, bf16[2,128,768]{2,1,0:T(8,128)(2,1)S(1)}, u32[]{:S(2)}, u32[]{:S(2)}) collective-permute-start(bf16[2,128,768]{2,1,0:T(8,128)(2,1)S(1)} %get-tuple-element.16.edge.refs_0_), channel_id=1, source_target_pairs={{0,1},{1,0},{2,3},{3,2},{4,5},{5,4},{6,7},{7,6},{8,9},{9,8},{10,11... | collective-permute-start | bytes 1179656 | tf_op jit(solution)/shard_map/ppermute | solution.py:335
  1.8 3.6 %collective-permute-start.6 = (bf16[5,128,128]{2,1,0:T(8,128)(2,1)S(1)}, bf16[5,128,128]{2,1,0:T(8,128)(2,1)S(1)}, u32[]{:S(2)}, u32[]{:S(2)}) collective-permute-start(bf16[5,128,128]{2,1,0:T(8,128)(2,1)S(1)} %get-tuple-element.17), channel_id=1, source_target_pairs={{0,6},{2,4},{4,2},{6,0},{8,14},{10,12},{12,10},{14,8},{1,7},{3,5},... | collective-permute-start | bytes 491528 | tf_op jit(solution)/shard_map/ppermute | solution.py:338
  5.4 0.4 %collective-permute-start.4 = (bf16[5,128,128]{2,1,0:T(8,128)(2,1)S(1)}, bf16[5,128,128]{2,1,0:T(8,128)(2,1)S(1)}, u32[]{:S(2)}, u32[]{:S(2)}) collective-permute-start(bf16[5,128,128]{2,1,0:T(8,128)(2,1)S(1)} %get-tuple-element.17), channel_id=1, source_target_pairs={{0,4},{2,6},{4,0},{6,2},{8,12},{10,14},{12,8},{14,10},{1,5},{3,7},... | collective-permute-start | bytes 491528 | tf_op jit(solution)/shard_map/ppermute | solution.py:338
  5.8 0.2 collective-permute-start.2
  6.0 4.4 %collective-permute-done.6.refs_7_ = bf16[5,128,128]{2,1,0:T(8,128)(2,1)S(1)} collective-permute-done((bf16[5,128,128]{2,1,0:T(8,128)(2,1)S(1)}, bf16[5,128,128]{2,1,0:T(8,128)(2,1)S(1)}, u32[]{:S(2)}, u32[]{:S(2)}) %collective-permute-start.6) | collective-permute-done | bytes 163872 | tf_op jit(solution)/shard_map/ppermute | solution.py:338
  10.4 3.4 %collective-permute-done.4.refs_5_ = bf16[5,128,128]{2,1,0:T(8,128)(2,1)S(1)} collective-permute-done((bf16[5,128,128]{2,1,0:T(8,128)(2,1)S(1)}, bf16[5,128,128]{2,1,0:T(8,128)(2,1)S(1)}, u32[]{:S(2)}, u32[]{:S(2)}) %collective-permute-start.4) | collective-permute-done | bytes 163872 | tf_op jit(solution)/shard_map/ppermute | solution.py:338
  13.9 0.5 %collective-permute-start.3 = (bf16[5,128,128]{2,1,0:T(8,128)(2,1)S(1)}, bf16[5,128,128]{2,1,0:T(8,128)(2,1)S(1)}, u32[]{:S(2)}, u32[]{:S(2)}) collective-permute-start(bf16[5,128,128]{2,1,0:T(8,128)(2,1)S(1)} %collective-permute-done.2.refs_3_), channel_id=1, source_target_pairs={{0,1},{1,0},{2,3},{3,2},{4,5},{5,4},{6,7},{7,6},{8,9},{9,8},{10,11... | collective-permute-start | bytes 491528 | tf_op jit(solution)/shard_map/ppermute | solution.py:335
  15.1 0.5 %shard_map.47.surfaces.refs_9_ = bf16[128,256]{1,0:T(8,128)(2,1)S(1)} custom-call(s32[8,128]{1,0:T(8,128)S(1)} %broadcast_in_dim.8.count, bf16[2,128,768]{2,1,0:T(8,128)(2,1)S(1)} %get-tuple-element.16.edge.refs_0_, bf16[2,128,768]{2,1,0:T(8,128)(2,1)S(1)} %collective-permute-done.1.edge_other.refs_1_, ...), custom_call_target="tpu_custom_call" | custom-call | tf_op jit(solution)/shard_map/pallas_call | solution.py:304
  15.6 2.0 %collective-permute-start.10 = (bf16[128,256]{1,0:T(8,128)(2,1)S(1)}, bf16[128,256]{1,0:T(8,128)(2,1)S(1)}, u32[]{:S(2)}, u32[]{:S(2)}) collective-permute-start(bf16[128,256]{1,0:T(8,128)(2,1)S(1)} %shard_map.47.surfaces.refs_9_), channel_id=1, source_target_pairs={{0,6},{2,4},{4,2},{6,0},{8,14},{10,12},{12,10},{14,8},{1,7},{3,5},... | collective-permute-start | bytes 196616 | tf_op jit(solution)/shard_map/ppermute | solution.py:338
  17.6 0.5 %collective-permute-start.9 = (bf16[128,256]{1,0:T(8,128)(2,1)S(1)}, bf16[128,256]{1,0:T(8,128)(2,1)S(1)}, u32[]{:S(2)}, u32[]{:S(2)}) collective-permute-start(bf16[128,256]{1,0:T(8,128)(2,1)S(1)} %shard_map.47.surfaces.refs_9_), channel_id=1, source_target_pairs={{0,4},{2,6},{4,0},{6,2},{8,12},{10,14},{12,8},{14,10},{1,5},{3,7},... | collective-permute-start | bytes 196616 | tf_op jit(solution)/shard_map/ppermute | solution.py:338
  18.1 1.1 %collective-permute-start.8 = (bf16[128,256]{1,0:T(8,128)(2,1)S(1)}, bf16[128,256]{1,0:T(8,128)(2,1)S(1)}, u32[]{:S(2)}, u32[]{:S(2)}) collective-permute-start(bf16[128,256]{1,0:T(8,128)(2,1)S(1)} %shard_map.47.surfaces.refs_9_), channel_id=1, source_target_pairs={{0,2},{2,0},{4,6},{6,4},{8,10},{10,8},{12,14},{14,12},{1,3},{3,1},... | collective-permute-start | bytes 196616 | tf_op jit(solution)/shard_map/ppermute | solution.py:338
  19.2 2.0 %collective-permute-done.10.refs_12_ = bf16[128,256]{1,0:T(8,128)(2,1)S(1)} collective-permute-done((bf16[128,256]{1,0:T(8,128)(2,1)S(1)}, bf16[128,256]{1,0:T(8,128)(2,1)S(1)}, u32[]{:S(2)}, u32[]{:S(2)}) %collective-permute-start.10) | collective-permute-done | bytes 65568 | tf_op jit(solution)/shard_map/ppermute | solution.py:338
  21.2 0.7 %collective-permute-done.9.refs_11_ = bf16[128,256]{1,0:T(8,128)(2,1)S(1)} collective-permute-done((bf16[128,256]{1,0:T(8,128)(2,1)S(1)}, bf16[128,256]{1,0:T(8,128)(2,1)S(1)}, u32[]{:S(2)}, u32[]{:S(2)}) %collective-permute-start.9) | collective-permute-done | bytes 65568 | tf_op jit(solution)/shard_map/ppermute | solution.py:338
  21.9 0.4 %collective-permute-done.8.refs_10_ = bf16[128,256]{1,0:T(8,128)(2,1)S(1)} collective-permute-done((bf16[128,256]{1,0:T(8,128)(2,1)S(1)}, bf16[128,256]{1,0:T(8,128)(2,1)S(1)}, u32[]{:S(2)}, u32[]{:S(2)}) %collective-permute-start.8) | collective-permute-done | bytes 65568 | tf_op jit(solution)/shard_map/ppermute | solution.py:338
  22.3 4.2 %shard_map.49 = (bf16[4,5,256,256]{3,2,1,0:T(8,128)(2,1)S(1)}, bf16[256,256]{1,0:T(8,128)(2,1)S(1)}, f32[192,256]{1,0:T(8,128)S(1)}, f32[192,256]{1,0:T(8,128)S(...) custom-call(bf16[2,128,768]{2,1,0:T(8,128)(2,1)S(1)} %get-tuple-element.16.edge.refs_0_, ...), custom_call_target="tpu_custom_call" | custom-call | tf_op jit(solution)/shard_map/pallas_call | solution.py:304
  26.5 2.6 %collective-permute-start.11 = (bf16[256,256]{1,0:T(8,128)(2,1)S(1)}, bf16[256,256]{1,0:T(8,128)(2,1)S(1)}, u32[]{:S(2)}, u32[]{:S(2)}) collective-permute-start(bf16[256,256]{1,0:T(8,128)(2,1)S(1)} %get-tuple-element.19), channel_id=1, source_target_pairs={{0,8},{2,10},{4,12},{6,14},{8,0},{10,2},{12,4},{14,6},{1,9},{3,11}... | collective-permute-start | bytes 393224 | tf_op jit(solution)/shard_map/ppermute | solution.py:338
  29.1 1.9 %shard_map.50 = (f32[128,256]{1,0:T(8,128)S(1)}, f32[128,256]{1,0:T(8,128)}) custom-call(bf16[4,5,256,256]{3,2,1,0:T(8,128)(2,1)S(1)} %get-tuple-element.23.maps), custom_call_target="tpu_custom_call" | custom-call | tf_op jit(solution)/shard_map/pallas_call | solution.py:304
  31.1 4.0 %collective-permute-done.11.seen = bf16[256,256]{1,0:T(8,128)(2,1)S(1)} collective-permute-done((bf16[256,256]{1,0:T(8,128)(2,1)S(1)}, bf16[256,256]{1,0:T(8,128)(2,1)S(1)}, u32[]{:S(2)}, u32[]{:S(2)}) %collective-permute-start.11) | collective-permute-done | bytes 131104 | tf_op jit(solution)/shard_map/ppermute | solution.py:338
  35.0 0.6 %shard_map.51.own = bf16[128,256]{1,0:T(8,128)(2,1)S(1)} custom-call(bf16[2,128,128]{2,1,0:T(8,128)(2,1)S(1)} %copy-done.1, f32[192,256]{1,0:T(8,128)S(1)} %get-tuple-element.18.leaving, bf16[64,256]{1,0:T(8,128)(2,1)S(1)} %slice.3.first, bf16[256,256]{1,0:T(8,128)(2,1)S(1)} %collective-permute-done.11.seen, f32[128,256]{1,0:T(8,128)S(1)} %get-tuple-element.20.last_term, ...), custom_call_target="tpu_custom_call" | custom-call | tf_op jit(solution)/shard_map/pallas_call | solution.py:304
  35.7 0.1 collective-permute-start.12
  35.8 0.5 %shard_map.48.direct = f32[384,256]{1,0:T(8,128)S(1)} custom-call(s32[8,128]{1,0:T(8,128)S(1)} %broadcast_in_dim.8.count, bf16[2,384,768]{2,1,0:T(8,128)(2,1)S(1)} %copy-done, bf16[2,384,128]{2,1,0:T(8,128)(2,1)S(1)} %get-tuple-element.15.source_own, bf16[2,384,128]{2,1,0:T(8,128)(2,1)S(1)} %collective-permute-done.source_other, ...), custom_call_target="tpu_custom_call" | custom-call | tf_op jit(solution)/shard_map/pallas_call | solution.py:304
  36.3 0.7 %collective-permute-done.12.other = bf16[128,256]{1,0:T(8,128)(2,1)S(1)} collective-permute-done((bf16[128,256]{1,0:T(8,128)(2,1)S(1)}, bf16[128,256]{1,0:T(8,128)(2,1)S(1)}, u32[]{:S(2)}, u32[]{:S(2)}) %collective-permute-start.12) | collective-permute-done | bytes 65568 | tf_op jit(solution)/shard_map/ppermute | solution.py:335
  37.0 1.1 %shard_map.52 = f32[2,384,128]{2,1,0:T(8,128)} custom-call(s32[8,128]{1,0:T(8,128)S(1)} %broadcast_in_dim.8.count, bf16[2,384,768]{2,1,0:T(8,128)(2,1)S(1)} %copy-done, f32[384,256]{1,0:T(8,128)S(1)} %shard_map.48.direct, bf16[128,256]{1,0:T(8,128)(2,1)S(1)} %shard_map.51.own, bf16[128,256]{1,0:T(8,128)(2,1)S(1)} %collective-permute-done.12.other), custom_call_target="tpu_custom_call" | custom-call | tf_op jit(solution)/shard_map/pallas_call | solution.py:304
  (15 shorter events, 0.0 us)
Async XLA Ops:
  0.0 22.3 %copy-start.1 = (bf16[2,128,128]{2,1,0:T(8,128)(2,1)S(1)}, bf16[2,128,128]{2,1,0:T(8,128)(2,1)}, u32[]{:S(2)}) copy-start(bf16[2,128,128]{2,1,0:T(8,128)(2,1)} %coupling.3) | copy-start | bytes 196612
  1.2 13.8 %collective-permute-start.1 = (bf16[2,128,768]{2,1,0:T(8,128)(2,1)S(1)}, bf16[2,128,768]{2,1,0:T(8,128)(2,1)S(1)}, u32[]{:S(2)}, u32[]{:S(2)}) collective-permute-start(bf16[2,128,768]{2,1,0:T(8,128)(2,1)S(1)} %get-tuple-element.16.edge.refs_0_), channel_id=1, source_target_pairs={{0,1},{1,0},{2,3},{3,2},{4,5},{5,4},{6,7},{7,6},{8,9},{9,8},{10,11... | collective-permute-start | bytes 1179656 | tf_op jit(solution)/shard_map/ppermute | solution.py:335
  1.8 8.7 %collective-permute-start.6 = (bf16[5,128,128]{2,1,0:T(8,128)(2,1)S(1)}, bf16[5,128,128]{2,1,0:T(8,128)(2,1)S(1)}, u32[]{:S(2)}, u32[]{:S(2)}) collective-permute-start(bf16[5,128,128]{2,1,0:T(8,128)(2,1)S(1)} %get-tuple-element.17), channel_id=1, source_target_pairs={{0,6},{2,4},{4,2},{6,0},{8,14},{10,12},{12,10},{14,8},{1,7},{3,5},... | collective-permute-start | bytes 491528 | tf_op jit(solution)/shard_map/ppermute | solution.py:338
  5.4 8.5 %collective-permute-start.4 = (bf16[5,128,128]{2,1,0:T(8,128)(2,1)S(1)}, bf16[5,128,128]{2,1,0:T(8,128)(2,1)S(1)}, u32[]{:S(2)}, u32[]{:S(2)}) collective-permute-start(bf16[5,128,128]{2,1,0:T(8,128)(2,1)S(1)} %get-tuple-element.17), channel_id=1, source_target_pairs={{0,4},{2,6},{4,0},{6,2},{8,12},{10,14},{12,8},{14,10},{1,5},{3,7},... | collective-permute-start | bytes 491528 | tf_op jit(solution)/shard_map/ppermute | solution.py:338
  5.8 8.1 %collective-permute-start.2 = (bf16[5,128,128]{2,1,0:T(8,128)(2,1)S(1)}, bf16[5,128,128]{2,1,0:T(8,128)(2,1)S(1)}, u32[]{:S(2)}, u32[]{:S(2)}) collective-permute-start(bf16[5,128,128]{2,1,0:T(8,128)(2,1)S(1)} %get-tuple-element.17), channel_id=1, source_target_pairs={{0,2},{2,0},{4,6},{6,4},{8,10},{10,8},{12,14},{14,12},{1,3},{3,1},... | collective-permute-start | bytes 491528 | tf_op jit(solution)/shard_map/ppermute | solution.py:338
  6.0 9.0 %collective-permute-start = (bf16[2,384,128]{2,1,0:T(8,128)(2,1)S(1)}, bf16[2,384,128]{2,1,0:T(8,128)(2,1)S(1)}, u32[]{:S(2)}, u32[]{:S(2)}) collective-permute-start(bf16[2,384,128]{2,1,0:T(8,128)(2,1)S(1)} %get-tuple-element.15.source_own), channel_id=1, source_target_pairs={{0,1},{1,0},{2,3},{3,2},{4,5},{5,4},{6,7},{7,6},{8,9},{9,8},{10,11... | collective-permute-start | bytes 589832 | tf_op jit(solution)/shard_map/ppermute | solution.py:335
  10.4 7.6 %collective-permute-start.7 = (bf16[5,128,128]{2,1,0:T(8,128)(2,1)S(1)}, bf16[5,128,128]{2,1,0:T(8,128)(2,1)S(1)}, u32[]{:S(2)}, u32[]{:S(2)}) collective-permute-start(bf16[5,128,128]{2,1,0:T(8,128)(2,1)S(1)} %collective-permute-done.6.refs_7_), channel_id=1, source_target_pairs={{0,1},{1,0},{2,3},{3,2},{4,5},{5,4},{6,7},{7,6},{8,9},{9,8},{10,11... | collective-permute-start | bytes 491528 | tf_op jit(solution)/shard_map/ppermute | solution.py:335
  13.9 5.3 %collective-permute-start.5 = (bf16[5,128,128]{2,1,0:T(8,128)(2,1)S(1)}, bf16[5,128,128]{2,1,0:T(8,128)(2,1)S(1)}, u32[]{:S(2)}, u32[]{:S(2)}) collective-permute-start(bf16[5,128,128]{2,1,0:T(8,128)(2,1)S(1)} %collective-permute-done.4.refs_5_), channel_id=1, source_target_pairs={{0,1},{1,0},{2,3},{3,2},{4,5},{5,4},{6,7},{7,6},{8,9},{9,8},{10,11... | collective-permute-start | bytes 491528 | tf_op jit(solution)/shard_map/ppermute | solution.py:335
  13.9 5.3 %collective-permute-start.3 = (bf16[5,128,128]{2,1,0:T(8,128)(2,1)S(1)}, bf16[5,128,128]{2,1,0:T(8,128)(2,1)S(1)}, u32[]{:S(2)}, u32[]{:S(2)}) collective-permute-start(bf16[5,128,128]{2,1,0:T(8,128)(2,1)S(1)} %collective-permute-done.2.refs_3_), channel_id=1, source_target_pairs={{0,1},{1,0},{2,3},{3,2},{4,5},{5,4},{6,7},{7,6},{8,9},{9,8},{10,11... | collective-permute-start | bytes 491528 | tf_op jit(solution)/shard_map/ppermute | solution.py:335
  15.6 20.2 %copy-start = (bf16[2,384,768]{2,1,0:T(8,128)(2,1)S(1)}, bf16[2,384,768]{2,1,0:T(8,128)(2,1)}, u32[]{:S(2)}) copy-start(bf16[2,384,768]{2,1,0:T(8,128)(2,1)} %green.5) | copy-start | bytes 3538948
  15.6 5.6 %collective-permute-start.10 = (bf16[128,256]{1,0:T(8,128)(2,1)S(1)}, bf16[128,256]{1,0:T(8,128)(2,1)S(1)}, u32[]{:S(2)}, u32[]{:S(2)}) collective-permute-start(bf16[128,256]{1,0:T(8,128)(2,1)S(1)} %shard_map.47.surfaces.refs_9_), channel_id=1, source_target_pairs={{0,6},{2,4},{4,2},{6,0},{8,14},{10,12},{12,10},{14,8},{1,7},{3,5},... | collective-permute-start | bytes 196616 | tf_op jit(solution)/shard_map/ppermute | solution.py:338
  17.6 4.3 %collective-permute-start.9 = (bf16[128,256]{1,0:T(8,128)(2,1)S(1)}, bf16[128,256]{1,0:T(8,128)(2,1)S(1)}, u32[]{:S(2)}, u32[]{:S(2)}) collective-permute-start(bf16[128,256]{1,0:T(8,128)(2,1)S(1)} %shard_map.47.surfaces.refs_9_), channel_id=1, source_target_pairs={{0,4},{2,6},{4,0},{6,2},{8,12},{10,14},{12,8},{14,10},{1,5},{3,7},... | collective-permute-start | bytes 196616 | tf_op jit(solution)/shard_map/ppermute | solution.py:338
  18.1 4.3 %collective-permute-start.8 = (bf16[128,256]{1,0:T(8,128)(2,1)S(1)}, bf16[128,256]{1,0:T(8,128)(2,1)S(1)}, u32[]{:S(2)}, u32[]{:S(2)}) collective-permute-start(bf16[128,256]{1,0:T(8,128)(2,1)S(1)} %shard_map.47.surfaces.refs_9_), channel_id=1, source_target_pairs={{0,2},{2,0},{4,6},{6,4},{8,10},{10,8},{12,14},{14,12},{1,3},{3,1},... | collective-permute-start | bytes 196616 | tf_op jit(solution)/shard_map/ppermute | solution.py:338
  26.5 8.5 %collective-permute-start.11 = (bf16[256,256]{1,0:T(8,128)(2,1)S(1)}, bf16[256,256]{1,0:T(8,128)(2,1)S(1)}, u32[]{:S(2)}, u32[]{:S(2)}) collective-permute-start(bf16[256,256]{1,0:T(8,128)(2,1)S(1)} %get-tuple-element.19), channel_id=1, source_target_pairs={{0,8},{2,10},{4,12},{6,14},{8,0},{10,2},{12,4},{14,6},{1,9},{3,11}... | collective-permute-start | bytes 393224 | tf_op jit(solution)/shard_map/ppermute | solution.py:338
  35.7 1.3 %collective-permute-start.12 = (bf16[128,256]{1,0:T(8,128)(2,1)S(1)}, bf16[128,256]{1,0:T(8,128)(2,1)S(1)}, u32[]{:S(2)}, u32[]{:S(2)}) collective-permute-start(bf16[128,256]{1,0:T(8,128)(2,1)S(1)} %shard_map.51.own), channel_id=1, source_target_pairs={{0,1},{1,0},{2,3},{3,2},{4,5},{5,4},{6,7},{7,6},{8,9},{9,8},{10,11... | collective-permute-start | bytes 196616 | tf_op jit(solution)/shard_map/ppermute | solution.py:335
where the time goes:
time: 38.2 us; the launch traced here: 38 us
  waiting for transfers between devices  15.7 us (41%)
  starting transfers between devices  11.5 us (30%)
  Pallas kernels  10 us (26%)
  between operations  0.75 us (2%)
    ppermute x7, waiting for transfers between devices, partner(): return lax.ppermute(x, 'slab', [(i, i ^ bit) for i in range(slabs)])  15 us
    ppermute x7, starting transfers between devices, partner(): return lax.ppermute(x, 'slab', [(i, i ^ bit) for i in range(slabs)])  10.4 us
    pallas_call x7, Pallas kernels, call(): pl.pallas_call(kernel, in_specs=specs, out_specs=[V] * len(outs), out_sha...  10 us
    ppermute x6, starting transfers between devices, across(): return lax.ppermute(x, 'row', [(0, 1), (1, 0)])  1.14 us
  transfers between devices with their start and end apart: 13, of which 7 were waited for; matrix products, arithmetic and copies ran while one was open for 0% of the time, Pallas kernels for 8%

commit v1 on v0

v1 whole, which is shorter than its diff:
```python
import functools

import jax
import jax.numpy as jnp
from jax import lax
from jax.experimental import pallas as pl
from jax.experimental.pallas import tpu as pltpu
from jax.sharding import PartitionSpec as P


F32 = jnp.float32
BF16 = jnp.bfloat16
GROUP = 4
ORDER = (2, 1, 3)


def contract(x, matrix, across):
    return lax.dot_general(
        x, matrix, (((1,), (1 if across else 0,)), ((), ())), preferred_element_type=F32
    )


def split(x):
    high = x.astype(BF16)
    return high, (x - high.astype(F32)).astype(BF16)


def apply(real_form, x, across=True):
    high, low = split(x)
    both = contract(jnp.concatenate([high, low], axis=0), real_form, across)
    return both[: x.shape[0]] + both[x.shape[0] :]


def apply_short(real_form, x, across=True):
    return contract(x.astype(BF16), real_form, across)


def turned(x):
    half = x.shape[1] // 2
    return jnp.concatenate([-x[:, half:], x[:, :half]], axis=1)


def stacked(x):
    return jnp.concatenate([x, turned(x)], axis=0)


def apply_computed(columns, x):
    high, low = split(stacked(columns))
    x_high, x_low = split(x)
    both = contract(jnp.concatenate([x_high, x_low], axis=0), high, False)
    return both[: x.shape[0]] + both[x.shape[0] :] + contract(x_high, low, False)


def pack_kernel(green, coupling, source, edge, pack, source_near, couple_near, sems):
    row = lax.axis_index("row")
    shard_rows, width = green.shape[1:]
    surface = edge.shape[1]
    rows = pl.ds(pl.multiple_of(row * (shard_rows - surface), surface), surface)
    last = pl.ds(width - surface, surface)
    copies = [
        pltpu.make_async_copy(green.at[:, rows, pl.ds(0, surface)], pack.at[pl.ds(0, 2)], sems.at[0]),
        pltpu.make_async_copy(green.at[:, rows, last], pack.at[pl.ds(2, 2)], sems.at[1]),
        pltpu.make_async_copy(coupling.at[pl.ds(row, 1)], pack.at[pl.ds(4, 1)], sems.at[2]),
        pltpu.make_async_copy(green.at[:, rows], edge, sems.at[3]),
        pltpu.make_async_copy(source, source_near, sems.at[4]),
        pltpu.make_async_copy(coupling, couple_near, sems.at[5]),
    ]
    for c in copies:
        c.start()
    for c in copies:
        c.wait()


def masked_source(count, own, other, surface):
    row = lax.axis_index("row")
    orbitals = 2 * own.shape[1]

    def masked(part):
        mine, theirs = own[part].astype(F32), other[part].astype(F32)
        whole = jnp.concatenate(
            [jnp.where(row == 0, mine, theirs), jnp.where(row == 0, theirs, mine)], axis=0
        )
        orbital = lax.broadcasted_iota(jnp.int32, whole.shape, 0)
        live = (orbital < surface + count[:1]) | (orbital >= orbitals - surface)
        return jnp.where(live, whole, 0.0)

    real, imag = masked(0), masked(1)
    return (
        jnp.concatenate([real, imag], axis=1).astype(BF16),
        jnp.concatenate([-imag, real], axis=1).astype(BF16),
    )


def edge_kernel(count, edge, edge_other, source_own, source_other, vectors):
    row = lax.axis_index("row")
    surface = edge.shape[1]
    columns = source_own.shape[2]
    half = columns // 2
    above, below = masked_source(count, source_own, source_other, surface)

    def surface_rows(blocks):
        x = contract(blocks[0], above, False) + contract(blocks[1], below, False)
        whole = jnp.concatenate([x[:, :columns].T, x[:, columns:].T], axis=1)
        return jnp.where(row == 0, whole[:half], whole[half:]).astype(BF16)

    own, other = surface_rows(edge), surface_rows(edge_other)

    @pl.when(row == 0)
    def _():
        vectors[:half] = own
        vectors[half:] = other

    @pl.when(row == 1)
    def _():
        vectors[:half] = other
        vectors[half:] = own


def direct_kernel(count, green, source_own, source_other, surfaces, direct):
    above, below = masked_source(count, source_own, source_other, surfaces.shape[1] // 2)
    direct[...] = contract(green[0], above, False) + contract(green[1], below, False)


def unit_columns(size):
    eye = (
        lax.broadcasted_iota(jnp.int32, (size, size), 0)
        == lax.broadcasted_iota(jnp.int32, (size, size), 1)
    ).astype(F32)
    return jnp.concatenate([eye, jnp.zeros_like(eye)], axis=1)


NEAR, COUPLE, ALONG, BACK, SHIFT = 0, 1, 2, 4, 6


def apply_pair(x, forms, index, name):
    high, low = split(x)
    both = contract(jnp.concatenate([high, low], axis=0), forms[index, name], False)
    rest = contract(high, forms[index, name + 1], False)
    return both[: x.shape[0]] + both[x.shape[0] :] + rest


def columns_of(forms, index, name):
    size = forms.shape[2] // 2
    return forms[index, name, :size].astype(F32) + forms[index, name + 1, :size].astype(F32)


def real_form(re, im):
    return jnp.concatenate(
        [jnp.concatenate([re, -im], axis=1), jnp.concatenate([im, re], axis=1)], axis=0
    )


def form_slab(forms, k, near, far_first, far_last, along, b):
    slab = lax.axis_index("slab")
    slabs = lax.axis_size("slab")
    member = slab % GROUP
    known = slab - member + (member ^ k) < slabs - 1
    b_re, b_im = (jnp.where(known, x, jnp.zeros_like(x)) for x in b)
    couple = real_form(b_re, b_im)
    forms[k, NEAR] = real_form(*near)
    forms[k, COUPLE] = couple

    def transposed(re, im):
        return jnp.concatenate([re.astype(F32).T, im.astype(F32).T], axis=1).astype(BF16)

    def keep(name, x):
        high, low = split(stacked(x))
        forms[k, name] = high
        forms[k, name + 1] = low

    b_columns = transposed(b_re, b_im)
    keep(ALONG, contract(transposed(*along), couple, False))
    keep(BACK, contract(b_columns, real_form(*far_first), True))
    keep(SHIFT, apply(couple, contract(b_columns, real_form(*far_last), True), False))


def form_kernel(order, *refs):
    edge, edge_other, coupling = refs[:3]
    packs, forms = refs[3:-1], refs[-1]
    row = lax.axis_index("row")
    size = coupling.shape[1]
    width = edge.shape[2]

    def fill(first_is_own):
        f, l = (edge, edge_other) if first_is_own else (edge_other, edge)

        def corner(ref, start):
            return ref[0, :, start : start + size], ref[1, :, start : start + size]

        last = width - size
        form_slab(
            forms,
            0,
            corner(f, 0),
            corner(f, last),
            corner(l, last),
            corner(l, 0),
            (coupling[0], coupling[1]),
        )
        for n, k in enumerate(order):
            form_packed(forms, k, packs[2 * n], packs[2 * n + 1], first_is_own)

    @pl.when(row == 0)
    def _():
        fill(True)

    @pl.when(row == 1)
    def _():
        fill(False)


def form_packed(forms, k, mine, other, first_is_own):
    f, l = (mine, other) if first_is_own else (other, mine)
    form_slab(forms, k, (f[0], f[1]), (f[2], f[3]), (l[2], l[3]), (l[0], l[1]), (f[4], l[4]))


def response_kernel(last_k, _, mine, other, forms, alpha, delta, shift, through, whole, states, backs):
    row = lax.axis_index("row")
    slabs = lax.axis_size("slab")
    member = lax.axis_index("slab") % GROUP

    @pl.when(row == 0)
    def _():
        form_packed(forms, last_k, mine, other, True)

    @pl.when(row == 1)
    def _():
        form_packed(forms, last_k, mine, other, False)

    unit = unit_columns(alpha.shape[0])
    states[0] = unit
    u = columns_of(forms, member, ALONG)
    states[1] = u
    for i in range(1, GROUP):
        if i < GROUP - 1 or 2 * GROUP < slabs:
            u = apply_pair(u, forms, member ^ i, ALONG)
        if i < GROUP - 1:
            states[i + 1] = u
    through[...] = u
    backs[GROUP] = jnp.zeros_like(unit)
    s = apply(forms[member ^ (GROUP - 1), NEAR], states[GROUP - 1])
    backs[GROUP - 1] = s
    for i in reversed(range(GROUP - 1)):
        near = forms[member ^ i, NEAR]
        e = apply(near, states[i]) if i else apply_short(near, unit)
        s = e + apply_pair(s, forms, member ^ i, BACK)
        backs[i] = s
    whole[...] = s
    shift[...] = columns_of(forms, member ^ (GROUP - 1), SHIFT)
    alpha[...] = states[member]
    delta[...] = backs[member + 1]


def sweep_kernel(
    forms, shift, whole, v0, v1, v2, v3, send, leaving, entering, pi, sigma, vectors, states, backs
):
    slab = lax.axis_index("slab")
    member = slab % GROUP
    half = pi.shape[0]
    for k, v in enumerate((v0, v1, v2, v3)):
        vectors[member ^ k] = v[...]
    first = [vectors[i, :half] for i in range(GROUP)]
    terms = []
    for i in range(GROUP):
        term = contract(vectors[i, half:], forms[member ^ i, COUPLE], False)
        if i < GROUP - 1:
            term = term + contract(first[i + 1], forms[member ^ i, SHIFT], False)
            term = term + contract(first[i + 1], forms[member ^ i, SHIFT + 1], False)
        terms.append(term)
    states[0] = jnp.zeros(pi.shape, F32)
    u = terms[0]
    for i in range(1, GROUP):
        states[i] = u
        u = apply_pair(u, forms, member ^ i, ALONG) + terms[i]
    leaving[...] = u
    backs[GROUP] = jnp.zeros(pi.shape, F32)
    s = apply(forms[member ^ (GROUP - 1), NEAR], states[GROUP - 1]) + first[GROUP - 1].astype(F32)
    backs[GROUP - 1] = s
    for i in reversed(range(GROUP - 1)):
        e = first[i].astype(F32)
        if i:
            e = e + apply(forms[member ^ i, NEAR], states[i])
        s = e + apply_pair(s, forms, member ^ i, BACK)
        backs[i] = s
    entering[...] = s
    left = slab < lax.axis_size("slab") // 2
    send[:half] = jnp.where(left, u, s).astype(BF16)
    send[half : 2 * half] = first[0]
    send[2 * half :] = jnp.where(left, shift[...], whole[...]).astype(BF16)
    pi[...] = states[member]
    sigma[...] = backs[member + 1]


def gamma_kernel(forms, gamma, whole, backs):
    member = lax.axis_index("slab") % GROUP
    backs[GROUP] = unit_columns(gamma.shape[0])
    s = columns_of(forms, member ^ (GROUP - 1), BACK)
    backs[GROUP - 1] = s
    for i in reversed(range(GROUP - 1)):
        s = apply_pair(s, forms, member ^ i, BACK)
        backs[i] = s
    whole[...] = s
    gamma[...] = backs[member + 1]


def close_kernel(coupling, leaving, first, seen, shift, pi, sigma, alpha, delta, gamma, out):
    half = first.shape[0]
    left = lax.axis_index("slab") < lax.axis_size("slab") // 2
    there = seen[:half].astype(F32)
    map_form = stacked(seen[2 * half :].astype(F32)).astype(BF16)
    b = real_form(coupling[0], coupling[1])

    @pl.when(left)
    def _():
        ahead = seen[half : 2 * half].astype(F32)
        past = leaving[...] + apply_computed(shift[...], ahead)
        entry = there + apply(map_form, past, False)
        behind = sigma[...] + apply_computed(gamma[...], entry)
        out[:half] = pi[...].astype(BF16)
        out[half:] = apply(b, behind).astype(BF16)

    @pl.when(jnp.logical_not(left))
    def _():
        before = there + apply_short(map_form, first[...], False)
        behind = sigma[...] + apply_computed(delta[...], before)
        out[:half] = (pi[...] + apply_computed(alpha[...], before)).astype(BF16)
        out[half:] = apply(b, behind).astype(BF16)


def final_kernel(count, green, direct, own, other, result, whole):
    row = lax.axis_index("row")
    shard_rows, width = green.shape[1:]
    half = own.shape[0] // 2
    columns = 2 * half
    surface = own.shape[1] // 2

    def place(first, second):
        for i in range(2):
            whole[i, :half] = first[i * half : (i + 1) * half]
            whole[i, half:] = second[i * half : (i + 1) * half]

    @pl.when(row == 0)
    def _():
        place(own, other)

    @pl.when(row == 1)
    def _():
        place(other, own)

    def product(start, x):
        g = jnp.concatenate(
            [green[0, :, start : start + surface], green[1, :, start : start + surface]], axis=1
        )
        x_re, x_im = x[:, :surface], x[:, surface:]
        return contract(g, real_form(x_re, x_im), True)

    total = direct[...] + product(0, whole[0]) + product(width - surface, whole[1])
    orbital = row * shard_rows + lax.broadcasted_iota(jnp.int32, total.shape, 0)
    limit = jnp.concatenate([count[:1]] * (total.shape[1] // count.shape[1]), axis=1)
    live = (orbital < surface + limit) | (orbital >= width - surface)
    total = jnp.where(live, total, 0.0)
    result[0] = total[:, :columns]
    result[1] = total[:, columns:]


V, H = (pl.BlockSpec(memory_space=m) for m in (pltpu.VMEM, pltpu.HBM))


def call(kernel, specs, outs, scratch, *args, keep=False, aliases={}):
    args = [
        pltpu.with_memory_space_constraint(a, s.memory_space)
        for a, s in zip(args, specs, strict=True)
    ]
    kind = jax.ShapeDtypeStruct if keep else pltpu.VMEM
    return pl.pallas_call(
        kernel,
        in_specs=specs,
        out_specs=[V] * len(outs),
        out_shape=[kind(s, d) for s, d in outs],
        scratch_shapes=[pltpu.VMEM(*x) if isinstance(x, tuple) else x for x in scratch],
        input_output_aliases=aliases,
        compiler_params=pltpu.CompilerParams(vmem_limit_bytes=24 << 20),
    )(*args)


def compute(columns, x):
    size = columns.shape[1] // 2

    def mul(a, b):
        return jnp.dot(a, b, preferred_element_type=F32, precision=lax.Precision.HIGHEST)

    c_re, c_im = columns[:, :size], columns[:, size:]
    x_re, x_im = x[:, :size], x[:, size:]
    return jnp.concatenate([mul(x_re, c_re) - mul(x_im, c_im), mul(x_re, c_im) + mul(x_im, c_re)], axis=1)


def body(green_blocks, coupling, source, interior_count):
    shard_rows = green_blocks.shape[1]
    width = green_blocks.shape[2]
    surface = coupling.shape[1]
    columns = source.shape[2]
    half = columns // 2
    slab = lax.axis_index("slab")
    slabs = lax.axis_size("slab")

    def across(x):
        return lax.ppermute(x, "row", [(0, 1), (1, 0)])

    def partner(x, bit):
        return lax.ppermute(x, "slab", [(i, i ^ bit) for i in range(slabs)])

    square = (surface, 2 * surface)
    thin = (half, 2 * surface)
    edge, pack, source_near, couple_near = call(
        pack_kernel,
        [H] * 3,
        [
            ((2, surface, width), BF16),
            ((5, surface, surface), BF16),
            (source.shape, BF16),
            (coupling.shape, BF16),
        ],
        [pltpu.SemaphoreType.DMA((6,))],
        green_blocks,
        coupling,
        source,
    )
    count = jnp.broadcast_to(interior_count.reshape(1, 1), (8, columns))
    source_other = across(source_near)
    edge_other = across(edge)
    packs = {}
    for k in ORDER:
        packs[k] = partner(pack, k)
    (vectors,) = call(
        edge_kernel,
        [V] * 5,
        [((columns, 2 * surface), BF16)],
        [],
        count,
        edge,
        edge_other,
        source_near,
        source_other,
    )
    (direct,) = call(
        direct_kernel,
        [V] * 5,
        [((shard_rows, 2 * columns), F32)],
        [],
        count,
        green_blocks,
        source_near,
        source_other,
        vectors,
    )
    gathered = []
    for k in range(1, GROUP):
        gathered.append(partner(vectors, k))
    swapped = {}
    for k in ORDER:
        swapped[k] = across(packs[k])
    both = [x for k in ORDER[:-1] for x in (packs[k], swapped[k])]
    forms_shape = ((GROUP, 8, 2 * surface, 2 * surface), BF16)
    (forms,) = call(
        functools.partial(form_kernel, ORDER[:-1]),
        [V] * (3 + len(both)),
        [forms_shape],
        [],
        edge,
        edge_other,
        couple_near,
        *both,
    )
    forms, alpha, delta, shift, through, whole = call(
        functools.partial(response_kernel, ORDER[-1]),
        [V] * 3,
        [forms_shape] + [(square, F32)] * 5,
        [((GROUP,) + square, F32), ((GROUP + 1,) + square, F32)],
        forms,
        packs[ORDER[-1]],
        swapped[ORDER[-1]],
        aliases={0: 0},
    )
    send, leaving, entering, pi, sigma = call(
        sweep_kernel,
        [V] * (3 + GROUP),
        [((columns + surface, 2 * surface), BF16)] + [(thin, F32)] * 4,
        [((GROUP, columns, 2 * surface), BF16), ((GROUP,) + thin, F32), ((GROUP + 1,) + thin, F32)],
        forms,
        shift,
        whole,
        vectors,
        *gathered,
    )
    gamma, back_whole = call(
        gamma_kernel, [V], [(square, F32), (square, F32)], [((GROUP + 1,) + square, F32)], forms
    )
    first = send[half:columns]
    bit = GROUP
    if 2 * bit < slabs:
        first = first.astype(F32)
        a_map, d_map, c_map = through, whole, back_whole
    while 2 * bit < slabs:
        right = (slab // bit) % 2 == 1

        def sides(own):
            seen = partner(own, bit)
            return jnp.where(right, seen, own), jnp.where(right, own, seen)

        (ax, ay), (cx, cy), (dx, dy) = sides(a_map), sides(c_map), sides(d_map)
        (wx, wy), (fx, fy) = sides(shift), sides(first)
        (px, py), (qx, qy) = sides(leaving), sides(entering)
        middle = px + compute(wx, fy)
        entry = qy + compute(dy, middle)
        carried = compute(dy, ax)
        pi = pi + jnp.where(right, compute(alpha, middle), 0.0)
        sigma = sigma + jnp.where(right, compute(delta, middle), compute(gamma, entry))
        delta = jnp.where(right, compute(delta, ax), delta + compute(gamma, carried))
        alpha = jnp.where(right, compute(alpha, ax), alpha)
        gamma = jnp.where(right, gamma, compute(gamma, cy))
        leaving, entering = py + compute(ay, middle), qx + compute(cx, entry)
        a_map, c_map, d_map = compute(ay, ax), compute(cx, cy), dx + compute(cx, carried)
        shift, first = wy, fx
        bit *= 2
        if 2 * bit == slabs:
            left = slab < slabs // 2
            parts = [jnp.where(left, leaving, entering), first, jnp.where(left, shift, d_map)]
            send = jnp.concatenate(parts, axis=0).astype(BF16)
            first = first.astype(BF16)
    seen = partner(send, slabs // 2)
    (closed,) = call(
        close_kernel,
        [V] * 10,
        [((columns, 2 * surface), BF16)],
        [],
        couple_near,
        leaving,
        first,
        seen,
        shift,
        pi,
        sigma,
        alpha,
        delta,
        gamma,
    )
    (result,) = call(
        final_kernel,
        [V] * 5,
        [((2, shard_rows, columns), F32)],
        [((2, columns, 2 * surface), BF16)],
        count,
        green_blocks,
        direct,
        closed,
        across(closed),
        keep=True,
    )
    return result


def solution(mesh):
    placed = (
        P(None, ("energy", "slab", "row"), None),
        P(None, "slab", None),
        P(None, ("energy", "slab", "row"), None),
        P("slab"),
    )
    return jax.shard_map(
        body,
        mesh=mesh,
        in_specs=placed,
        out_specs=P(None, ("energy", "slab", "row"), None),
        check_vma=False,
    )
```

time: 38.2 us -> 36.1 us (0.945)
  waiting for transfers between devices: 15.7 us -> 13.8 us
    ppermute x7, waiting for transfers between devices: 15 us -> 13.1 us  [partner(): return lax.ppermute(x, 'slab', [(i, i ^ bit) for i in range(slabs)])]
    pallas_call x7 -> x9, Pallas kernels: 10 us -> 9.84 us  [call(): pl.pallas_call(kernel, in_specs=specs, out_specs=[V] * len(outs), out_sha...]
  transfers between devices with their start and end apart: 13 -> 13, of which waited for: 7 -> 5; matrix products, arithmetic and copies ran while one was open for 0% -> 0% of each run, Pallas kernels for 8% -> 14%
where the time goes in v1:
time: 36.1 us; the launch traced here: 35.9 us
  waiting for transfers between devices  13.8 us (38%)
  starting transfers between devices  11.5 us (32%)
  Pallas kernels  9.84 us (27%)
  between operations  0.75 us (2%)
    ppermute x7, waiting for transfers between devices, partner(): return lax.ppermute(x, 'slab', [(i, i ^ bit) for i in range(slabs)])  13.1 us
    ppermute x7, starting transfers between devices, partner(): return lax.ppermute(x, 'slab', [(i, i ^ bit) for i in range(slabs)])  10.3 us
    pallas_call x9, Pallas kernels, call(): pl.pallas_call(kernel, in_specs=specs, out_specs=[V] * len(outs), out_sha...  9.84 us
    ppermute x6, starting transfers between devices, across(): return lax.ppermute(x, 'row', [(0, 1), (1, 0)])  1.14 us
    ppermute x6, waiting for transfers between devices, across(): return lax.ppermute(x, 'row', [(0, 1), (1, 0)])  0.74 us
  transfers between devices with their start and end apart: 13, of which 5 were waited for; matrix products, arithmetic and copies ran while one was open for 0% of the time, Pallas kernels for 14%

profile of v1, /device:TPU:0, one launch (start us, length us, event | category | flops | bytes accessed | tf_op | source)
XLA Modules:
  0.0 35.9 jit_solution(5157672536049064344)
XLA Ops:
  0.0 1.2 %shard_map.46 = (bf16[2,128,768]{2,1,0:T(8,128)(2,1)S(1)}, bf16[5,128,128]{2,1,0:T(8,128)(2,1)S(1)}, bf16[2,384,128]{2,1,0:T(8,128)(2,1)S(1)}, bf16[2,128,128]{2,1,0:T(8,128)(2,1)S(1)}) custom-call(bf16[2,384,768]{2,1,0:T(8,128)(2,1)} %green.5, bf16[2,128,128]{2,1,0:T(8,128)(2,1)} %coupling.1, bf16[2,384,128]{2,1,0:T(8,128)(2,1)} %source.1), custom_call_target="tpu_custom_call" | custom-call | tf_op jit(solution)/shard_map/pallas_call | solution.py:375
  1.2 0.6 %collective-permute-start.1 = (bf16[2,128,768]{2,1,0:T(8,128)(2,1)S(1)}, bf16[2,128,768]{2,1,0:T(8,128)(2,1)S(1)}, u32[]{:S(2)}, u32[]{:S(2)}) collective-permute-start(bf16[2,128,768]{2,1,0:T(8,128)(2,1)S(1)} %get-tuple-element.20.edge.refs_0_), channel_id=1, source_target_pairs={{0,1},{1,0},{2,3},{3,2},{4,5},{5,4},{6,7},{7,6},{8,9},{9,8},{10,11... | collective-permute-start | bytes 1179656 | tf_op jit(solution)/shard_map/ppermute | solution.py:407
  1.8 2.6 %collective-permute-start.2 = (bf16[5,128,128]{2,1,0:T(8,128)(2,1)S(1)}, bf16[5,128,128]{2,1,0:T(8,128)(2,1)S(1)}, u32[]{:S(2)}, u32[]{:S(2)}) collective-permute-start(bf16[5,128,128]{2,1,0:T(8,128)(2,1)S(1)} %get-tuple-element.22), channel_id=1, source_target_pairs={{0,4},{2,6},{4,0},{6,2},{8,12},{10,14},{12,8},{14,10},{1,5},{3,7},... | collective-permute-start | bytes 491528 | tf_op jit(solution)/shard_map/ppermute | solution.py:410
  4.4 1.5 %collective-permute-start.4 = (bf16[5,128,128]{2,1,0:T(8,128)(2,1)S(1)}, bf16[5,128,128]{2,1,0:T(8,128)(2,1)S(1)}, u32[]{:S(2)}, u32[]{:S(2)}) collective-permute-start(bf16[5,128,128]{2,1,0:T(8,128)(2,1)S(1)} %get-tuple-element.22), channel_id=1, source_target_pairs={{0,2},{2,0},{4,6},{6,4},{8,10},{10,8},{12,14},{14,12},{1,3},{3,1},... | collective-permute-start | bytes 491528 | tf_op jit(solution)/shard_map/ppermute | solution.py:410
  5.9 0.0 collective-permute-start.6
  5.9 3.5 %collective-permute-done.2.refs_3_ = bf16[5,128,128]{2,1,0:T(8,128)(2,1)S(1)} collective-permute-done((bf16[5,128,128]{2,1,0:T(8,128)(2,1)S(1)}, bf16[5,128,128]{2,1,0:T(8,128)(2,1)S(1)}, u32[]{:S(2)}, u32[]{:S(2)}) %collective-permute-start.2) | collective-permute-done | bytes 163872 | tf_op jit(solution)/shard_map/ppermute | solution.py:410
  9.5 4.7 %collective-permute-done.4.refs_5_ = bf16[5,128,128]{2,1,0:T(8,128)(2,1)S(1)} collective-permute-done((bf16[5,128,128]{2,1,0:T(8,128)(2,1)S(1)}, bf16[5,128,128]{2,1,0:T(8,128)(2,1)S(1)}, u32[]{:S(2)}, u32[]{:S(2)}) %collective-permute-start.4) | collective-permute-done | bytes 163872 | tf_op jit(solution)/shard_map/ppermute | solution.py:410
  14.2 0.5 %collective-permute-start.7 = (bf16[5,128,128]{2,1,0:T(8,128)(2,1)S(1)}, bf16[5,128,128]{2,1,0:T(8,128)(2,1)S(1)}, u32[]{:S(2)}, u32[]{:S(2)}) collective-permute-start(bf16[5,128,128]{2,1,0:T(8,128)(2,1)S(1)} %collective-permute-done.6.mine), channel_id=1, source_target_pairs={{0,1},{1,0},{2,3},{3,2},{4,5},{5,4},{6,7},{7,6},{8,9},{9,8},{10,11... | collective-permute-start | bytes 491528 | tf_op jit(solution)/shard_map/ppermute | solution.py:407
  15.4 0.5 %shard_map.47.surfaces.v0 = bf16[128,256]{1,0:T(8,128)(2,1)S(1)} custom-call(s32[8,128]{1,0:T(8,128)S(1)} %broadcast_in_dim.8.count, bf16[2,128,768]{2,1,0:T(8,128)(2,1)S(1)} %get-tuple-element.20.edge.refs_0_, bf16[2,128,768]{2,1,0:T(8,128)(2,1)S(1)} %collective-permute-done.1.edge_other.refs_1_, bf16[2,384,128]{2,1,0:T(8,128)(2,1)S(1)} %get-tuple-element.19.source_own, ...), custom_call_target="tpu_custom_call" | custom-call | tf_op jit(solution)/shard_map/pallas_call | solution.py:375
  15.9 1.6 %collective-permute-start.8 = (bf16[128,256]{1,0:T(8,128)(2,1)S(1)}, bf16[128,256]{1,0:T(8,128)(2,1)S(1)}, u32[]{:S(2)}, u32[]{:S(2)}) collective-permute-start(bf16[128,256]{1,0:T(8,128)(2,1)S(1)} %shard_map.47.surfaces.v0), channel_id=1, source_target_pairs={{0,2},{2,0},{4,6},{6,4},{8,10},{10,8},{12,14},{14,12},{1,3},{3,1},... | collective-permute-start | bytes 196616 | tf_op jit(solution)/shard_map/ppermute | solution.py:410
  17.5 0.4 %collective-permute-start.9 = (bf16[128,256]{1,0:T(8,128)(2,1)S(1)}, bf16[128,256]{1,0:T(8,128)(2,1)S(1)}, u32[]{:S(2)}, u32[]{:S(2)}) collective-permute-start(bf16[128,256]{1,0:T(8,128)(2,1)S(1)} %shard_map.47.surfaces.v0), channel_id=1, source_target_pairs={{0,4},{2,6},{4,0},{6,2},{8,12},{10,14},{12,8},{14,10},{1,5},{3,7},... | collective-permute-start | bytes 196616 | tf_op jit(solution)/shard_map/ppermute | solution.py:410
  17.9 1.5 %collective-permute-start.10 = (bf16[128,256]{1,0:T(8,128)(2,1)S(1)}, bf16[128,256]{1,0:T(8,128)(2,1)S(1)}, u32[]{:S(2)}, u32[]{:S(2)}) collective-permute-start(bf16[128,256]{1,0:T(8,128)(2,1)S(1)} %shard_map.47.surfaces.v0), channel_id=1, source_target_pairs={{0,6},{2,4},{4,2},{6,0},{8,14},{10,12},{12,10},{14,8},{1,7},{3,5},... | collective-permute-start | bytes 196616 | tf_op jit(solution)/shard_map/ppermute | solution.py:410
  19.4 0.7 %shard_map.49._ = bf16[4,8,256,256]{3,2,1,0:T(8,128)(2,1)S(1)} custom-call(bf16[2,128,768]{2,1,0:T(8,128)(2,1)S(1)} %get-tuple-element.20.edge.refs_0_, bf16[2,128,768]{2,1,0:T(8,128)(2,1)S(1)} %collective-permute-done.1.edge_other.refs_1_, bf16[2,128,128]{2,1,0:T(8,128)(2,1)S(1)} %get-tuple-element.21.refs_2_.coupling, ...), custom_call_target="tpu_custom_call" | custom-call | tf_op jit(solution)/shard_map/pallas_call | solution.py:375
  20.2 2.1 %shard_map.50 = (bf16[4,8,256,256]{3,2,1,0:T(8,128)(2,1)S(1)}, f32[128,256]{1,0:T(8,128)S(1)}, f32[128,256]{1,0:T(8,128)S(1)}, f32[128,256]{1,0:T(8,128)S(1)}, f...) custom-call(bf16[4,8,256,256]{3,2,1,0:T(8,128)(2,1)S(1)} %shard_map.49._, ...), custom_call_target="tpu_custom_call", output_to_operand_aliasing={{0}: (0, {})} | custom-call | tf_op jit(solution)/shard_map/pallas_call | solution.py:375
  22.3 0.8 %collective-permute-done.10.v3 = bf16[128,256]{1,0:T(8,128)(2,1)S(1)} collective-permute-done((bf16[128,256]{1,0:T(8,128)(2,1)S(1)}, bf16[128,256]{1,0:T(8,128)(2,1)S(1)}, u32[]{:S(2)}, u32[]{:S(2)}) %collective-permute-start.10) | collective-permute-done | bytes 65568 | tf_op jit(solution)/shard_map/ppermute | solution.py:410
  23.1 1.8 %shard_map.51 = (bf16[256,256]{1,0:T(8,128)(2,1)S(1)}, f32[64,256]{1,0:T(8,128)S(1)}, f32[64,256]{1,0:T(8,128)}, f32[64,256]{1,0:T(8,128)S(1)}, f32[64,256]{1,0:T(8,128)S(1)}) custom-call(bf16[4,8,256,256]{3,2,1,0:T(8,128)(2,1)S(1)} %get-tuple-element.23.forms, f32[128,256]{1,0:T(8,128)S(1)} %get-tuple-element.24.shift, ...), custom_call_target="tpu_custom_call" | custom-call | tf_op jit(solution)/shard_map/pallas_call | solution.py:375
  24.9 2.6 %collective-permute-start.11 = (bf16[256,256]{1,0:T(8,128)(2,1)S(1)}, bf16[256,256]{1,0:T(8,128)(2,1)S(1)}, u32[]{:S(2)}, u32[]{:S(2)}) collective-permute-start(bf16[256,256]{1,0:T(8,128)(2,1)S(1)} %get-tuple-element.27), channel_id=1, source_target_pairs={{0,8},{2,10},{4,12},{6,14},{8,0},{10,2},{12,4},{14,6},{1,9},{3,11}... | collective-permute-start | bytes 393224 | tf_op jit(solution)/shard_map/ppermute | solution.py:410
  27.5 1.3 %shard_map.52 = (f32[128,256]{1,0:T(8,128)S(1)}, f32[128,256]{1,0:T(8,128)}) custom-call(bf16[4,8,256,256]{3,2,1,0:T(8,128)(2,1)S(1)} %get-tuple-element.23.forms), custom_call_target="tpu_custom_call" | custom-call | tf_op jit(solution)/shard_map/pallas_call | solution.py:375
  28.8 4.1 %collective-permute-done.11.seen = bf16[256,256]{1,0:T(8,128)(2,1)S(1)} collective-permute-done((bf16[256,256]{1,0:T(8,128)(2,1)S(1)}, bf16[256,256]{1,0:T(8,128)(2,1)S(1)}, u32[]{:S(2)}, u32[]{:S(2)}) %collective-permute-start.11) | collective-permute-done | bytes 131104 | tf_op jit(solution)/shard_map/ppermute | solution.py:410
  32.9 0.6 %shard_map.53.own = bf16[128,256]{1,0:T(8,128)(2,1)S(1)} custom-call(bf16[2,128,128]{2,1,0:T(8,128)(2,1)S(1)} %get-tuple-element.21.refs_2_.coupling, f32[64,256]{1,0:T(8,128)S(1)} %get-tuple-element.26.leaving, bf16[64,256]{1,0:T(8,128)(2,1)S(1)} %slice.3.first, bf16[256,256]{1,0:T(8,128)(2,1)S(1)} %collective-permute-done.11.seen, ...), custom_call_target="tpu_custom_call" | custom-call | tf_op jit(solution)/shard_map/pallas_call | solution.py:375
  33.5 0.1 collective-permute-start.12
  33.6 0.5 %shard_map.48.direct = f32[384,256]{1,0:T(8,128)S(1)} custom-call(s32[8,128]{1,0:T(8,128)S(1)} %broadcast_in_dim.8.count, bf16[2,384,768]{2,1,0:T(8,128)(2,1)S(1)} %copy-done, bf16[2,384,128]{2,1,0:T(8,128)(2,1)S(1)} %get-tuple-element.19.source_own, bf16[2,384,128]{2,1,0:T(8,128)(2,1)S(1)} %collective-permute-done.source_other, ...), custom_call_target="tpu_custom_call" | custom-call | tf_op jit(solution)/shard_map/pallas_call | solution.py:375
  34.1 0.7 %collective-permute-done.12.other = bf16[128,256]{1,0:T(8,128)(2,1)S(1)} collective-permute-done((bf16[128,256]{1,0:T(8,128)(2,1)S(1)}, bf16[128,256]{1,0:T(8,128)(2,1)S(1)}, u32[]{:S(2)}, u32[]{:S(2)}) %collective-permute-start.12) | collective-permute-done | bytes 65568 | tf_op jit(solution)/shard_map/ppermute | solution.py:407
  34.9 1.1 %shard_map.54 = f32[2,384,128]{2,1,0:T(8,128)} custom-call(s32[8,128]{1,0:T(8,128)S(1)} %broadcast_in_dim.8.count, bf16[2,384,768]{2,1,0:T(8,128)(2,1)S(1)} %copy-done, f32[384,256]{1,0:T(8,128)S(1)} %shard_map.48.direct, bf16[128,256]{1,0:T(8,128)(2,1)S(1)} %shard_map.53.own, bf16[128,256]{1,0:T(8,128)(2,1)S(1)} %collective-permute-done.12.other), custom_call_target="tpu_custom_call" | custom-call | tf_op jit(solution)/shard_map/pallas_call | solution.py:375
  (15 shorter events, 0.0 us)
Async XLA Ops:
  1.2 14.1 %collective-permute-start.1 = (bf16[2,128,768]{2,1,0:T(8,128)(2,1)S(1)}, bf16[2,128,768]{2,1,0:T(8,128)(2,1)S(1)}, u32[]{:S(2)}, u32[]{:S(2)}) collective-permute-start(bf16[2,128,768]{2,1,0:T(8,128)(2,1)S(1)} %get-tuple-element.20.edge.refs_0_), channel_id=1, source_target_pairs={{0,1},{1,0},{2,3},{3,2},{4,5},{5,4},{6,7},{7,6},{8,9},{9,8},{10,11... | collective-permute-start | bytes 1179656 | tf_op jit(solution)/shard_map/ppermute | solution.py:407
  1.8 7.7 %collective-permute-start.2 = (bf16[5,128,128]{2,1,0:T(8,128)(2,1)S(1)}, bf16[5,128,128]{2,1,0:T(8,128)(2,1)S(1)}, u32[]{:S(2)}, u32[]{:S(2)}) collective-permute-start(bf16[5,128,128]{2,1,0:T(8,128)(2,1)S(1)} %get-tuple-element.22), channel_id=1, source_target_pairs={{0,4},{2,6},{4,0},{6,2},{8,12},{10,14},{12,8},{14,10},{1,5},{3,7},... | collective-permute-start | bytes 491528 | tf_op jit(solution)/shard_map/ppermute | solution.py:410
  4.4 9.8 %collective-permute-start.4 = (bf16[5,128,128]{2,1,0:T(8,128)(2,1)S(1)}, bf16[5,128,128]{2,1,0:T(8,128)(2,1)S(1)}, u32[]{:S(2)}, u32[]{:S(2)}) collective-permute-start(bf16[5,128,128]{2,1,0:T(8,128)(2,1)S(1)} %get-tuple-element.22), channel_id=1, source_target_pairs={{0,2},{2,0},{4,6},{6,4},{8,10},{10,8},{12,14},{14,12},{1,3},{3,1},... | collective-permute-start | bytes 491528 | tf_op jit(solution)/shard_map/ppermute | solution.py:410
  5.9 8.3 %collective-permute-start.6 = (bf16[5,128,128]{2,1,0:T(8,128)(2,1)S(1)}, bf16[5,128,128]{2,1,0:T(8,128)(2,1)S(1)}, u32[]{:S(2)}, u32[]{:S(2)}) collective-permute-start(bf16[5,128,128]{2,1,0:T(8,128)(2,1)S(1)} %get-tuple-element.22), channel_id=1, source_target_pairs={{0,6},{2,4},{4,2},{6,0},{8,14},{10,12},{12,10},{14,8},{1,7},{3,5},... | collective-permute-start | bytes 491528 | tf_op jit(solution)/shard_map/ppermute | solution.py:410
  5.9 9.4 %collective-permute-start = (bf16[2,384,128]{2,1,0:T(8,128)(2,1)S(1)}, bf16[2,384,128]{2,1,0:T(8,128)(2,1)S(1)}, u32[]{:S(2)}, u32[]{:S(2)}) collective-permute-start(bf16[2,384,128]{2,1,0:T(8,128)(2,1)S(1)} %get-tuple-element.19.source_own), channel_id=1, source_target_pairs={{0,1},{1,0},{2,3},{3,2},{4,5},{5,4},{6,7},{7,6},{8,9},{9,8},{10,11... | collective-permute-start | bytes 589832 | tf_op jit(solution)/shard_map/ppermute | solution.py:407
  9.5 8.5 %collective-permute-start.3 = (bf16[5,128,128]{2,1,0:T(8,128)(2,1)S(1)}, bf16[5,128,128]{2,1,0:T(8,128)(2,1)S(1)}, u32[]{:S(2)}, u32[]{:S(2)}) collective-permute-start(bf16[5,128,128]{2,1,0:T(8,128)(2,1)S(1)} %collective-permute-done.2.refs_3_), channel_id=1, source_target_pairs={{0,1},{1,0},{2,3},{3,2},{4,5},{5,4},{6,7},{7,6},{8,9},{9,8},{10,11... | collective-permute-start | bytes 491528 | tf_op jit(solution)/shard_map/ppermute | solution.py:407
  14.2 5.3 %collective-permute-start.5 = (bf16[5,128,128]{2,1,0:T(8,128)(2,1)S(1)}, bf16[5,128,128]{2,1,0:T(8,128)(2,1)S(1)}, u32[]{:S(2)}, u32[]{:S(2)}) collective-permute-start(bf16[5,128,128]{2,1,0:T(8,128)(2,1)S(1)} %collective-permute-done.4.refs_5_), channel_id=1, source_target_pairs={{0,1},{1,0},{2,3},{3,2},{4,5},{5,4},{6,7},{7,6},{8,9},{9,8},{10,11... | collective-permute-start | bytes 491528 | tf_op jit(solution)/shard_map/ppermute | solution.py:407
  14.2 6.0 %collective-permute-start.7 = (bf16[5,128,128]{2,1,0:T(8,128)(2,1)S(1)}, bf16[5,128,128]{2,1,0:T(8,128)(2,1)S(1)}, u32[]{:S(2)}, u32[]{:S(2)}) collective-permute-start(bf16[5,128,128]{2,1,0:T(8,128)(2,1)S(1)} %collective-permute-done.6.mine), channel_id=1, source_target_pairs={{0,1},{1,0},{2,3},{3,2},{4,5},{5,4},{6,7},{7,6},{8,9},{9,8},{10,11... | collective-permute-start | bytes 491528 | tf_op jit(solution)/shard_map/ppermute | solution.py:407
  15.9 6.4 %collective-permute-start.8 = (bf16[128,256]{1,0:T(8,128)(2,1)S(1)}, bf16[128,256]{1,0:T(8,128)(2,1)S(1)}, u32[]{:S(2)}, u32[]{:S(2)}) collective-permute-start(bf16[128,256]{1,0:T(8,128)(2,1)S(1)} %shard_map.47.surfaces.v0), channel_id=1, source_target_pairs={{0,2},{2,0},{4,6},{6,4},{8,10},{10,8},{12,14},{14,12},{1,3},{3,1},... | collective-permute-start | bytes 196616 | tf_op jit(solution)/shard_map/ppermute | solution.py:410
  17.5 4.9 %collective-permute-start.9 = (bf16[128,256]{1,0:T(8,128)(2,1)S(1)}, bf16[128,256]{1,0:T(8,128)(2,1)S(1)}, u32[]{:S(2)}, u32[]{:S(2)}) collective-permute-start(bf16[128,256]{1,0:T(8,128)(2,1)S(1)} %shard_map.47.surfaces.v0), channel_id=1, source_target_pairs={{0,4},{2,6},{4,0},{6,2},{8,12},{10,14},{12,8},{14,10},{1,5},{3,7},... | collective-permute-start | bytes 196616 | tf_op jit(solution)/shard_map/ppermute | solution.py:410
  17.9 5.2 %collective-permute-start.10 = (bf16[128,256]{1,0:T(8,128)(2,1)S(1)}, bf16[128,256]{1,0:T(8,128)(2,1)S(1)}, u32[]{:S(2)}, u32[]{:S(2)}) collective-permute-start(bf16[128,256]{1,0:T(8,128)(2,1)S(1)} %shard_map.47.surfaces.v0), channel_id=1, source_target_pairs={{0,6},{2,4},{4,2},{6,0},{8,14},{10,12},{12,10},{14,8},{1,7},{3,5},... | collective-permute-start | bytes 196616 | tf_op jit(solution)/shard_map/ppermute | solution.py:410
  23.1 10.5 %copy-start = (bf16[2,384,768]{2,1,0:T(8,128)(2,1)S(1)}, bf16[2,384,768]{2,1,0:T(8,128)(2,1)}, u32[]{:S(2)}) copy-start(bf16[2,384,768]{2,1,0:T(8,128)(2,1)} %green.5) | copy-start | bytes 3538948
  24.9 8.0 %collective-permute-start.11 = (bf16[256,256]{1,0:T(8,128)(2,1)S(1)}, bf16[256,256]{1,0:T(8,128)(2,1)S(1)}, u32[]{:S(2)}, u32[]{:S(2)}) collective-permute-start(bf16[256,256]{1,0:T(8,128)(2,1)S(1)} %get-tuple-element.27), channel_id=1, source_target_pairs={{0,8},{2,10},{4,12},{6,14},{8,0},{10,2},{12,4},{14,6},{1,9},{3,11}... | collective-permute-start | bytes 393224 | tf_op jit(solution)/shard_map/ppermute | solution.py:410
  33.5 1.3 %collective-permute-start.12 = (bf16[128,256]{1,0:T(8,128)(2,1)S(1)}, bf16[128,256]{1,0:T(8,128)(2,1)S(1)}, u32[]{:S(2)}, u32[]{:S(2)}) collective-permute-start(bf16[128,256]{1,0:T(8,128)(2,1)S(1)} %shard_map.53.own), channel_id=1, source_target_pairs={{0,1},{1,0},{2,3},{3,2},{4,5},{5,4},{6,7},{7,6},{8,9},{9,8},{10,11... | collective-permute-start | bytes 196616 | tf_op jit(solution)/shard_map/ppermute | solution.py:407

commit v2 on v1

--- a/solution.py
+++ b/solution.py
@@ -11,7 +11,7 @@
 F32 = jnp.float32
 BF16 = jnp.bfloat16
 GROUP = 4
-ORDER = (2, 1, 3)
+ORDER = (3, 1, 2)
 
 
 def contract(x, matrix, across):
@@ -214,10 +214,16 @@
     form_slab(forms, k, (f[0], f[1]), (f[2], f[3]), (l[2], l[3]), (l[0], l[1]), (f[4], l[4]))
 
 
-def response_kernel(last_k, _, mine, other, forms, alpha, delta, shift, through, whole, states, backs):
+def solve_kernel(
+    last_k, _, mine, other, v0, v1, v2, v3,
+    forms, send, leaving, entering, here, after, shift, vectors, states, backs,
+):
     row = lax.axis_index("row")
+    slab = lax.axis_index("slab")
     slabs = lax.axis_size("slab")
-    member = lax.axis_index("slab") % GROUP
+    member = slab % GROUP
+    size = shift.shape[0]
+    half = vectors.shape[1] // 2
 
     @pl.when(row == 0)
     def _():
@@ -227,39 +233,15 @@
     def _():
         form_packed(forms, last_k, mine, other, False)
 
-    unit = unit_columns(alpha.shape[0])
-    states[0] = unit
-    u = columns_of(forms, member, ALONG)
-    states[1] = u
-    for i in range(1, GROUP):
-        if i < GROUP - 1 or 2 * GROUP < slabs:
-            u = apply_pair(u, forms, member ^ i, ALONG)
-        if i < GROUP - 1:
-            states[i + 1] = u
-    through[...] = u
-    backs[GROUP] = jnp.zeros_like(unit)
-    s = apply(forms[member ^ (GROUP - 1), NEAR], states[GROUP - 1])
-    backs[GROUP - 1] = s
-    for i in reversed(range(GROUP - 1)):
-        near = forms[member ^ i, NEAR]
-        e = apply(near, states[i]) if i else apply_short(near, unit)
-        s = e + apply_pair(s, forms, member ^ i, BACK)
-        backs[i] = s
-    whole[...] = s
-    shift[...] = columns_of(forms, member ^ (GROUP - 1), SHIFT)
-    alpha[...] = states[member]
-    delta[...] = backs[member + 1]
-
-
-def sweep_kernel(
-    forms, shift, whole, v0, v1, v2, v3, send, leaving, entering, pi, sigma, vectors, states, backs
-):
-    slab = lax.axis_index("slab")
-    member = slab % GROUP
-    half = pi.shape[0]
     for k, v in enumerate((v0, v1, v2, v3)):
         vectors[member ^ k] = v[...]
     first = [vectors[i, :half] for i in range(GROUP)]
+    unit = unit_columns(size)
+    nothing = jnp.zeros_like(unit)
+
+    def beside(x, below=nothing):
+        return jnp.concatenate([x, below], axis=0)
+
     terms = []
     for i in range(GROUP):
         term = contract(vectors[i, half:], forms[member ^ i, COUPLE], False)
@@ -267,28 +249,40 @@
             term = term + contract(first[i + 1], forms[member ^ i, SHIFT], False)
             term = term + contract(first[i + 1], forms[member ^ i, SHIFT + 1], False)
         terms.append(term)
-    states[0] = jnp.zeros(pi.shape, F32)
-    u = terms[0]
-    for i in range(1, GROUP):
+    states[0] = beside(jnp.zeros_like(terms[0]), unit)
+    u = beside(terms[0], columns_of(forms, member, ALONG))
+    for i in range(1, GROUP - 1):
         states[i] = u
-        u = apply_pair(u, forms, member ^ i, ALONG) + terms[i]
-    leaving[...] = u
-    backs[GROUP] = jnp.zeros(pi.shape, F32)
-    s = apply(forms[member ^ (GROUP - 1), NEAR], states[GROUP - 1]) + first[GROUP - 1].astype(F32)
+        u = apply_pair(u, forms, member ^ i, ALONG) + beside(terms[i])
+    states[GROUP - 1] = u
+    last = member ^ (GROUP - 1)
+    s = apply(forms[last, NEAR], u) + beside(first[GROUP - 1].astype(F32))
+    if 2 * GROUP < slabs:
+        u = apply_pair(u, forms, last, ALONG) + beside(terms[GROUP - 1])
+        leaving[...] = u
+    else:
+        u = apply_pair(u[:half], forms, last, ALONG) + terms[GROUP - 1]
+        leaving[:half] = u
+        leaving[half:] = nothing
+    backs[GROUP] = jnp.zeros_like(s)
     backs[GROUP - 1] = s
     for i in reversed(range(GROUP - 1)):
-        e = first[i].astype(F32)
+        near = forms[member ^ i, NEAR]
         if i:
-            e = e + apply(forms[member ^ i, NEAR], states[i])
+            e = apply(near, states[i]) + beside(first[i].astype(F32))
+        else:
+            e = beside(first[i].astype(F32), apply_short(near, unit))
         s = e + apply_pair(s, forms, member ^ i, BACK)
         backs[i] = s
     entering[...] = s
-    left = slab < lax.axis_size("slab") // 2
-    send[:half] = jnp.where(left, u, s).astype(BF16)
+    w = columns_of(forms, last, SHIFT)
+    shift[...] = w
+    left = slab < slabs // 2
+    send[:half] = jnp.where(left, u[:half], s[:half]).astype(BF16)
     send[half : 2 * half] = first[0]
-    send[2 * half :] = jnp.where(left, shift[...], whole[...]).astype(BF16)
-    pi[...] = states[member]
-    sigma[...] = backs[member + 1]
+    send[2 * half :] = jnp.where(left, w, s[half:]).astype(BF16)
+    here[...] = states[member]
+    after[...] = backs[member + 1]
 
 
 def gamma_kernel(forms, gamma, whole, backs):
@@ -303,7 +297,7 @@
     gamma[...] = backs[member + 1]
 
 
-def close_kernel(coupling, leaving, first, seen, shift, pi, sigma, alpha, delta, gamma, out):
+def close_kernel(coupling, leaving, first, seen, shift, here, after, gamma, out):
     half = first.shape[0]
     left = lax.axis_index("slab") < lax.axis_size("slab") // 2
     there = seen[:half].astype(F32)
@@ -313,17 +307,17 @@
     @pl.when(left)
     def _():
         ahead = seen[half : 2 * half].astype(F32)
-        past = leaving[...] + apply_computed(shift[...], ahead)
+        past = leaving[:half] + apply_computed(shift[...], ahead)
         entry = there + apply(map_form, past, False)
-        behind = sigma[...] + apply_computed(gamma[...], entry)
-        out[:half] = pi[...].astype(BF16)
+        behind = after[:half] + apply_computed(gamma[...], entry)
+        out[:half] = here[:half].astype(BF16)
         out[half:] = apply(b, behind).astype(BF16)
 
     @pl.when(jnp.logical_not(left))
     def _():
         before = there + apply_short(map_form, first[...], False)
-        behind = sigma[...] + apply_computed(delta[...], before)
-        out[:half] = (pi[...] + apply_computed(alpha[...], before)).astype(BF16)
+        behind = after[:half] + apply_computed(after[half:], before)
+        out[:half] = (here[:half] + apply_computed(here[half:], before)).astype(BF16)
         out[half:] = apply(b, behind).astype(BF16)
 
 
@@ -410,7 +404,7 @@
         return lax.ppermute(x, "slab", [(i, i ^ bit) for i in range(slabs)])
 
     square = (surface, 2 * surface)
-    thin = (half, 2 * surface)
+    joint = (half + surface, 2 * surface)
     edge, pack, source_near, couple_near = call(
         pack_kernel,
         [H] * 3,
@@ -471,26 +465,23 @@
         couple_near,
         *both,
     )
-    forms, alpha, delta, shift, through, whole = call(
-        functools.partial(response_kernel, ORDER[-1]),
-        [V] * 3,
-        [forms_shape] + [(square, F32)] * 5,
-        [((GROUP,) + square, F32), ((GROUP + 1,) + square, F32)],
+    forms, send, leaving, entering, here, after, shift = call(
+        functools.partial(solve_kernel, ORDER[-1]),
+        [V] * (3 + GROUP),
+        [forms_shape, ((columns + surface, 2 * surface), BF16)]
+        + [(joint, F32)] * 4
+        + [(square, F32)],
+        [
+            ((GROUP, columns, 2 * surface), BF16),
+            ((GROUP,) + joint, F32),
+            ((GROUP + 1,) + joint, F32),
+        ],
         forms,
         packs[ORDER[-1]],
         swapped[ORDER[-1]],
-        aliases={0: 0},
-    )
-    send, leaving, entering, pi, sigma = call(
-        sweep_kernel,
-        [V] * (3 + GROUP),
-        [((columns + surface, 2 * surface), BF16)] + [(thin, F32)] * 4,
-        [((GROUP, columns, 2 * surface), BF16), ((GROUP,) + thin, F32), ((GROUP + 1,) + thin, F32)],
-        forms,
-        shift,
-        whole,
         vectors,
         *gathered,
+        aliases={0: 0},
     )
     gamma, back_whole = call(
         gamma_kernel, [V], [(square, F32), (square, F32)], [((GROUP + 1,) + square, F32)], forms
@@ -499,7 +490,10 @@
     bit = GROUP
     if 2 * bit < slabs:
         first = first.astype(F32)
-        a_map, d_map, c_map = through, whole, back_whole
+        leave, a_map = leaving[:half], leaving[half:]
+        back, d_map = entering[:half], entering[half:]
+        pi, alpha, sigma, delta = here[:half], here[half:], after[:half], after[half:]
+        c_map = back_whole
     while 2 * bit < slabs:
         right = (slab // bit) % 2 == 1
 
@@ -509,7 +503,7 @@
 
         (ax, ay), (cx, cy), (dx, dy) = sides(a_map), sides(c_map), sides(d_map)
         (wx, wy), (fx, fy) = sides(shift), sides(first)
-        (px, py), (qx, qy) = sides(leaving), sides(entering)
+        (px, py), (qx, qy) = sides(leave), sides(back)
         middle = px + compute(wx, fy)
         entry = qy + compute(dy, middle)
         carried = compute(dy, ax)
@@ -518,19 +512,22 @@
         delta = jnp.where(right, compute(delta, ax), delta + compute(gamma, carried))
         alpha = jnp.where(right, compute(alpha, ax), alpha)
         gamma = jnp.where(right, gamma, compute(gamma, cy))
-        leaving, entering = py + compute(ay, middle), qx + compute(cx, entry)
+        leave, back = py + compute(ay, middle), qx + compute(cx, entry)
         a_map, c_map, d_map = compute(ay, ax), compute(cx, cy), dx + compute(cx, carried)
         shift, first = wy, fx
         bit *= 2
         if 2 * bit == slabs:
             left = slab < slabs // 2
-            parts = [jnp.where(left, leaving, entering), first, jnp.where(left, shift, d_map)]
+            parts = [jnp.where(left, leave, back), first, jnp.where(left, shift, d_map)]
             send = jnp.concatenate(parts, axis=0).astype(BF16)
             first = first.astype(BF16)
+            leaving = jnp.concatenate([leave, a_map], axis=0)
+            here = jnp.concatenate([pi, alpha], axis=0)
+            after = jnp.concatenate([sigma, delta], axis=0)
     seen = partner(send, slabs // 2)
     (closed,) = call(
         close_kernel,
-        [V] * 10,
+        [V] * 8,
         [((columns, 2 * surface), BF16)],
         [],
         couple_near,
@@ -538,10 +535,8 @@
         first,
         seen,
         shift,
-        pi,
-        sigma,
-        alpha,
-        delta,
+        here,
+        after,
         gamma,
     )
     (result,) = call(

time: 36.1 us -> 36.7 us (1.017)
  waiting for transfers between devices: 13.8 us -> 15.8 us
  Pallas kernels: 9.84 us -> 8.58 us
    ppermute x7, waiting for transfers between devices: 13.1 us -> 15 us  [partner(): return lax.ppermute(x, 'slab', [(i, i ^ bit) for i in range(slabs)])]
    pallas_call x9 -> x8, Pallas kernels: 9.84 us -> 8.58 us  [call(): pl.pallas_call(kernel, in_specs=specs, out_specs=[V] * len(outs), out_sha...]
  transfers between devices with their start and end apart: 13 -> 13, of which waited for: 5 -> 7; matrix products, arithmetic and copies ran while one was open for 0% -> 0% of each run, Pallas kernels for 14% -> 8%
where the time goes in v2:
time: 36.7 us; the launch traced here: 36.6 us
  waiting for transfers between devices  15.8 us (43%)
  starting transfers between devices  11.4 us (31%)
  Pallas kernels  8.58 us (23%)
  between operations  0.76 us (2%)
    ppermute x7, waiting for transfers between devices, partner(): return lax.ppermute(x, 'slab', [(i, i ^ bit) for i in range(slabs)])  15 us
    ppermute x7, starting transfers between devices, partner(): return lax.ppermute(x, 'slab', [(i, i ^ bit) for i in range(slabs)])  10.3 us
    pallas_call x8, Pallas kernels, call(): pl.pallas_call(kernel, in_specs=specs, out_specs=[V] * len(outs), out_sha...  8.58 us
    ppermute x6, starting transfers between devices, across(): return lax.ppermute(x, 'row', [(0, 1), (1, 0)])  1.14 us
    ppermute x6, waiting for transfers between devices, across(): return lax.ppermute(x, 'row', [(0, 1), (1, 0)])  0.74 us
  transfers between devices with their start and end apart: 13, of which 7 were waited for; matrix products, arithmetic and copies ran while one was open for 0% of the time, Pallas kernels for 8%

profile of v2, /device:TPU:0, one launch (start us, length us, event | category | flops | bytes accessed | tf_op | source)
XLA Modules:
  0.0 36.6 jit_solution(13662027253541911000)
XLA Ops:
  0.0 1.2 %shard_map.46 = (bf16[2,128,768]{2,1,0:T(8,128)(2,1)S(1)}, bf16[5,128,128]{2,1,0:T(8,128)(2,1)S(1)}, bf16[2,384,128]{2,1,0:T(8,128)(2,1)S(1)}, bf16[2,128,128]{2,1,0:T(8,128)(2,1)S(1)}) custom-call(bf16[2,384,768]{2,1,0:T(8,128)(2,1)} %green.5, bf16[2,128,128]{2,1,0:T(8,128)(2,1)} %coupling.1, bf16[2,384,128]{2,1,0:T(8,128)(2,1)} %source.1), custom_call_target="tpu_custom_call" | custom-call | tf_op jit(solution)/shard_map/pallas_call | solution.py:369
  1.2 0.6 %collective-permute-start.1 = (bf16[2,128,768]{2,1,0:T(8,128)(2,1)S(1)}, bf16[2,128,768]{2,1,0:T(8,128)(2,1)S(1)}, u32[]{:S(2)}, u32[]{:S(2)}) collective-permute-start(bf16[2,128,768]{2,1,0:T(8,128)(2,1)S(1)} %get-tuple-element.17.edge.refs_0_), channel_id=1, source_target_pairs={{0,1},{1,0},{2,3},{3,2},{4,5},{5,4},{6,7},{7,6},{8,9},{9,8},{10,11... | collective-permute-start | bytes 1179656 | tf_op jit(solution)/shard_map/ppermute | solution.py:401
  1.8 2.6 %collective-permute-start.4 = (bf16[5,128,128]{2,1,0:T(8,128)(2,1)S(1)}, bf16[5,128,128]{2,1,0:T(8,128)(2,1)S(1)}, u32[]{:S(2)}, u32[]{:S(2)}) collective-permute-start(bf16[5,128,128]{2,1,0:T(8,128)(2,1)S(1)} %get-tuple-element.19), channel_id=1, source_target_pairs={{0,2},{2,0},{4,6},{6,4},{8,10},{10,8},{12,14},{14,12},{1,3},{3,1},... | collective-permute-start | bytes 491528 | tf_op jit(solution)/shard_map/ppermute | solution.py:404
  4.3 1.5 %collective-permute-start.2 = (bf16[5,128,128]{2,1,0:T(8,128)(2,1)S(1)}, bf16[5,128,128]{2,1,0:T(8,128)(2,1)S(1)}, u32[]{:S(2)}, u32[]{:S(2)}) collective-permute-start(bf16[5,128,128]{2,1,0:T(8,128)(2,1)S(1)} %get-tuple-element.19), channel_id=1, source_target_pairs={{0,6},{2,4},{4,2},{6,0},{8,14},{10,12},{12,10},{14,8},{1,7},{3,5},... | collective-permute-start | bytes 491528 | tf_op jit(solution)/shard_map/ppermute | solution.py:404
  5.9 6.7 %collective-permute-done.4.refs_5_ = bf16[5,128,128]{2,1,0:T(8,128)(2,1)S(1)} collective-permute-done((bf16[5,128,128]{2,1,0:T(8,128)(2,1)S(1)}, bf16[5,128,128]{2,1,0:T(8,128)(2,1)S(1)}, u32[]{:S(2)}, u32[]{:S(2)}) %collective-permute-start.4) | collective-permute-done | bytes 163872 | tf_op jit(solution)/shard_map/ppermute | solution.py:404
  12.7 0.5 %collective-permute-start.3 = (bf16[5,128,128]{2,1,0:T(8,128)(2,1)S(1)}, bf16[5,128,128]{2,1,0:T(8,128)(2,1)S(1)}, u32[]{:S(2)}, u32[]{:S(2)}) collective-permute-start(bf16[5,128,128]{2,1,0:T(8,128)(2,1)S(1)} %collective-permute-done.2.refs_3_), channel_id=1, source_target_pairs={{0,1},{1,0},{2,3},{3,2},{4,5},{5,4},{6,7},{7,6},{8,9},{9,8},{10,11... | collective-permute-start | bytes 491528 | tf_op jit(solution)/shard_map/ppermute | solution.py:401
  13.2 0.8 %collective-permute-done.6.mine = bf16[5,128,128]{2,1,0:T(8,128)(2,1)S(1)} collective-permute-done((bf16[5,128,128]{2,1,0:T(8,128)(2,1)S(1)}, bf16[5,128,128]{2,1,0:T(8,128)(2,1)S(1)}, u32[]{:S(2)}, u32[]{:S(2)}) %collective-permute-start.6) | collective-permute-done | bytes 163872 | tf_op jit(solution)/shard_map/ppermute | solution.py:404
  14.7 0.5 %shard_map.47.surfaces.v0 = bf16[128,256]{1,0:T(8,128)(2,1)S(1)} custom-call(s32[8,128]{1,0:T(8,128)S(1)} %broadcast_in_dim.8.count, bf16[2,128,768]{2,1,0:T(8,128)(2,1)S(1)} %get-tuple-element.17.edge.refs_0_, bf16[2,128,768]{2,1,0:T(8,128)(2,1)S(1)} %collective-permute-done.1.edge_other.refs_1_, bf16[2,384,128]{2,1,0:T(8,128)(2,1)S(1)} %get-tuple-element.16.source_own, ...), custom_call_target="tpu_custom_call" | custom-call | tf_op jit(solution)/shard_map/pallas_call | solution.py:369
  15.2 2.7 %collective-permute-start.10 = (bf16[128,256]{1,0:T(8,128)(2,1)S(1)}, bf16[128,256]{1,0:T(8,128)(2,1)S(1)}, u32[]{:S(2)}, u32[]{:S(2)}) collective-permute-start(bf16[128,256]{1,0:T(8,128)(2,1)S(1)} %shard_map.47.surfaces.v0), channel_id=1, source_target_pairs={{0,6},{2,4},{4,2},{6,0},{8,14},{10,12},{12,10},{14,8},{1,7},{3,5},... | collective-permute-start | bytes 196616 | tf_op jit(solution)/shard_map/ppermute | solution.py:404
  17.9 0.5 %collective-permute-start.9 = (bf16[128,256]{1,0:T(8,128)(2,1)S(1)}, bf16[128,256]{1,0:T(8,128)(2,1)S(1)}, u32[]{:S(2)}, u32[]{:S(2)}) collective-permute-start(bf16[128,256]{1,0:T(8,128)(2,1)S(1)} %shard_map.47.surfaces.v0), channel_id=1, source_target_pairs={{0,4},{2,6},{4,0},{6,2},{8,12},{10,14},{12,8},{14,10},{1,5},{3,7},... | collective-permute-start | bytes 196616 | tf_op jit(solution)/shard_map/ppermute | solution.py:404
  18.3 0.4 %collective-permute-start.8 = (bf16[128,256]{1,0:T(8,128)(2,1)S(1)}, bf16[128,256]{1,0:T(8,128)(2,1)S(1)}, u32[]{:S(2)}, u32[]{:S(2)}) collective-permute-start(bf16[128,256]{1,0:T(8,128)(2,1)S(1)} %shard_map.47.surfaces.v0), channel_id=1, source_target_pairs={{0,2},{2,0},{4,6},{6,4},{8,10},{10,8},{12,14},{14,12},{1,3},{3,1},... | collective-permute-start | bytes 196616 | tf_op jit(solution)/shard_map/ppermute | solution.py:404
  18.7 0.7 %shard_map.49._ = bf16[4,8,256,256]{3,2,1,0:T(8,128)(2,1)S(1)} custom-call(bf16[2,128,768]{2,1,0:T(8,128)(2,1)S(1)} %get-tuple-element.17.edge.refs_0_, bf16[2,128,768]{2,1,0:T(8,128)(2,1)S(1)} %collective-permute-done.1.edge_other.refs_1_, bf16[2,128,128]{2,1,0:T(8,128)(2,1)S(1)} %get-tuple-element.18.refs_2_.coupling, ...), custom_call_target="tpu_custom_call" | custom-call | tf_op jit(solution)/shard_map/pallas_call | solution.py:369
  19.5 1.2 %collective-permute-done.10.v3 = bf16[128,256]{1,0:T(8,128)(2,1)S(1)} collective-permute-done((bf16[128,256]{1,0:T(8,128)(2,1)S(1)}, bf16[128,256]{1,0:T(8,128)(2,1)S(1)}, u32[]{:S(2)}, u32[]{:S(2)}) %collective-permute-start.10) | collective-permute-done | bytes 65568 | tf_op jit(solution)/shard_map/ppermute | solution.py:404
  20.7 1.6 %collective-permute-done.9.v2 = bf16[128,256]{1,0:T(8,128)(2,1)S(1)} collective-permute-done((bf16[128,256]{1,0:T(8,128)(2,1)S(1)}, bf16[128,256]{1,0:T(8,128)(2,1)S(1)}, u32[]{:S(2)}, u32[]{:S(2)}) %collective-permute-start.9) | collective-permute-done | bytes 65568 | tf_op jit(solution)/shard_map/ppermute | solution.py:404
  22.2 0.4 %collective-permute-done.8.v1 = bf16[128,256]{1,0:T(8,128)(2,1)S(1)} collective-permute-done((bf16[128,256]{1,0:T(8,128)(2,1)S(1)}, bf16[128,256]{1,0:T(8,128)(2,1)S(1)}, u32[]{:S(2)}, u32[]{:S(2)}) %collective-permute-start.8) | collective-permute-done | bytes 65568 | tf_op jit(solution)/shard_map/ppermute | solution.py:404
  22.6 2.7 %shard_map.50 = (bf16[4,8,256,256]{3,2,1,0:T(8,128)(2,1)S(1)}, bf16[256,256]{1,0:T(8,128)(2,1)S(1)}, f32[192,256]{1,0:T(8,128)S(1)}, f32[192,256]{1,0:T(8,128)},...) custom-call(bf16[4,8,256,256]{3,2,1,0:T(8,128)(2,1)S(1)} %shard_map., ...), custom_call_target="tpu_custom_call", output_to_operand_aliasing={{0}: (0, {})} | custom-call | tf_op jit(solution)/shard_map/pallas_call | solution.py:369
  25.3 2.6 %collective-permute-start.11 = (bf16[256,256]{1,0:T(8,128)(2,1)S(1)}, bf16[256,256]{1,0:T(8,128)(2,1)S(1)}, u32[]{:S(2)}, u32[]{:S(2)}) collective-permute-start(bf16[256,256]{1,0:T(8,128)(2,1)S(1)} %get-tuple-element.21), channel_id=1, source_target_pairs={{0,8},{2,10},{4,12},{6,14},{8,0},{10,2},{12,4},{14,6},{1,9},{3,11}... | collective-permute-start | bytes 393224 | tf_op jit(solution)/shard_map/ppermute | solution.py:404
  27.9 1.3 %shard_map.51 = (f32[128,256]{1,0:T(8,128)S(1)}, f32[128,256]{1,0:T(8,128)}) custom-call(bf16[4,8,256,256]{3,2,1,0:T(8,128)(2,1)S(1)} %get-tuple-element.25.forms), custom_call_target="tpu_custom_call" | custom-call | tf_op jit(solution)/shard_map/pallas_call | solution.py:369
  29.2 4.3 %collective-permute-done.11.seen = bf16[256,256]{1,0:T(8,128)(2,1)S(1)} collective-permute-done((bf16[256,256]{1,0:T(8,128)(2,1)S(1)}, bf16[256,256]{1,0:T(8,128)(2,1)S(1)}, u32[]{:S(2)}, u32[]{:S(2)}) %collective-permute-start.11) | collective-permute-done | bytes 131104 | tf_op jit(solution)/shard_map/ppermute | solution.py:404
  33.5 0.6 %shard_map.52.own = bf16[128,256]{1,0:T(8,128)(2,1)S(1)} custom-call(bf16[2,128,128]{2,1,0:T(8,128)(2,1)S(1)} %get-tuple-element.18.refs_2_.coupling, f32[192,256]{1,0:T(8,128)S(1)} %get-tuple-element.20.leaving, bf16[64,256]{1,0:T(8,128)(2,1)S(1)} %slice.3.first, bf16[256,256]{1,0:T(8,128)(2,1)S(1)} %collective-permute-done.11.seen, ...), custom_call_target="tpu_custom_call" | custom-call | tf_op jit(solution)/shard_map/pallas_call | solution.py:369
  34.2 0.1 collective-permute-start.12
  34.3 0.5 %shard_map.48.direct = f32[384,256]{1,0:T(8,128)S(1)} custom-call(s32[8,128]{1,0:T(8,128)S(1)} %broadcast_in_dim.8.count, bf16[2,384,768]{2,1,0:T(8,128)(2,1)S(1)} %copy-done, bf16[2,384,128]{2,1,0:T(8,128)(2,1)S(1)} %get-tuple-element.16.source_own, bf16[2,384,128]{2,1,0:T(8,128)(2,1)S(1)} %collective-permute-done.source_other, ...), custom_call_target="tpu_custom_call" | custom-call | tf_op jit(solution)/shard_map/pallas_call | solution.py:369
  34.8 0.7 %collective-permute-done.12.other = bf16[128,256]{1,0:T(8,128)(2,1)S(1)} collective-permute-done((bf16[128,256]{1,0:T(8,128)(2,1)S(1)}, bf16[128,256]{1,0:T(8,128)(2,1)S(1)}, u32[]{:S(2)}, u32[]{:S(2)}) %collective-permute-start.12) | collective-permute-done | bytes 65568 | tf_op jit(solution)/shard_map/ppermute | solution.py:401
  35.5 1.1 %shard_map.53 = f32[2,384,128]{2,1,0:T(8,128)} custom-call(s32[8,128]{1,0:T(8,128)S(1)} %broadcast_in_dim.8.count, bf16[2,384,768]{2,1,0:T(8,128)(2,1)S(1)} %copy-done, f32[384,256]{1,0:T(8,128)S(1)} %shard_map.48.direct, bf16[128,256]{1,0:T(8,128)(2,1)S(1)} %shard_map.52.own, bf16[128,256]{1,0:T(8,128)(2,1)S(1)} %collective-permute-done.12.other), custom_call_target="tpu_custom_call" | custom-call | tf_op jit(solution)/shard_map/pallas_call | solution.py:369
  (14 shorter events, 0.1 us)
Async XLA Ops:
  1.2 13.5 %collective-permute-start.1 = (bf16[2,128,768]{2,1,0:T(8,128)(2,1)S(1)}, bf16[2,128,768]{2,1,0:T(8,128)(2,1)S(1)}, u32[]{:S(2)}, u32[]{:S(2)}) collective-permute-start(bf16[2,128,768]{2,1,0:T(8,128)(2,1)S(1)} %get-tuple-element.17.edge.refs_0_), channel_id=1, source_target_pairs={{0,1},{1,0},{2,3},{3,2},{4,5},{5,4},{6,7},{7,6},{8,9},{9,8},{10,11... | collective-permute-start | bytes 1179656 | tf_op jit(solution)/shard_map/ppermute | solution.py:401
  1.8 10.9 %collective-permute-start.4 = (bf16[5,128,128]{2,1,0:T(8,128)(2,1)S(1)}, bf16[5,128,128]{2,1,0:T(8,128)(2,1)S(1)}, u32[]{:S(2)}, u32[]{:S(2)}) collective-permute-start(bf16[5,128,128]{2,1,0:T(8,128)(2,1)S(1)} %get-tuple-element.19), channel_id=1, source_target_pairs={{0,2},{2,0},{4,6},{6,4},{8,10},{10,8},{12,14},{14,12},{1,3},{3,1},... | collective-permute-start | bytes 491528 | tf_op jit(solution)/shard_map/ppermute | solution.py:404
  4.3 8.3 %collective-permute-start.2 = (bf16[5,128,128]{2,1,0:T(8,128)(2,1)S(1)}, bf16[5,128,128]{2,1,0:T(8,128)(2,1)S(1)}, u32[]{:S(2)}, u32[]{:S(2)}) collective-permute-start(bf16[5,128,128]{2,1,0:T(8,128)(2,1)S(1)} %get-tuple-element.19), channel_id=1, source_target_pairs={{0,6},{2,4},{4,2},{6,0},{8,14},{10,12},{12,10},{14,8},{1,7},{3,5},... | collective-permute-start | bytes 491528 | tf_op jit(solution)/shard_map/ppermute | solution.py:404
  5.9 8.1 %collective-permute-start.6 = (bf16[5,128,128]{2,1,0:T(8,128)(2,1)S(1)}, bf16[5,128,128]{2,1,0:T(8,128)(2,1)S(1)}, u32[]{:S(2)}, u32[]{:S(2)}) collective-permute-start(bf16[5,128,128]{2,1,0:T(8,128)(2,1)S(1)} %get-tuple-element.19), channel_id=1, source_target_pairs={{0,4},{2,6},{4,0},{6,2},{8,12},{10,14},{12,8},{14,10},{1,5},{3,7},... | collective-permute-start | bytes 491528 | tf_op jit(solution)/shard_map/ppermute | solution.py:404
  5.9 8.7 %collective-permute-start = (bf16[2,384,128]{2,1,0:T(8,128)(2,1)S(1)}, bf16[2,384,128]{2,1,0:T(8,128)(2,1)S(1)}, u32[]{:S(2)}, u32[]{:S(2)}) collective-permute-start(bf16[2,384,128]{2,1,0:T(8,128)(2,1)S(1)} %get-tuple-element.16.source_own), channel_id=1, source_target_pairs={{0,1},{1,0},{2,3},{3,2},{4,5},{5,4},{6,7},{7,6},{8,9},{9,8},{10,11... | collective-permute-start | bytes 589832 | tf_op jit(solution)/shard_map/ppermute | solution.py:401
  12.7 5.7 %collective-permute-start.5 = (bf16[5,128,128]{2,1,0:T(8,128)(2,1)S(1)}, bf16[5,128,128]{2,1,0:T(8,128)(2,1)S(1)}, u32[]{:S(2)}, u32[]{:S(2)}) collective-permute-start(bf16[5,128,128]{2,1,0:T(8,128)(2,1)S(1)} %collective-permute-done.4.refs_5_), channel_id=1, source_target_pairs={{0,1},{1,0},{2,3},{3,2},{4,5},{5,4},{6,7},{7,6},{8,9},{9,8},{10,11... | collective-permute-start | bytes 491528 | tf_op jit(solution)/shard_map/ppermute | solution.py:401
  12.7 6.1 %collective-permute-start.3 = (bf16[5,128,128]{2,1,0:T(8,128)(2,1)S(1)}, bf16[5,128,128]{2,1,0:T(8,128)(2,1)S(1)}, u32[]{:S(2)}, u32[]{:S(2)}) collective-permute-start(bf16[5,128,128]{2,1,0:T(8,128)(2,1)S(1)} %collective-permute-done.2.refs_3_), channel_id=1, source_target_pairs={{0,1},{1,0},{2,3},{3,2},{4,5},{5,4},{6,7},{7,6},{8,9},{9,8},{10,11... | collective-permute-start | bytes 491528 | tf_op jit(solution)/shard_map/ppermute | solution.py:401
  14.0 5.5 %collective-permute-start.7 = (bf16[5,128,128]{2,1,0:T(8,128)(2,1)S(1)}, bf16[5,128,128]{2,1,0:T(8,128)(2,1)S(1)}, u32[]{:S(2)}, u32[]{:S(2)}) collective-permute-start(bf16[5,128,128]{2,1,0:T(8,128)(2,1)S(1)} %collective-permute-done.6.mine), channel_id=1, source_target_pairs={{0,1},{1,0},{2,3},{3,2},{4,5},{5,4},{6,7},{7,6},{8,9},{9,8},{10,11... | collective-permute-start | bytes 491528 | tf_op jit(solution)/shard_map/ppermute | solution.py:401
  15.2 5.5 %collective-permute-start.10 = (bf16[128,256]{1,0:T(8,128)(2,1)S(1)}, bf16[128,256]{1,0:T(8,128)(2,1)S(1)}, u32[]{:S(2)}, u32[]{:S(2)}) collective-permute-start(bf16[128,256]{1,0:T(8,128)(2,1)S(1)} %shard_map.47.surfaces.v0), channel_id=1, source_target_pairs={{0,6},{2,4},{4,2},{6,0},{8,14},{10,12},{12,10},{14,8},{1,7},{3,5},... | collective-permute-start | bytes 196616 | tf_op jit(solution)/shard_map/ppermute | solution.py:404
  17.9 4.3 %collective-permute-start.9 = (bf16[128,256]{1,0:T(8,128)(2,1)S(1)}, bf16[128,256]{1,0:T(8,128)(2,1)S(1)}, u32[]{:S(2)}, u32[]{:S(2)}) collective-permute-start(bf16[128,256]{1,0:T(8,128)(2,1)S(1)} %shard_map.47.surfaces.v0), channel_id=1, source_target_pairs={{0,4},{2,6},{4,0},{6,2},{8,12},{10,14},{12,8},{14,10},{1,5},{3,7},... | collective-permute-start | bytes 196616 | tf_op jit(solution)/shard_map/ppermute | solution.py:404
  18.3 4.3 %collective-permute-start.8 = (bf16[128,256]{1,0:T(8,128)(2,1)S(1)}, bf16[128,256]{1,0:T(8,128)(2,1)S(1)}, u32[]{:S(2)}, u32[]{:S(2)}) collective-permute-start(bf16[128,256]{1,0:T(8,128)(2,1)S(1)} %shard_map.47.surfaces.v0), channel_id=1, source_target_pairs={{0,2},{2,0},{4,6},{6,4},{8,10},{10,8},{12,14},{14,12},{1,3},{3,1},... | collective-permute-start | bytes 196616 | tf_op jit(solution)/shard_map/ppermute | solution.py:404
  19.5 14.8 %copy-start = (bf16[2,384,768]{2,1,0:T(8,128)(2,1)S(1)}, bf16[2,384,768]{2,1,0:T(8,128)(2,1)}, u32[]{:S(2)}) copy-start(bf16[2,384,768]{2,1,0:T(8,128)(2,1)} %green.5) | copy-start | bytes 3538948
  25.3 8.2 %collective-permute-start.11 = (bf16[256,256]{1,0:T(8,128)(2,1)S(1)}, bf16[256,256]{1,0:T(8,128)(2,1)S(1)}, u32[]{:S(2)}, u32[]{:S(2)}) collective-permute-start(bf16[256,256]{1,0:T(8,128)(2,1)S(1)} %get-tuple-element.21), channel_id=1, source_target_pairs={{0,8},{2,10},{4,12},{6,14},{8,0},{10,2},{12,4},{14,6},{1,9},{3,11}... | collective-permute-start | bytes 393224 | tf_op jit(solution)/shard_map/ppermute | solution.py:404
  34.2 1.3 %collective-permute-start.12 = (bf16[128,256]{1,0:T(8,128)(2,1)S(1)}, bf16[128,256]{1,0:T(8,128)(2,1)S(1)}, u32[]{:S(2)}, u32[]{:S(2)}) collective-permute-start(bf16[128,256]{1,0:T(8,128)(2,1)S(1)} %shard_map.52.own), channel_id=1, source_target_pairs={{0,1},{1,0},{2,3},{3,2},{4,5},{5,4},{6,7},{7,6},{8,9},{9,8},{10,11... | collective-permute-start | bytes 196616 | tf_op jit(solution)/shard_map/ppermute | solution.py:401

commit v3 on v2

--- a/solution.py
+++ b/solution.py
@@ -11,7 +11,8 @@
 F32 = jnp.float32
 BF16 = jnp.bfloat16
 GROUP = 4
-ORDER = (3, 1, 2)
+ORDER = (3, 2, 1)
+EARLY = 2
 
 
 def contract(x, matrix, across):
@@ -44,31 +45,39 @@
     return jnp.concatenate([x, turned(x)], axis=0)
 
 
-def apply_computed(columns, x):
-    high, low = split(stacked(columns))
-    x_high, x_low = split(x)
-    both = contract(jnp.concatenate([x_high, x_low], axis=0), high, False)
-    return both[: x.shape[0]] + both[x.shape[0] :] + contract(x_high, low, False)
-
-
-def pack_kernel(green, coupling, source, edge, pack, source_near, couple_near, sems):
-    row = lax.axis_index("row")
-    shard_rows, width = green.shape[1:]
-    surface = edge.shape[1]
-    rows = pl.ds(pl.multiple_of(row * (shard_rows - surface), surface), surface)
-    last = pl.ds(width - surface, surface)
-    copies = [
-        pltpu.make_async_copy(green.at[:, rows, pl.ds(0, surface)], pack.at[pl.ds(0, 2)], sems.at[0]),
-        pltpu.make_async_copy(green.at[:, rows, last], pack.at[pl.ds(2, 2)], sems.at[1]),
-        pltpu.make_async_copy(coupling.at[pl.ds(row, 1)], pack.at[pl.ds(4, 1)], sems.at[2]),
-        pltpu.make_async_copy(green.at[:, rows], edge, sems.at[3]),
-        pltpu.make_async_copy(source, source_near, sems.at[4]),
-        pltpu.make_async_copy(coupling, couple_near, sems.at[5]),
-    ]
+def run_copies(pairs, sems):
+    copies = [pltpu.make_async_copy(a, b, sems.at[n]) for n, (a, b) in enumerate(pairs)]
     for c in copies:
         c.start()
     for c in copies:
         c.wait()
+
+
+def own_rows(green, surface):
+    row = lax.axis_index("row")
+    return pl.ds(pl.multiple_of(row * (green.shape[1] - surface), surface), surface)
+
+
+def pack_kernel(green, coupling, pack, sems):
+    surface = pack.shape[1]
+    rows = own_rows(green, surface)
+    last = pl.ds(green.shape[2] - surface, surface)
+    part = pl.ds(lax.axis_index("row"), 1)
+    run_copies(
+        [
+            (green.at[:, rows, pl.ds(0, surface)], pack.at[pl.ds(0, 2)]),
+            (green.at[:, rows, last], pack.at[pl.ds(2, 2)]),
+            (coupling.at[part], pack.at[pl.ds(4, 1)]),
+        ],
+        sems,
+    )
+
+
+def near_kernel(green, coupling, source, pack, edge, source_near, couple_near, sems):
+    rows = own_rows(green, edge.shape[1])
+    run_copies(
+        [(green.at[:, rows], edge), (source, source_near), (coupling, couple_near)], sems
+    )
 
 
 def masked_source(count, own, other, surface):
@@ -121,10 +130,10 @@
     direct[...] = contract(green[0], above, False) + contract(green[1], below, False)
 
 
-def unit_columns(size):
+def unit_rows(start, count, size):
     eye = (
-        lax.broadcasted_iota(jnp.int32, (size, size), 0)
-        == lax.broadcasted_iota(jnp.int32, (size, size), 1)
+        start + lax.broadcasted_iota(jnp.int32, (count, size), 0)
+        == lax.broadcasted_iota(jnp.int32, (count, size), 1)
     ).astype(F32)
     return jnp.concatenate([eye, jnp.zeros_like(eye)], axis=1)
 
@@ -139,9 +148,9 @@
     return both[: x.shape[0]] + both[x.shape[0] :] + rest
 
 
-def columns_of(forms, index, name):
-    size = forms.shape[2] // 2
-    return forms[index, name, :size].astype(F32) + forms[index, name + 1, :size].astype(F32)
+def columns_of(forms, index, name, rows=None):
+    rows = pl.ds(0, forms.shape[2] // 2) if rows is None else rows
+    return forms[index, name, rows].astype(F32) + forms[index, name + 1, rows].astype(F32)
 
 
 def real_form(re, im):
@@ -215,9 +224,12 @@
 
 
 def solve_kernel(
-    last_k, _, mine, other, v0, v1, v2, v3,
-    forms, send, leaving, entering, here, after, shift, vectors, states, backs,
+    later, _, *refs
 ):
+    packed, given = refs[: 2 * len(later)], refs[2 * len(later) : 2 * len(later) + GROUP]
+    forms, send, send_map, leaving, entering, pi, sigma, response, shift, vectors, states, backs = refs[
+        2 * len(later) + GROUP :
+    ]
     row = lax.axis_index("row")
     slab = lax.axis_index("slab")
     slabs = lax.axis_size("slab")
@@ -225,18 +237,23 @@
     size = shift.shape[0]
     half = vectors.shape[1] // 2
 
+    def fill(first_is_own):
+        for n, k in enumerate(later):
+            form_packed(forms, k, packed[2 * n], packed[2 * n + 1], first_is_own)
+
     @pl.when(row == 0)
     def _():
-        form_packed(forms, last_k, mine, other, True)
+        fill(True)
 
     @pl.when(row == 1)
     def _():
-        form_packed(forms, last_k, mine, other, False)
-
-    for k, v in enumerate((v0, v1, v2, v3)):
+        fill(False)
+
+    for k, v in enumerate(given):
         vectors[member ^ k] = v[...]
     first = [vectors[i, :half] for i in range(GROUP)]
-    unit = unit_columns(size)
+    rows = pl.ds(pl.multiple_of(row * half, half), half)
+    unit = unit_rows(row * half, half, size)
     nothing = jnp.zeros_like(unit)
 
     def beside(x, below=nothing):
@@ -250,7 +267,7 @@
             term = term + contract(first[i + 1], forms[member ^ i, SHIFT + 1], False)
         terms.append(term)
     states[0] = beside(jnp.zeros_like(terms[0]), unit)
-    u = beside(terms[0], columns_of(forms, member, ALONG))
+    u = beside(terms[0], columns_of(forms, member, ALONG, rows))
     for i in range(1, GROUP - 1):
         states[i] = u
         u = apply_pair(u, forms, member ^ i, ALONG) + beside(terms[i])
@@ -275,19 +292,21 @@
         s = e + apply_pair(s, forms, member ^ i, BACK)
         backs[i] = s
     entering[...] = s
-    w = columns_of(forms, last, SHIFT)
-    shift[...] = w
+    shift[...] = columns_of(forms, last, SHIFT)
     left = slab < slabs // 2
     send[:half] = jnp.where(left, u[:half], s[:half]).astype(BF16)
-    send[half : 2 * half] = first[0]
-    send[2 * half :] = jnp.where(left, w, s[half:]).astype(BF16)
-    here[...] = states[member]
-    after[...] = backs[member + 1]
+    send[half:] = first[0]
+    send_map[...] = jnp.where(left, columns_of(forms, last, SHIFT, rows), s[half:]).astype(BF16)
+    here, after = states[member], backs[member + 1]
+    pi[...] = here[:half]
+    sigma[...] = after[:half]
+    response[:half] = here[half:]
+    response[half:] = after[half:]
 
 
 def gamma_kernel(forms, gamma, whole, backs):
     member = lax.axis_index("slab") % GROUP
-    backs[GROUP] = unit_columns(gamma.shape[0])
+    backs[GROUP] = unit_rows(0, gamma.shape[0], gamma.shape[0])
     s = columns_of(forms, member ^ (GROUP - 1), BACK)
     backs[GROUP - 1] = s
     for i in reversed(range(GROUP - 1)):
@@ -297,28 +316,70 @@
     gamma[...] = backs[member + 1]
 
 
-def close_kernel(coupling, leaving, first, seen, shift, here, after, gamma, out):
+def ready_kernel(coupling, sigma, response, response_other, gamma, shift, hand, base, whole):
+    row = lax.axis_index("row")
+    half = base.shape[0]
+    left = lax.axis_index("slab") < lax.axis_size("slab") // 2
+    b = real_form(coupling[0], coupling[1])
+
+    def place(first, second):
+        for i in range(2):
+            whole[i, :half] = first[i * half : (i + 1) * half]
+            whole[i, half:] = second[i * half : (i + 1) * half]
+
+    @pl.when(row == 0)
+    def _():
+        place(response, response_other)
+
+    @pl.when(row == 1)
+    def _():
+        place(response_other, response)
+
+    def keep(index, x):
+        hand[index], hand[index + 1] = split(stacked(x))
+
+    keep(0, jnp.where(left, shift[...], whole[0]))
+    keep(2, apply(b, jnp.where(left, gamma[...], whole[1])))
+    base[...] = apply(b, sigma[...])
+
+
+def close_kernel(hand, base, pi, leaving, first, seen, map_seen, map_other, out, rows):
+    row = lax.axis_index("row")
     half = first.shape[0]
+    part = map_seen.shape[0]
     left = lax.axis_index("slab") < lax.axis_size("slab") // 2
     there = seen[:half].astype(F32)
-    map_form = stacked(seen[2 * half :].astype(F32)).astype(BF16)
-    b = real_form(coupling[0], coupling[1])
+
+    @pl.when(row == 0)
+    def _():
+        rows[:part] = map_seen[...]
+        rows[part:] = map_other[...]
+
+    @pl.when(row == 1)
+    def _():
+        rows[:part] = map_other[...]
+        rows[part:] = map_seen[...]
+
+    map_form = stacked(rows[...])
+
+    def times(x, index):
+        high, low = split(x)
+        both = contract(jnp.concatenate([high, low], axis=0), hand[index], False)
+        return both[:half] + both[half:] + contract(high, hand[index + 1], False)
 
     @pl.when(left)
     def _():
-        ahead = seen[half : 2 * half].astype(F32)
-        past = leaving[:half] + apply_computed(shift[...], ahead)
+        ahead = seen[half:]
+        past = leaving[:half] + contract(ahead, hand[0], False) + contract(ahead, hand[1], False)
         entry = there + apply(map_form, past, False)
-        behind = after[:half] + apply_computed(gamma[...], entry)
-        out[:half] = here[:half].astype(BF16)
-        out[half:] = apply(b, behind).astype(BF16)
+        out[:half] = pi[...].astype(BF16)
+        out[half:] = (base[...] + times(entry, 2)).astype(BF16)
 
     @pl.when(jnp.logical_not(left))
     def _():
         before = there + apply_short(map_form, first[...], False)
-        behind = after[:half] + apply_computed(after[half:], before)
-        out[:half] = (here[:half] + apply_computed(here[half:], before)).astype(BF16)
-        out[half:] = apply(b, behind).astype(BF16)
+        out[:half] = (pi[...] + times(before, 0)).astype(BF16)
+        out[half:] = (base[...] + times(before, 2)).astype(BF16)
 
 
 def final_kernel(count, green, direct, own, other, result, whole):
@@ -341,14 +402,11 @@
     def _():
         place(other, own)
 
-    def product(start, x):
-        g = jnp.concatenate(
-            [green[0, :, start : start + surface], green[1, :, start : start + surface]], axis=1
-        )
-        x_re, x_im = x[:, :surface], x[:, surface:]
-        return contract(g, real_form(x_re, x_im), True)
-
-    total = direct[...] + product(0, whole[0]) + product(width - surface, whole[1])
+    total = direct[...]
+    for start, x in ((0, whole[0]), (width - surface, whole[1])):
+        cols = slice(start, start + surface)
+        g = jnp.concatenate([green[0, :, cols], green[1, :, cols]], axis=1)
+        total = total + contract(g, real_form(x[:, :surface], x[:, surface:]), True)
     orbital = row * shard_rows + lax.broadcasted_iota(jnp.int32, total.shape, 0)
     limit = jnp.concatenate([count[:1]] * (total.shape[1] // count.shape[1]), axis=1)
     live = (orbital < surface + limit) | (orbital >= width - surface)
@@ -404,20 +462,24 @@
         return lax.ppermute(x, "slab", [(i, i ^ bit) for i in range(slabs)])
 
     square = (surface, 2 * surface)
-    joint = (half + surface, 2 * surface)
-    edge, pack, source_near, couple_near = call(
+    thin, joint = (half, 2 * surface), (columns, 2 * surface)
+    (pack,) = call(
         pack_kernel,
-        [H] * 3,
-        [
-            ((2, surface, width), BF16),
-            ((5, surface, surface), BF16),
-            (source.shape, BF16),
-            (coupling.shape, BF16),
-        ],
-        [pltpu.SemaphoreType.DMA((6,))],
+        [H] * 2,
+        [((5, surface, surface), BF16)],
+        [pltpu.SemaphoreType.DMA((3,))],
+        green_blocks,
+        coupling,
+    )
+    edge, source_near, couple_near = call(
+        near_kernel,
+        [H] * 3 + [V],
+        [((2, surface, width), BF16), (source.shape, BF16), (coupling.shape, BF16)],
+        [pltpu.SemaphoreType.DMA((3,))],
         green_blocks,
         coupling,
         source,
+        pack,
     )
     count = jnp.broadcast_to(interior_count.reshape(1, 1), (8, columns))
     source_other = across(source_near)
@@ -453,32 +515,32 @@
     swapped = {}
     for k in ORDER:
         swapped[k] = across(packs[k])
-    both = [x for k in ORDER[:-1] for x in (packs[k], swapped[k])]
+    sooner, later = ORDER[:EARLY], ORDER[EARLY:]
     forms_shape = ((GROUP, 8, 2 * surface, 2 * surface), BF16)
     (forms,) = call(
-        functools.partial(form_kernel, ORDER[:-1]),
-        [V] * (3 + len(both)),
+        functools.partial(form_kernel, sooner),
+        [V] * (3 + 2 * len(sooner)),
         [forms_shape],
         [],
         edge,
         edge_other,
         couple_near,
-        *both,
-    )
-    forms, send, leaving, entering, here, after, shift = call(
-        functools.partial(solve_kernel, ORDER[-1]),
-        [V] * (3 + GROUP),
-        [forms_shape, ((columns + surface, 2 * surface), BF16)]
-        + [(joint, F32)] * 4
-        + [(square, F32)],
+        *(x for k in sooner for x in (packs[k], swapped[k])),
+    )
+    forms, send, send_map, leaving, entering, pi, sigma, response, shift = call(
+        functools.partial(solve_kernel, later),
+        [V] * (1 + 2 * len(later) + GROUP),
+        [forms_shape, ((columns, 2 * surface), BF16), (thin, BF16)]
+        + [(joint, F32)] * 2
+        + [(thin, F32)] * 2
+        + [(joint, F32), (square, F32)],
         [
             ((GROUP, columns, 2 * surface), BF16),
             ((GROUP,) + joint, F32),
             ((GROUP + 1,) + joint, F32),
         ],
         forms,
-        packs[ORDER[-1]],
-        swapped[ORDER[-1]],
+        *(x for k in later for x in (packs[k], swapped[k])),
         vectors,
         *gathered,
         aliases={0: 0},
@@ -490,9 +552,17 @@
     bit = GROUP
     if 2 * bit < slabs:
         first = first.astype(F32)
-        leave, a_map = leaving[:half], leaving[half:]
-        back, d_map = entering[:half], entering[half:]
-        pi, alpha, sigma, delta = here[:half], here[half:], after[:half], after[half:]
+        row = lax.axis_index("row")
+
+        def joined(part):
+            other = across(part)
+            return jnp.where(
+                row == 0, jnp.concatenate([part, other], 0), jnp.concatenate([other, part], 0)
+            )
+
+        leave, a_map = leaving[:half], joined(leaving[half:])
+        back, d_map = entering[:half], joined(entering[half:])
+        alpha, delta = joined(response[:half]), joined(response[half:])
         c_map = back_whole
     while 2 * bit < slabs:
         right = (slab // bit) % 2 == 1
@@ -518,26 +588,47 @@
         bit *= 2
         if 2 * bit == slabs:
             left = slab < slabs // 2
-            parts = [jnp.where(left, leave, back), first, jnp.where(left, shift, d_map)]
-            send = jnp.concatenate(parts, axis=0).astype(BF16)
+            send = jnp.concatenate([jnp.where(left, leave, back), first], axis=0).astype(BF16)
+            send_map = lax.dynamic_slice_in_dim(
+                jnp.where(left, shift, d_map).astype(BF16),
+                row * half,
+                half,
+                0,
+            )
             first = first.astype(BF16)
-            leaving = jnp.concatenate([leave, a_map], axis=0)
-            here = jnp.concatenate([pi, alpha], axis=0)
-            after = jnp.concatenate([sigma, delta], axis=0)
+            leaving = jnp.concatenate([leave, leave], axis=0)
+            response = jnp.concatenate(
+                [lax.dynamic_slice_in_dim(x, row * half, half, 0) for x in (alpha, delta)], axis=0
+            )
+    map_seen = partner(send_map, slabs // 2)
     seen = partner(send, slabs // 2)
+    response_other = across(response)
+    map_other = across(map_seen)
+    hand, base = call(
+        ready_kernel,
+        [V] * 6,
+        [((4, 2 * surface, 2 * surface), BF16), (thin, F32)],
+        [((2,) + square, F32)],
+        couple_near,
+        sigma,
+        response,
+        response_other,
+        gamma,
+        shift,
+    )
     (closed,) = call(
         close_kernel,
         [V] * 8,
         [((columns, 2 * surface), BF16)],
-        [],
-        couple_near,
+        [((surface, 2 * surface), BF16)],
+        hand,
+        base,
+        pi,
         leaving,
         first,
         seen,
-        shift,
-        here,
-        after,
-        gamma,
+        map_seen,
+        map_other,
     )
     (result,) = call(
         final_kernel,

time: 36.7 us -> 38.9 us (1.060)
  waiting for transfers between devices: 15.8 us -> 17.3 us
  Pallas kernels: 8.58 us -> 9.32 us
    ppermute x7 -> x8, waiting for transfers between devices: 15 us -> 16.6 us  [partner(): return lax.ppermute(x, 'slab', [(i, i ^ bit) for i in range(slabs)])]
    pallas_call x8 -> x10, Pallas kernels: 8.58 us -> 9.32 us  [call(): pl.pallas_call(kernel, in_specs=specs, out_specs=[V] * len(outs), out_sha...]
    ppermute x6 -> x8, starting transfers between devices: 1.14 us -> 0.66 us  [across(): return lax.ppermute(x, 'row', [(0, 1), (1, 0)])]
    ppermute x7 -> x8, starting transfers between devices: 10.3 us -> 10.7 us  [partner(): return lax.ppermute(x, 'slab', [(i, i ^ bit) for i in range(slabs)])]
  transfers between devices with their start and end apart: 13 -> 16, of which waited for: 7 -> 9; matrix products, arithmetic and copies ran while one was open for 0% -> 0% of each run, Pallas kernels for 8% -> 8%
where the time goes in v3:
time: 38.9 us; the launch traced here: 38.7 us
  waiting for transfers between devices  17.3 us (44%)
  starting transfers between devices  11.3 us (29%)
  Pallas kernels  9.32 us (24%)
  between operations  0.78 us (2%)
    ppermute x8, waiting for transfers between devices, partner(): return lax.ppermute(x, 'slab', [(i, i ^ bit) for i in range(slabs)])  16.6 us
    ppermute x8, starting transfers between devices, partner(): return lax.ppermute(x, 'slab', [(i, i ^ bit) for i in range(slabs)])  10.7 us
    pallas_call x10, Pallas kernels, call(): pl.pallas_call(kernel, in_specs=specs, out_specs=[V] * len(outs), out_sha...  9.32 us
  transfers between devices with their start and end apart: 16, of which 9 were waited for; matrix products, arithmetic and copies ran while one was open for 0% of the time, Pallas kernels for 8%

profile of v3, /device:TPU:0, one launch (start us, length us, event | category | flops | bytes accessed | tf_op | source)
XLA Modules:
  0.0 38.7 jit_solution(8443993012966697909)
XLA Ops:
  0.0 0.9 %shard_map.46.pack = bf16[5,128,128]{2,1,0:T(8,128)(2,1)S(1)} custom-call(bf16[2,384,768]{2,1,0:T(8,128)(2,1)} %green.7, bf16[2,128,128]{2,1,0:T(8,128)(2,1)} %coupling.3), custom_call_target="tpu_custom_call" | custom-call | tf_op jit(solution)/shard_map/pallas_call | solution.py:427
  0.9 1.1 %shard_map.47 = (bf16[2,128,768]{2,1,0:T(8,128)(2,1)S(1)}, bf16[2,384,128]{2,1,0:T(8,128)(2,1)S(1)}, bf16[2,128,128]{2,1,0:T(8,128)(2,1)S(1)}) custom-call(bf16[2,384,768]{2,1,0:T(8,128)(2,1)} %green.7, bf16[2,128,128]{2,1,0:T(8,128)(2,1)} %coupling.3, bf16[2,384,128]{2,1,0:T(8,128)(2,1)} %source.1, bf16[5,128,128]{2,1,0:T(8,128)(2,1)S(1)} %shard_map.46.pack), custom_call_target="tpu_custom_call" | custom-call | tf_op jit(solution)/shard_map/pallas_call | solution.py:427
  2.0 0.6 %collective-permute-start.1 = (bf16[2,128,768]{2,1,0:T(8,128)(2,1)S(1)}, bf16[2,128,768]{2,1,0:T(8,128)(2,1)S(1)}, u32[]{:S(2)}, u32[]{:S(2)}) collective-permute-start(bf16[2,128,768]{2,1,0:T(8,128)(2,1)S(1)} %get-tuple-element.20.edge.refs_0_), channel_id=1, source_target_pairs={{0,1},{1,0},{2,3},{3,2},{4,5},{5,4},{6,7},{7,6},{8,9},{9,8},{10,11... | collective-permute-start | bytes 1179656 | tf_op jit(solution)/shard_map/ppermute | solution.py:459
  2.6 2.6 %collective-permute-start.4 = (bf16[5,128,128]{2,1,0:T(8,128)(2,1)S(1)}, bf16[5,128,128]{2,1,0:T(8,128)(2,1)S(1)}, u32[]{:S(2)}, u32[]{:S(2)}) collective-permute-start(bf16[5,128,128]{2,1,0:T(8,128)(2,1)S(1)} %shard_map.46.pack), channel_id=1, source_target_pairs={{0,4},{2,6},{4,0},{6,2},{8,12},{10,14},{12,8},{14,10},{1,5},{3,7},... | collective-permute-start | bytes 491528 | tf_op jit(solution)/shard_map/ppermute | solution.py:462
  5.2 1.4 %collective-permute-start.2 = (bf16[5,128,128]{2,1,0:T(8,128)(2,1)S(1)}, bf16[5,128,128]{2,1,0:T(8,128)(2,1)S(1)}, u32[]{:S(2)}, u32[]{:S(2)}) collective-permute-start(bf16[5,128,128]{2,1,0:T(8,128)(2,1)S(1)} %shard_map.46.pack), channel_id=1, source_target_pairs={{0,6},{2,4},{4,2},{6,0},{8,14},{10,12},{12,10},{14,8},{1,7},{3,5},... | collective-permute-start | bytes 491528 | tf_op jit(solution)/shard_map/ppermute | solution.py:462
  6.8 3.5 %collective-permute-done.4.refs_5_ = bf16[5,128,128]{2,1,0:T(8,128)(2,1)S(1)} collective-permute-done((bf16[5,128,128]{2,1,0:T(8,128)(2,1)S(1)}, bf16[5,128,128]{2,1,0:T(8,128)(2,1)S(1)}, u32[]{:S(2)}, u32[]{:S(2)}) %collective-permute-start.4) | collective-permute-done | bytes 163872 | tf_op jit(solution)/shard_map/ppermute | solution.py:462
  10.3 4.5 %collective-permute-done.2.refs_3_ = bf16[5,128,128]{2,1,0:T(8,128)(2,1)S(1)} collective-permute-done((bf16[5,128,128]{2,1,0:T(8,128)(2,1)S(1)}, bf16[5,128,128]{2,1,0:T(8,128)(2,1)S(1)}, u32[]{:S(2)}, u32[]{:S(2)}) %collective-permute-start.2) | collective-permute-done | bytes 163872 | tf_op jit(solution)/shard_map/ppermute | solution.py:462
  14.7 1.4 %collective-permute-done.6.refs_0_ = bf16[5,128,128]{2,1,0:T(8,128)(2,1)S(1)} collective-permute-done((bf16[5,128,128]{2,1,0:T(8,128)(2,1)S(1)}, bf16[5,128,128]{2,1,0:T(8,128)(2,1)S(1)}, u32[]{:S(2)}, u32[]{:S(2)}) %collective-permute-start.6) | collective-permute-done | bytes 163872 | tf_op jit(solution)/shard_map/ppermute | solution.py:462
  16.8 0.5 %shard_map.48.surfaces.refs_2_ = bf16[128,256]{1,0:T(8,128)(2,1)S(1)} custom-call(s32[8,128]{1,0:T(8,128)S(1)} %broadcast_in_dim.8.count, bf16[2,128,768]{2,1,0:T(8,128)(2,1)S(1)} %get-tuple-element.20.edge.refs_0_, bf16[2,128,768]{2,1,0:T(8,128)(2,1)S(1)} %collective-permute-done.1.edge_other.refs_1_, ...), custom_call_target="tpu_custom_call" | custom-call | tf_op jit(solution)/shard_map/pallas_call | solution.py:427
  17.3 1.6 %collective-permute-start.10 = (bf16[128,256]{1,0:T(8,128)(2,1)S(1)}, bf16[128,256]{1,0:T(8,128)(2,1)S(1)}, u32[]{:S(2)}, u32[]{:S(2)}) collective-permute-start(bf16[128,256]{1,0:T(8,128)(2,1)S(1)} %shard_map.48.surfaces.refs_2_), channel_id=1, source_target_pairs={{0,6},{2,4},{4,2},{6,0},{8,14},{10,12},{12,10},{14,8},{1,7},{3,5},... | collective-permute-start | bytes 196616 | tf_op jit(solution)/shard_map/ppermute | solution.py:462
  19.2 1.6 %collective-permute-start.8 = (bf16[128,256]{1,0:T(8,128)(2,1)S(1)}, bf16[128,256]{1,0:T(8,128)(2,1)S(1)}, u32[]{:S(2)}, u32[]{:S(2)}) collective-permute-start(bf16[128,256]{1,0:T(8,128)(2,1)S(1)} %shard_map.48.surfaces.refs_2_), channel_id=1, source_target_pairs={{0,2},{2,0},{4,6},{6,4},{8,10},{10,8},{12,14},{14,12},{1,3},{3,1},... | collective-permute-start | bytes 196616 | tf_op jit(solution)/shard_map/ppermute | solution.py:462
  20.9 0.7 %shard_map.50._ = bf16[4,8,256,256]{3,2,1,0:T(8,128)(2,1)S(1)} custom-call(bf16[2,128,768]{2,1,0:T(8,128)(2,1)S(1)} %get-tuple-element.20.edge.refs_0_, bf16[2,128,768]{2,1,0:T(8,128)(2,1)S(1)} %collective-permute-done.1.edge_other.refs_1_, bf16[2,128,128]{2,1,0:T(8,128)(2,1)S(1)} %get-tuple-element.21.refs_2_.coupling, ...), custom_call_target="tpu_custom_call" | custom-call | tf_op jit(solution)/shard_map/pallas_call | solution.py:427
  21.6 1.3 %collective-permute-done.10.refs_5_ = bf16[128,256]{1,0:T(8,128)(2,1)S(1)} collective-permute-done((bf16[128,256]{1,0:T(8,128)(2,1)S(1)}, bf16[128,256]{1,0:T(8,128)(2,1)S(1)}, u32[]{:S(2)}, u32[]{:S(2)}) %collective-permute-start.10) | collective-permute-done | bytes 65568 | tf_op jit(solution)/shard_map/ppermute | solution.py:462
  23.1 1.0 %collective-permute-done.8.refs_3_ = bf16[128,256]{1,0:T(8,128)(2,1)S(1)} collective-permute-done((bf16[128,256]{1,0:T(8,128)(2,1)S(1)}, bf16[128,256]{1,0:T(8,128)(2,1)S(1)}, u32[]{:S(2)}, u32[]{:S(2)}) %collective-permute-start.8) | collective-permute-done | bytes 65568 | tf_op jit(solution)/shard_map/ppermute | solution.py:462
  24.2 2.5 %shard_map.51 = (bf16[4,8,256,256]{3,2,1,0:T(8,128)(2,1)S(1)}, bf16[128,256]{1,0:T(8,128)(2,1)S(1)}, bf16[64,256]{1,0:T(8,128)(2,1)S(1)}, f32[128,256]{1,0:T(8,1...) custom-call(bf16[4,8,256,256]{3,2,1,0:T(8,128)(2,1)S(1)} %shard_map., ...), custom_call_target="tpu_custom_call", output_to_operand_aliasing={{0}: (0, {})} | custom-call | tf_op jit(solution)/shard_map/pallas_call | solution.py:427
  26.7 2.6 %collective-permute-start.13 = (bf16[64,256]{1,0:T(8,128)(2,1)S(1)}, bf16[64,256]{1,0:T(8,128)(2,1)S(1)}, u32[]{:S(2)}, u32[]{:S(2)}) collective-permute-start(bf16[64,256]{1,0:T(8,128)(2,1)S(1)} %get-tuple-element.32), channel_id=1, source_target_pairs={{0,8},{2,10},{4,12},{6,14},{8,0},{10,2},{12,4},{14,6},{1,9},{3,11}... | collective-permute-start | bytes 98312 | tf_op jit(solution)/shard_map/ppermute | solution.py:462
  29.3 0.4 collective-permute-start.12
  29.6 1.9 %collective-permute-done.13.map_seen = bf16[64,256]{1,0:T(8,128)(2,1)S(1)} collective-permute-done((bf16[64,256]{1,0:T(8,128)(2,1)S(1)}, bf16[64,256]{1,0:T(8,128)(2,1)S(1)}, u32[]{:S(2)}, u32[]{:S(2)}) %collective-permute-start.13) | collective-permute-done | bytes 32800 | tf_op jit(solution)/shard_map/ppermute | solution.py:462
  31.5 1.3 %shard_map.52 = (f32[128,256]{1,0:T(8,128)S(1)}, f32[128,256]{1,0:T(8,128)}) custom-call(bf16[4,8,256,256]{3,2,1,0:T(8,128)(2,1)S(1)} %get-tuple-element.24.forms), custom_call_target="tpu_custom_call" | custom-call | tf_op jit(solution)/shard_map/pallas_call | solution.py:427
  33.1 2.7 %collective-permute-done.12.seen = bf16[128,256]{1,0:T(8,128)(2,1)S(1)} collective-permute-done((bf16[128,256]{1,0:T(8,128)(2,1)S(1)}, bf16[128,256]{1,0:T(8,128)(2,1)S(1)}, u32[]{:S(2)}, u32[]{:S(2)}) %collective-permute-start.12) | collective-permute-done | bytes 65568 | tf_op jit(solution)/shard_map/ppermute | solution.py:462
  35.8 0.5 %shard_map.54.own = bf16[128,256]{1,0:T(8,128)(2,1)S(1)} custom-call(bf16[4,256,256]{2,1,0:T(8,128)(2,1)S(1)} %get-tuple-element.27.hand, f32[64,256]{1,0:T(8,128)S(1)} %get-tuple-element.28.base, f32[64,256]{1,0:T(8,128)S(1)} %get-tuple-element.29.pi, f32[128,256]{1,0:T(8,128)S(1)} %get-tuple-element.30.leaving, bf16[64,256]{1,0:T(8,128)(2,1)S(1)} %slice.3.first, ...), custom_call_target="tpu_custom_call" | custom-call | tf_op jit(solution)/shard_map/pallas_call | solution.py:427
  36.4 0.5 %shard_map.49.direct = f32[384,256]{1,0:T(8,128)S(1)} custom-call(s32[8,128]{1,0:T(8,128)S(1)} %broadcast_in_dim.8.count, bf16[2,384,768]{2,1,0:T(8,128)(2,1)S(1)} %copy-done, bf16[2,384,128]{2,1,0:T(8,128)(2,1)S(1)} %get-tuple-element.19.source_own, bf16[2,384,128]{2,1,0:T(8,128)(2,1)S(1)} %collective-permute-done.source_other, ...), custom_call_target="tpu_custom_call" | custom-call | tf_op jit(solution)/shard_map/pallas_call | solution.py:427
  36.9 0.7 %collective-permute-done.15.other = bf16[128,256]{1,0:T(8,128)(2,1)S(1)} collective-permute-done((bf16[128,256]{1,0:T(8,128)(2,1)S(1)}, bf16[128,256]{1,0:T(8,128)(2,1)S(1)}, u32[]{:S(2)}, u32[]{:S(2)}) %collective-permute-start.15) | collective-permute-done | bytes 65568 | tf_op jit(solution)/shard_map/ppermute | solution.py:459
  37.7 1.1 %shard_map.55 = f32[2,384,128]{2,1,0:T(8,128)} custom-call(s32[8,128]{1,0:T(8,128)S(1)} %broadcast_in_dim.8.count, bf16[2,384,768]{2,1,0:T(8,128)(2,1)S(1)} %copy-done, f32[384,256]{1,0:T(8,128)S(1)} %shard_map.49.direct, bf16[128,256]{1,0:T(8,128)(2,1)S(1)} %shard_map.54.own, bf16[128,256]{1,0:T(8,128)(2,1)S(1)} %collective-permute-done.15.other), custom_call_target="tpu_custom_call" | custom-call | tf_op jit(solution)/shard_map/pallas_call | solution.py:427
  (22 shorter events, 1.2 us)
Async XLA Ops:
  2.0 14.8 %collective-permute-start.1 = (bf16[2,128,768]{2,1,0:T(8,128)(2,1)S(1)}, bf16[2,128,768]{2,1,0:T(8,128)(2,1)S(1)}, u32[]{:S(2)}, u32[]{:S(2)}) collective-permute-start(bf16[2,128,768]{2,1,0:T(8,128)(2,1)S(1)} %get-tuple-element.20.edge.refs_0_), channel_id=1, source_target_pairs={{0,1},{1,0},{2,3},{3,2},{4,5},{5,4},{6,7},{7,6},{8,9},{9,8},{10,11... | collective-permute-start | bytes 1179656 | tf_op jit(solution)/shard_map/ppermute | solution.py:459
  2.6 7.7 %collective-permute-start.4 = (bf16[5,128,128]{2,1,0:T(8,128)(2,1)S(1)}, bf16[5,128,128]{2,1,0:T(8,128)(2,1)S(1)}, u32[]{:S(2)}, u32[]{:S(2)}) collective-permute-start(bf16[5,128,128]{2,1,0:T(8,128)(2,1)S(1)} %shard_map.46.pack), channel_id=1, source_target_pairs={{0,4},{2,6},{4,0},{6,2},{8,12},{10,14},{12,8},{14,10},{1,5},{3,7},... | collective-permute-start | bytes 491528 | tf_op jit(solution)/shard_map/ppermute | solution.py:462
  5.2 9.5 %collective-permute-start.2 = (bf16[5,128,128]{2,1,0:T(8,128)(2,1)S(1)}, bf16[5,128,128]{2,1,0:T(8,128)(2,1)S(1)}, u32[]{:S(2)}, u32[]{:S(2)}) collective-permute-start(bf16[5,128,128]{2,1,0:T(8,128)(2,1)S(1)} %shard_map.46.pack), channel_id=1, source_target_pairs={{0,6},{2,4},{4,2},{6,0},{8,14},{10,12},{12,10},{14,8},{1,7},{3,5},... | collective-permute-start | bytes 491528 | tf_op jit(solution)/shard_map/ppermute | solution.py:462
  6.6 9.5 %collective-permute-start.6 = (bf16[5,128,128]{2,1,0:T(8,128)(2,1)S(1)}, bf16[5,128,128]{2,1,0:T(8,128)(2,1)S(1)}, u32[]{:S(2)}, u32[]{:S(2)}) collective-permute-start(bf16[5,128,128]{2,1,0:T(8,128)(2,1)S(1)} %shard_map.46.pack), channel_id=1, source_target_pairs={{0,2},{2,0},{4,6},{6,4},{8,10},{10,8},{12,14},{14,12},{1,3},{3,1},... | collective-permute-start | bytes 491528 | tf_op jit(solution)/shard_map/ppermute | solution.py:462
  6.7 10.0 %collective-permute-start = (bf16[2,384,128]{2,1,0:T(8,128)(2,1)S(1)}, bf16[2,384,128]{2,1,0:T(8,128)(2,1)S(1)}, u32[]{:S(2)}, u32[]{:S(2)}) collective-permute-start(bf16[2,384,128]{2,1,0:T(8,128)(2,1)S(1)} %get-tuple-element.19.source_own), channel_id=1, source_target_pairs={{0,1},{1,0},{2,3},{3,2},{4,5},{5,4},{6,7},{7,6},{8,9},{9,8},{10,11... | collective-permute-start | bytes 589832 | tf_op jit(solution)/shard_map/ppermute | solution.py:459
  10.3 9.0 %collective-permute-start.5 = (bf16[5,128,128]{2,1,0:T(8,128)(2,1)S(1)}, bf16[5,128,128]{2,1,0:T(8,128)(2,1)S(1)}, u32[]{:S(2)}, u32[]{:S(2)}) collective-permute-start(bf16[5,128,128]{2,1,0:T(8,128)(2,1)S(1)} %collective-permute-done.4.refs_5_), channel_id=1, source_target_pairs={{0,1},{1,0},{2,3},{3,2},{4,5},{5,4},{6,7},{7,6},{8,9},{9,8},{10,11... | collective-permute-start | bytes 491528 | tf_op jit(solution)/shard_map/ppermute | solution.py:459
  14.7 6.1 %collective-permute-start.3 = (bf16[5,128,128]{2,1,0:T(8,128)(2,1)S(1)}, bf16[5,128,128]{2,1,0:T(8,128)(2,1)S(1)}, u32[]{:S(2)}, u32[]{:S(2)}) collective-permute-start(bf16[5,128,128]{2,1,0:T(8,128)(2,1)S(1)} %collective-permute-done.2.refs_3_), channel_id=1, source_target_pairs={{0,1},{1,0},{2,3},{3,2},{4,5},{5,4},{6,7},{7,6},{8,9},{9,8},{10,11... | collective-permute-start | bytes 491528 | tf_op jit(solution)/shard_map/ppermute | solution.py:459
  16.1 5.5 %collective-permute-start.7 = (bf16[5,128,128]{2,1,0:T(8,128)(2,1)S(1)}, bf16[5,128,128]{2,1,0:T(8,128)(2,1)S(1)}, u32[]{:S(2)}, u32[]{:S(2)}) collective-permute-start(bf16[5,128,128]{2,1,0:T(8,128)(2,1)S(1)} %collective-permute-done.6.refs_0_), channel_id=1, source_target_pairs={{0,1},{1,0},{2,3},{3,2},{4,5},{5,4},{6,7},{7,6},{8,9},{9,8},{10,11... | collective-permute-start | bytes 491528 | tf_op jit(solution)/shard_map/ppermute | solution.py:459
  17.3 5.6 %collective-permute-start.10 = (bf16[128,256]{1,0:T(8,128)(2,1)S(1)}, bf16[128,256]{1,0:T(8,128)(2,1)S(1)}, u32[]{:S(2)}, u32[]{:S(2)}) collective-permute-start(bf16[128,256]{1,0:T(8,128)(2,1)S(1)} %shard_map.48.surfaces.refs_2_), channel_id=1, source_target_pairs={{0,6},{2,4},{4,2},{6,0},{8,14},{10,12},{12,10},{14,8},{1,7},{3,5},... | collective-permute-start | bytes 196616 | tf_op jit(solution)/shard_map/ppermute | solution.py:462
  18.9 4.3 %collective-permute-start.9 = (bf16[128,256]{1,0:T(8,128)(2,1)S(1)}, bf16[128,256]{1,0:T(8,128)(2,1)S(1)}, u32[]{:S(2)}, u32[]{:S(2)}) collective-permute-start(bf16[128,256]{1,0:T(8,128)(2,1)S(1)} %shard_map.48.surfaces.refs_2_), channel_id=1, source_target_pairs={{0,4},{2,6},{4,0},{6,2},{8,12},{10,14},{12,8},{14,10},{1,5},{3,7},... | collective-permute-start | bytes 196616 | tf_op jit(solution)/shard_map/ppermute | solution.py:462
  19.2 4.9 %collective-permute-start.8 = (bf16[128,256]{1,0:T(8,128)(2,1)S(1)}, bf16[128,256]{1,0:T(8,128)(2,1)S(1)}, u32[]{:S(2)}, u32[]{:S(2)}) collective-permute-start(bf16[128,256]{1,0:T(8,128)(2,1)S(1)} %shard_map.48.surfaces.refs_2_), channel_id=1, source_target_pairs={{0,2},{2,0},{4,6},{6,4},{8,10},{10,8},{12,14},{14,12},{1,3},{3,1},... | collective-permute-start | bytes 196616 | tf_op jit(solution)/shard_map/ppermute | solution.py:462
  21.6 14.9 %copy-start = (bf16[2,384,768]{2,1,0:T(8,128)(2,1)S(1)}, bf16[2,384,768]{2,1,0:T(8,128)(2,1)}, u32[]{:S(2)}) copy-start(bf16[2,384,768]{2,1,0:T(8,128)(2,1)} %green.7) | copy-start | bytes 3538948
  26.7 6.1 %collective-permute-start.11 = (f32[128,256]{1,0:T(8,128)S(1)}, f32[128,256]{1,0:T(8,128)S(1)}, u32[]{:S(2)}, u32[]{:S(2)}) collective-permute-start(f32[128,256]{1,0:T(8,128)S(1)} %get-tuple-element.23.response), channel_id=1, source_target_pairs={{0,1},{1,0},{2,3},{3,2},{4,5},{5,4},{6,7},{7,6},{8,9},{9,8},{10,11... | collective-permute-start | bytes 393224 | tf_op jit(solution)/shard_map/ppermute | solution.py:459
  26.7 4.8 %collective-permute-start.13 = (bf16[64,256]{1,0:T(8,128)(2,1)S(1)}, bf16[64,256]{1,0:T(8,128)(2,1)S(1)}, u32[]{:S(2)}, u32[]{:S(2)}) collective-permute-start(bf16[64,256]{1,0:T(8,128)(2,1)S(1)} %get-tuple-element.32), channel_id=1, source_target_pairs={{0,8},{2,10},{4,12},{6,14},{8,0},{10,2},{12,4},{14,6},{1,9},{3,11}... | collective-permute-start | bytes 98312 | tf_op jit(solution)/shard_map/ppermute | solution.py:462
  29.3 6.6 %collective-permute-start.12 = (bf16[128,256]{1,0:T(8,128)(2,1)S(1)}, bf16[128,256]{1,0:T(8,128)(2,1)S(1)}, u32[]{:S(2)}, u32[]{:S(2)}) collective-permute-start(bf16[128,256]{1,0:T(8,128)(2,1)S(1)} %get-tuple-element.31), channel_id=1, source_target_pairs={{0,8},{2,10},{4,12},{6,14},{8,0},{10,2},{12,4},{14,6},{1,9},{3,11}... | collective-permute-start | bytes 196616 | tf_op jit(solution)/shard_map/ppermute | solution.py:462
  31.5 4.3 %collective-permute-start.14 = (bf16[64,256]{1,0:T(8,128)(2,1)S(1)}, bf16[64,256]{1,0:T(8,128)(2,1)S(1)}, u32[]{:S(2)}, u32[]{:S(2)}) collective-permute-start(bf16[64,256]{1,0:T(8,128)(2,1)S(1)} %collective-permute-done.13.map_seen), channel_id=1, source_target_pairs={{0,1},{1,0},{2,3},{3,2},{4,5},{5,4},{6,7},{7,6},{8,9},{9,8},{10,11... | collective-permute-start | bytes 98312 | tf_op jit(solution)/shard_map/ppermute | solution.py:459
  36.3 1.3 %collective-permute-start.15 = (bf16[128,256]{1,0:T(8,128)(2,1)S(1)}, bf16[128,256]{1,0:T(8,128)(2,1)S(1)}, u32[]{:S(2)}, u32[]{:S(2)}) collective-permute-start(bf16[128,256]{1,0:T(8,128)(2,1)S(1)} %shard_map.54.own), channel_id=1, source_target_pairs={{0,1},{1,0},{2,3},{3,2},{4,5},{5,4},{6,7},{7,6},{8,9},{9,8},{10,11... | collective-permute-start | bytes 196616 | tf_op jit(solution)/shard_map/ppermute | solution.py:459

commit v4 on v3

--- a/solution.py
+++ b/solution.py
@@ -142,9 +142,10 @@
 
 
 def apply_pair(x, forms, index, name):
+    at = (name,) if index is None else (index, name)
     high, low = split(x)
-    both = contract(jnp.concatenate([high, low], axis=0), forms[index, name], False)
-    rest = contract(high, forms[index, name + 1], False)
+    both = contract(jnp.concatenate([high, low], axis=0), forms[at], False)
+    rest = contract(high, forms[at[:-1] + (name + 1,)], False)
     return both[: x.shape[0]] + both[x.shape[0] :] + rest
 
 
@@ -343,12 +344,11 @@
     base[...] = apply(b, sigma[...])
 
 
-def close_kernel(hand, base, pi, leaving, first, seen, map_seen, map_other, out, rows):
+def merge_kernel(hand, base, pi, leaving, first, map_seen, map_other, ends, ahead_map, rows):
     row = lax.axis_index("row")
     half = first.shape[0]
     part = map_seen.shape[0]
     left = lax.axis_index("slab") < lax.axis_size("slab") // 2
-    there = seen[:half].astype(F32)
 
     @pl.when(row == 0)
     def _():
@@ -361,25 +361,42 @@
         rows[part:] = map_seen[...]
 
     map_form = stacked(rows[...])
-
-    def times(x, index):
-        high, low = split(x)
-        both = contract(jnp.concatenate([high, low], axis=0), hand[index], False)
-        return both[:half] + both[half:] + contract(high, hand[index + 1], False)
+    ends[0] = pi[...]
 
     @pl.when(left)
     def _():
+        size = rows.shape[0]
+        w = hand[0, :size].astype(F32) + hand[1, :size].astype(F32)
+        both = jnp.concatenate([leaving[:half], w], axis=0)
+        both = apply_pair(apply(map_form, both, False), hand, None, 2)
+        ends[1] = base[...] + both[:half]
+        ahead_map[0], ahead_map[1] = split(stacked(both[half:]))
+
+    @pl.when(jnp.logical_not(left))
+    def _():
+        w = apply_short(map_form, first[...], False)
+        ends[0] = pi[...] + apply_pair(w, hand, None, 0)
+        ends[1] = base[...] + apply_pair(w, hand, None, 2)
+
+
+def close_kernel(hand, ends, ahead_map, seen, out):
+    half = ends.shape[1]
+    left = lax.axis_index("slab") < lax.axis_size("slab") // 2
+    there = seen[:half]
+    upper = ends[1] + contract(there, hand[2], False) + contract(there, hand[3], False)
+
+    @pl.when(left)
+    def _():
         ahead = seen[half:]
-        past = leaving[:half] + contract(ahead, hand[0], False) + contract(ahead, hand[1], False)
-        entry = there + apply(map_form, past, False)
-        out[:half] = pi[...].astype(BF16)
-        out[half:] = (base[...] + times(entry, 2)).astype(BF16)
+        more = contract(ahead, ahead_map[0], False) + contract(ahead, ahead_map[1], False)
+        out[:half] = ends[0].astype(BF16)
+        out[half:] = (upper + more).astype(BF16)
 
     @pl.when(jnp.logical_not(left))
     def _():
-        before = there + apply_short(map_form, first[...], False)
-        out[:half] = (pi[...] + times(before, 0)).astype(BF16)
-        out[half:] = (base[...] + times(before, 2)).astype(BF16)
+        more = contract(there, hand[0], False) + contract(there, hand[1], False)
+        out[:half] = (ends[0] + more).astype(BF16)
+        out[half:] = upper.astype(BF16)
 
 
 def final_kernel(count, green, direct, own, other, result, whole):
@@ -482,7 +499,7 @@
         pack,
     )
     count = jnp.broadcast_to(interior_count.reshape(1, 1), (8, columns))
-    source_other = across(source_near)
+    source_other = across(source)
     edge_other = across(edge)
     packs = {}
     for k in ORDER:
@@ -616,19 +633,21 @@
         gamma,
         shift,
     )
-    (closed,) = call(
-        close_kernel,
-        [V] * 8,
-        [((columns, 2 * surface), BF16)],
-        [((surface, 2 * surface), BF16)],
+    ends, ahead_map = call(
+        merge_kernel,
+        [V] * 7,
+        [((2,) + thin, F32), ((2, 2 * surface, 2 * surface), BF16)],
+        [(square, BF16)],
         hand,
         base,
         pi,
         leaving,
         first,
-        seen,
         map_seen,
         map_other,
+    )
+    (closed,) = call(
+        close_kernel, [V] * 4, [((columns, 2 * surface), BF16)], [], hand, ends, ahead_map, seen
     )
     (result,) = call(
         final_kernel,

time: 38.9 us -> 38.7 us (level)
  waiting for transfers between devices: 17.3 us -> 16.8 us
    ppermute x8, waiting for transfers between devices: 16.6 us -> 16 us  [partner(): return lax.ppermute(x, 'slab', [(i, i ^ bit) for i in range(slabs)])]
    pallas_call x10 -> x11, Pallas kernels: 9.32 us -> 9.66 us  [call(): pl.pallas_call(kernel, in_specs=specs, out_specs=[V] * len(outs), out_sha...]
  transfers between devices with their start and end apart: 16 -> 16, of which waited for: 9 -> 9; matrix products, arithmetic and copies ran while one was open for 0% -> 0% of each run, Pallas kernels for 8% -> 10%
where the time goes in v4:
time: 38.7 us; the launch traced here: 38.5 us
  waiting for transfers between devices  16.8 us (43%)
  starting transfers between devices  11.3 us (29%)
  Pallas kernels  9.66 us (25%)
  between operations  0.78 us (2%)
    ppermute x8, waiting for transfers between devices, partner(): return lax.ppermute(x, 'slab', [(i, i ^ bit) for i in range(slabs)])  16 us
    ppermute x8, starting transfers between devices, partner(): return lax.ppermute(x, 'slab', [(i, i ^ bit) for i in range(slabs)])  10.7 us
    pallas_call x11, Pallas kernels, call(): pl.pallas_call(kernel, in_specs=specs, out_specs=[V] * len(outs), out_sha...  9.66 us
  transfers between devices with their start and end apart: 16, of which 9 were waited for; matrix products, arithmetic and copies ran while one was open for 0% of the time, Pallas kernels for 10%

profile of v4, /device:TPU:0, one launch (start us, length us, event | category | flops | bytes accessed | tf_op | source)
XLA Modules:
  0.0 38.5 jit_solution(9786709989395064707)
XLA Ops:
  0.0 0.9 %shard_map.46.pack = bf16[5,128,128]{2,1,0:T(8,128)(2,1)S(1)} custom-call(bf16[2,384,768]{2,1,0:T(8,128)(2,1)} %green.7, bf16[2,128,128]{2,1,0:T(8,128)(2,1)} %coupling.3), custom_call_target="tpu_custom_call" | custom-call | tf_op jit(solution)/shard_map/pallas_call | solution.py:444
  0.9 1.1 %shard_map.47 = (bf16[2,128,768]{2,1,0:T(8,128)(2,1)S(1)}, bf16[2,384,128]{2,1,0:T(8,128)(2,1)S(1)}, bf16[2,128,128]{2,1,0:T(8,128)(2,1)S(1)}) custom-call(bf16[2,384,768]{2,1,0:T(8,128)(2,1)} %green.7, bf16[2,128,128]{2,1,0:T(8,128)(2,1)} %coupling.3, bf16[2,384,128]{2,1,0:T(8,128)(2,1)} %source.1, bf16[5,128,128]{2,1,0:T(8,128)(2,1)S(1)} %shard_map.46.pack), custom_call_target="tpu_custom_call" | custom-call | tf_op jit(solution)/shard_map/pallas_call | solution.py:444
  2.0 0.6 %collective-permute-start.1 = (bf16[2,128,768]{2,1,0:T(8,128)(2,1)S(1)}, bf16[2,128,768]{2,1,0:T(8,128)(2,1)S(1)}, u32[]{:S(2)}, u32[]{:S(2)}) collective-permute-start(bf16[2,128,768]{2,1,0:T(8,128)(2,1)S(1)} %get-tuple-element.22.edge.refs_0_), channel_id=1, source_target_pairs={{0,1},{1,0},{2,3},{3,2},{4,5},{5,4},{6,7},{7,6},{8,9},{9,8},{10,11... | collective-permute-start | bytes 1179656 | tf_op jit(solution)/shard_map/ppermute | solution.py:476
  2.6 2.6 %collective-permute-start.4 = (bf16[5,128,128]{2,1,0:T(8,128)(2,1)S(1)}, bf16[5,128,128]{2,1,0:T(8,128)(2,1)S(1)}, u32[]{:S(2)}, u32[]{:S(2)}) collective-permute-start(bf16[5,128,128]{2,1,0:T(8,128)(2,1)S(1)} %shard_map.46.pack), channel_id=1, source_target_pairs={{0,4},{2,6},{4,0},{6,2},{8,12},{10,14},{12,8},{14,10},{1,5},{3,7},... | collective-permute-start | bytes 491528 | tf_op jit(solution)/shard_map/ppermute | solution.py:479
  5.2 1.4 %collective-permute-start.2 = (bf16[5,128,128]{2,1,0:T(8,128)(2,1)S(1)}, bf16[5,128,128]{2,1,0:T(8,128)(2,1)S(1)}, u32[]{:S(2)}, u32[]{:S(2)}) collective-permute-start(bf16[5,128,128]{2,1,0:T(8,128)(2,1)S(1)} %shard_map.46.pack), channel_id=1, source_target_pairs={{0,6},{2,4},{4,2},{6,0},{8,14},{10,12},{12,10},{14,8},{1,7},{3,5},... | collective-permute-start | bytes 491528 | tf_op jit(solution)/shard_map/ppermute | solution.py:479
  6.8 3.5 %collective-permute-done.4.refs_5_ = bf16[5,128,128]{2,1,0:T(8,128)(2,1)S(1)} collective-permute-done((bf16[5,128,128]{2,1,0:T(8,128)(2,1)S(1)}, bf16[5,128,128]{2,1,0:T(8,128)(2,1)S(1)}, u32[]{:S(2)}, u32[]{:S(2)}) %collective-permute-start.4) | collective-permute-done | bytes 163872 | tf_op jit(solution)/shard_map/ppermute | solution.py:479
  10.3 4.5 %collective-permute-done.2.refs_3_ = bf16[5,128,128]{2,1,0:T(8,128)(2,1)S(1)} collective-permute-done((bf16[5,128,128]{2,1,0:T(8,128)(2,1)S(1)}, bf16[5,128,128]{2,1,0:T(8,128)(2,1)S(1)}, u32[]{:S(2)}, u32[]{:S(2)}) %collective-permute-start.2) | collective-permute-done | bytes 163872 | tf_op jit(solution)/shard_map/ppermute | solution.py:479
  14.7 1.4 %collective-permute-done.6.refs_0_ = bf16[5,128,128]{2,1,0:T(8,128)(2,1)S(1)} collective-permute-done((bf16[5,128,128]{2,1,0:T(8,128)(2,1)S(1)}, bf16[5,128,128]{2,1,0:T(8,128)(2,1)S(1)}, u32[]{:S(2)}, u32[]{:S(2)}) %collective-permute-start.6) | collective-permute-done | bytes 163872 | tf_op jit(solution)/shard_map/ppermute | solution.py:479
  16.8 0.5 %shard_map.48.surfaces.refs_2_ = bf16[128,256]{1,0:T(8,128)(2,1)S(1)} custom-call(s32[8,128]{1,0:T(8,128)S(1)} %broadcast_in_dim.8.count, bf16[2,128,768]{2,1,0:T(8,128)(2,1)S(1)} %get-tuple-element.22.edge.refs_0_, bf16[2,128,768]{2,1,0:T(8,128)(2,1)S(1)} %collective-permute-done.1.edge_other.refs_1_, ...), custom_call_target="tpu_custom_call" | custom-call | tf_op jit(solution)/shard_map/pallas_call | solution.py:444
  17.3 1.6 %collective-permute-start.10 = (bf16[128,256]{1,0:T(8,128)(2,1)S(1)}, bf16[128,256]{1,0:T(8,128)(2,1)S(1)}, u32[]{:S(2)}, u32[]{:S(2)}) collective-permute-start(bf16[128,256]{1,0:T(8,128)(2,1)S(1)} %shard_map.48.surfaces.refs_2_), channel_id=1, source_target_pairs={{0,6},{2,4},{4,2},{6,0},{8,14},{10,12},{12,10},{14,8},{1,7},{3,5},... | collective-permute-start | bytes 196616 | tf_op jit(solution)/shard_map/ppermute | solution.py:479
  19.2 1.6 %collective-permute-start.8 = (bf16[128,256]{1,0:T(8,128)(2,1)S(1)}, bf16[128,256]{1,0:T(8,128)(2,1)S(1)}, u32[]{:S(2)}, u32[]{:S(2)}) collective-permute-start(bf16[128,256]{1,0:T(8,128)(2,1)S(1)} %shard_map.48.surfaces.refs_2_), channel_id=1, source_target_pairs={{0,2},{2,0},{4,6},{6,4},{8,10},{10,8},{12,14},{14,12},{1,3},{3,1},... | collective-permute-start | bytes 196616 | tf_op jit(solution)/shard_map/ppermute | solution.py:479
  20.9 0.7 %shard_map.50._ = bf16[4,8,256,256]{3,2,1,0:T(8,128)(2,1)S(1)} custom-call(bf16[2,128,768]{2,1,0:T(8,128)(2,1)S(1)} %get-tuple-element.22.edge.refs_0_, bf16[2,128,768]{2,1,0:T(8,128)(2,1)S(1)} %collective-permute-done.1.edge_other.refs_1_, bf16[2,128,128]{2,1,0:T(8,128)(2,1)S(1)} %get-tuple-element.23.refs_2_.coupling, ...), custom_call_target="tpu_custom_call" | custom-call | tf_op jit(solution)/shard_map/pallas_call | solution.py:444
  21.6 1.3 %collective-permute-done.10.refs_5_ = bf16[128,256]{1,0:T(8,128)(2,1)S(1)} collective-permute-done((bf16[128,256]{1,0:T(8,128)(2,1)S(1)}, bf16[128,256]{1,0:T(8,128)(2,1)S(1)}, u32[]{:S(2)}, u32[]{:S(2)}) %collective-permute-start.10) | collective-permute-done | bytes 65568 | tf_op jit(solution)/shard_map/ppermute | solution.py:479
  23.1 1.0 %collective-permute-done.8.refs_3_ = bf16[128,256]{1,0:T(8,128)(2,1)S(1)} collective-permute-done((bf16[128,256]{1,0:T(8,128)(2,1)S(1)}, bf16[128,256]{1,0:T(8,128)(2,1)S(1)}, u32[]{:S(2)}, u32[]{:S(2)}) %collective-permute-start.8) | collective-permute-done | bytes 65568 | tf_op jit(solution)/shard_map/ppermute | solution.py:479
  24.2 2.5 %shard_map.51 = (bf16[4,8,256,256]{3,2,1,0:T(8,128)(2,1)S(1)}, bf16[128,256]{1,0:T(8,128)(2,1)S(1)}, bf16[64,256]{1,0:T(8,128)(2,1)S(1)}, f32[128,256]{1,0:T(8,1...) custom-call(bf16[4,8,256,256]{3,2,1,0:T(8,128)(2,1)S(1)} %shard_map., ...), custom_call_target="tpu_custom_call", output_to_operand_aliasing={{0}: (0, {})} | custom-call | tf_op jit(solution)/shard_map/pallas_call | solution.py:444
  26.7 2.6 %collective-permute-start.12 = (bf16[64,256]{1,0:T(8,128)(2,1)S(1)}, bf16[64,256]{1,0:T(8,128)(2,1)S(1)}, u32[]{:S(2)}, u32[]{:S(2)}) collective-permute-start(bf16[64,256]{1,0:T(8,128)(2,1)S(1)} %get-tuple-element.34), channel_id=1, source_target_pairs={{0,8},{2,10},{4,12},{6,14},{8,0},{10,2},{12,4},{14,6},{1,9},{3,11}... | collective-permute-start | bytes 98312 | tf_op jit(solution)/shard_map/ppermute | solution.py:479
  29.3 0.4 collective-permute-start.14
  29.6 1.9 %collective-permute-done.12.map_seen = bf16[64,256]{1,0:T(8,128)(2,1)S(1)} collective-permute-done((bf16[64,256]{1,0:T(8,128)(2,1)S(1)}, bf16[64,256]{1,0:T(8,128)(2,1)S(1)}, u32[]{:S(2)}, u32[]{:S(2)}) %collective-permute-start.12) | collective-permute-done | bytes 32800 | tf_op jit(solution)/shard_map/ppermute | solution.py:479
  31.5 1.3 %shard_map.52 = (f32[128,256]{1,0:T(8,128)S(1)}, f32[128,256]{1,0:T(8,128)}) custom-call(bf16[4,8,256,256]{3,2,1,0:T(8,128)(2,1)S(1)} %get-tuple-element.26.forms), custom_call_target="tpu_custom_call" | custom-call | tf_op jit(solution)/shard_map/pallas_call | solution.py:444
  33.1 0.5 %shard_map.54 = (f32[2,64,256]{2,1,0:T(8,128)S(1)}, bf16[2,256,256]{2,1,0:T(8,128)(2,1)S(1)}) custom-call(bf16[4,256,256]{2,1,0:T(8,128)(2,1)S(1)} %get-tuple-element.29.hand, f32[64,256]{1,0:T(8,128)S(1)} %get-tuple-element.30.base, f32[64,256]{1,0:T(8,128)S(1)} %get-tuple-element.31.pi, f32[128,256]{1,0:T(8,128)S(1)} %get-tuple-element.32.leaving, ...), custom_call_target="tpu_custom_call" | custom-call | tf_op jit(solution)/shard_map/pallas_call | solution.py:444
  33.6 2.2 %collective-permute-done.14.seen = bf16[128,256]{1,0:T(8,128)(2,1)S(1)} collective-permute-done((bf16[128,256]{1,0:T(8,128)(2,1)S(1)}, bf16[128,256]{1,0:T(8,128)(2,1)S(1)}, u32[]{:S(2)}, u32[]{:S(2)}) %collective-permute-start.14) | collective-permute-done | bytes 65568 | tf_op jit(solution)/shard_map/ppermute | solution.py:479
  36.3 0.5 %shard_map.49.direct = f32[384,256]{1,0:T(8,128)S(1)} custom-call(s32[8,128]{1,0:T(8,128)S(1)} %broadcast_in_dim.8.count, bf16[2,384,768]{2,1,0:T(8,128)(2,1)S(1)} %copy-done, bf16[2,384,128]{2,1,0:T(8,128)(2,1)S(1)} %get-tuple-element.21.source_own, bf16[2,384,128]{2,1,0:T(8,128)(2,1)S(1)} %collective-permute-done.source_other, ...), custom_call_target="tpu_custom_call" | custom-call | tf_op jit(solution)/shard_map/pallas_call | solution.py:444
  36.8 0.7 %collective-permute-done.15.other = bf16[128,256]{1,0:T(8,128)(2,1)S(1)} collective-permute-done((bf16[128,256]{1,0:T(8,128)(2,1)S(1)}, bf16[128,256]{1,0:T(8,128)(2,1)S(1)}, u32[]{:S(2)}, u32[]{:S(2)}) %collective-permute-start.15) | collective-permute-done | bytes 65568 | tf_op jit(solution)/shard_map/ppermute | solution.py:476
  37.5 1.1 %shard_map.56 = f32[2,384,128]{2,1,0:T(8,128)} custom-call(s32[8,128]{1,0:T(8,128)S(1)} %broadcast_in_dim.8.count, bf16[2,384,768]{2,1,0:T(8,128)(2,1)S(1)} %copy-done, f32[384,256]{1,0:T(8,128)S(1)} %shard_map.49.direct, bf16[128,256]{1,0:T(8,128)(2,1)S(1)} %shard_map.55.own, bf16[128,256]{1,0:T(8,128)(2,1)S(1)} %collective-permute-done.15.other), custom_call_target="tpu_custom_call" | custom-call | tf_op jit(solution)/shard_map/pallas_call | solution.py:444
  (23 shorter events, 1.5 us)
Async XLA Ops:
  2.0 14.8 %collective-permute-start.1 = (bf16[2,128,768]{2,1,0:T(8,128)(2,1)S(1)}, bf16[2,128,768]{2,1,0:T(8,128)(2,1)S(1)}, u32[]{:S(2)}, u32[]{:S(2)}) collective-permute-start(bf16[2,128,768]{2,1,0:T(8,128)(2,1)S(1)} %get-tuple-element.22.edge.refs_0_), channel_id=1, source_target_pairs={{0,1},{1,0},{2,3},{3,2},{4,5},{5,4},{6,7},{7,6},{8,9},{9,8},{10,11... | collective-permute-start | bytes 1179656 | tf_op jit(solution)/shard_map/ppermute | solution.py:476
  2.6 7.7 %collective-permute-start.4 = (bf16[5,128,128]{2,1,0:T(8,128)(2,1)S(1)}, bf16[5,128,128]{2,1,0:T(8,128)(2,1)S(1)}, u32[]{:S(2)}, u32[]{:S(2)}) collective-permute-start(bf16[5,128,128]{2,1,0:T(8,128)(2,1)S(1)} %shard_map.46.pack), channel_id=1, source_target_pairs={{0,4},{2,6},{4,0},{6,2},{8,12},{10,14},{12,8},{14,10},{1,5},{3,7},... | collective-permute-start | bytes 491528 | tf_op jit(solution)/shard_map/ppermute | solution.py:479
  5.2 9.5 %collective-permute-start.2 = (bf16[5,128,128]{2,1,0:T(8,128)(2,1)S(1)}, bf16[5,128,128]{2,1,0:T(8,128)(2,1)S(1)}, u32[]{:S(2)}, u32[]{:S(2)}) collective-permute-start(bf16[5,128,128]{2,1,0:T(8,128)(2,1)S(1)} %shard_map.46.pack), channel_id=1, source_target_pairs={{0,6},{2,4},{4,2},{6,0},{8,14},{10,12},{12,10},{14,8},{1,7},{3,5},... | collective-permute-start | bytes 491528 | tf_op jit(solution)/shard_map/ppermute | solution.py:479
  6.6 9.5 %collective-permute-start.6 = (bf16[5,128,128]{2,1,0:T(8,128)(2,1)S(1)}, bf16[5,128,128]{2,1,0:T(8,128)(2,1)S(1)}, u32[]{:S(2)}, u32[]{:S(2)}) collective-permute-start(bf16[5,128,128]{2,1,0:T(8,128)(2,1)S(1)} %shard_map.46.pack), channel_id=1, source_target_pairs={{0,2},{2,0},{4,6},{6,4},{8,10},{10,8},{12,14},{14,12},{1,3},{3,1},... | collective-permute-start | bytes 491528 | tf_op jit(solution)/shard_map/ppermute | solution.py:479
  6.7 10.0 %collective-permute-start = (bf16[2,384,128]{2,1,0:T(8,128)(2,1)}, bf16[2,384,128]{2,1,0:T(8,128)(2,1)S(1)}, u32[]{:S(2)}, u32[]{:S(2)}) collective-permute-start(bf16[2,384,128]{2,1,0:T(8,128)(2,1)} %source.1), channel_id=1, source_target_pairs={{0,1},{1,0},{2,3},{3,2},{4,5},{5,4},{6,7},{7,6},{8,9},{9,8},{10,11... | collective-permute-start | bytes 589832 | tf_op jit(solution)/shard_map/ppermute | solution.py:476
  10.3 9.0 %collective-permute-start.5 = (bf16[5,128,128]{2,1,0:T(8,128)(2,1)S(1)}, bf16[5,128,128]{2,1,0:T(8,128)(2,1)S(1)}, u32[]{:S(2)}, u32[]{:S(2)}) collective-permute-start(bf16[5,128,128]{2,1,0:T(8,128)(2,1)S(1)} %collective-permute-done.4.refs_5_), channel_id=1, source_target_pairs={{0,1},{1,0},{2,3},{3,2},{4,5},{5,4},{6,7},{7,6},{8,9},{9,8},{10,11... | collective-permute-start | bytes 491528 | tf_op jit(solution)/shard_map/ppermute | solution.py:476
  14.7 6.1 %collective-permute-start.3 = (bf16[5,128,128]{2,1,0:T(8,128)(2,1)S(1)}, bf16[5,128,128]{2,1,0:T(8,128)(2,1)S(1)}, u32[]{:S(2)}, u32[]{:S(2)}) collective-permute-start(bf16[5,128,128]{2,1,0:T(8,128)(2,1)S(1)} %collective-permute-done.2.refs_3_), channel_id=1, source_target_pairs={{0,1},{1,0},{2,3},{3,2},{4,5},{5,4},{6,7},{7,6},{8,9},{9,8},{10,11... | collective-permute-start | bytes 491528 | tf_op jit(solution)/shard_map/ppermute | solution.py:476
  16.1 5.5 %collective-permute-start.7 = (bf16[5,128,128]{2,1,0:T(8,128)(2,1)S(1)}, bf16[5,128,128]{2,1,0:T(8,128)(2,1)S(1)}, u32[]{:S(2)}, u32[]{:S(2)}) collective-permute-start(bf16[5,128,128]{2,1,0:T(8,128)(2,1)S(1)} %collective-permute-done.6.refs_0_), channel_id=1, source_target_pairs={{0,1},{1,0},{2,3},{3,2},{4,5},{5,4},{6,7},{7,6},{8,9},{9,8},{10,11... | collective-permute-start | bytes 491528 | tf_op jit(solution)/shard_map/ppermute | solution.py:476
  17.3 5.6 %collective-permute-start.10 = (bf16[128,256]{1,0:T(8,128)(2,1)S(1)}, bf16[128,256]{1,0:T(8,128)(2,1)S(1)}, u32[]{:S(2)}, u32[]{:S(2)}) collective-permute-start(bf16[128,256]{1,0:T(8,128)(2,1)S(1)} %shard_map.48.surfaces.refs_2_), channel_id=1, source_target_pairs={{0,6},{2,4},{4,2},{6,0},{8,14},{10,12},{12,10},{14,8},{1,7},{3,5},... | collective-permute-start | bytes 196616 | tf_op jit(solution)/shard_map/ppermute | solution.py:479
  18.9 4.3 %collective-permute-start.9 = (bf16[128,256]{1,0:T(8,128)(2,1)S(1)}, bf16[128,256]{1,0:T(8,128)(2,1)S(1)}, u32[]{:S(2)}, u32[]{:S(2)}) collective-permute-start(bf16[128,256]{1,0:T(8,128)(2,1)S(1)} %shard_map.48.surfaces.refs_2_), channel_id=1, source_target_pairs={{0,4},{2,6},{4,0},{6,2},{8,12},{10,14},{12,8},{14,10},{1,5},{3,7},... | collective-permute-start | bytes 196616 | tf_op jit(solution)/shard_map/ppermute | solution.py:479
  19.2 4.9 %collective-permute-start.8 = (bf16[128,256]{1,0:T(8,128)(2,1)S(1)}, bf16[128,256]{1,0:T(8,128)(2,1)S(1)}, u32[]{:S(2)}, u32[]{:S(2)}) collective-permute-start(bf16[128,256]{1,0:T(8,128)(2,1)S(1)} %shard_map.48.surfaces.refs_2_), channel_id=1, source_target_pairs={{0,2},{2,0},{4,6},{6,4},{8,10},{10,8},{12,14},{14,12},{1,3},{3,1},... | collective-permute-start | bytes 196616 | tf_op jit(solution)/shard_map/ppermute | solution.py:479
  26.7 9.6 %copy-start = (bf16[2,384,768]{2,1,0:T(8,128)(2,1)S(1)}, bf16[2,384,768]{2,1,0:T(8,128)(2,1)}, u32[]{:S(2)}) copy-start(bf16[2,384,768]{2,1,0:T(8,128)(2,1)} %green.7) | copy-start | bytes 3538948
  26.7 6.1 %collective-permute-start.11 = (f32[128,256]{1,0:T(8,128)S(1)}, f32[128,256]{1,0:T(8,128)S(1)}, u32[]{:S(2)}, u32[]{:S(2)}) collective-permute-start(f32[128,256]{1,0:T(8,128)S(1)} %get-tuple-element.25.response), channel_id=1, source_target_pairs={{0,1},{1,0},{2,3},{3,2},{4,5},{5,4},{6,7},{7,6},{8,9},{9,8},{10,11... | collective-permute-start | bytes 393224 | tf_op jit(solution)/shard_map/ppermute | solution.py:476
  26.7 4.8 %collective-permute-start.12 = (bf16[64,256]{1,0:T(8,128)(2,1)S(1)}, bf16[64,256]{1,0:T(8,128)(2,1)S(1)}, u32[]{:S(2)}, u32[]{:S(2)}) collective-permute-start(bf16[64,256]{1,0:T(8,128)(2,1)S(1)} %get-tuple-element.34), channel_id=1, source_target_pairs={{0,8},{2,10},{4,12},{6,14},{8,0},{10,2},{12,4},{14,6},{1,9},{3,11}... | collective-permute-start | bytes 98312 | tf_op jit(solution)/shard_map/ppermute | solution.py:479
  29.3 6.6 %collective-permute-start.14 = (bf16[128,256]{1,0:T(8,128)(2,1)S(1)}, bf16[128,256]{1,0:T(8,128)(2,1)S(1)}, u32[]{:S(2)}, u32[]{:S(2)}) collective-permute-start(bf16[128,256]{1,0:T(8,128)(2,1)S(1)} %get-tuple-element.33), channel_id=1, source_target_pairs={{0,8},{2,10},{4,12},{6,14},{8,0},{10,2},{12,4},{14,6},{1,9},{3,11}... | collective-permute-start | bytes 196616 | tf_op jit(solution)/shard_map/ppermute | solution.py:479
  31.5 1.6 %collective-permute-start.13 = (bf16[64,256]{1,0:T(8,128)(2,1)S(1)}, bf16[64,256]{1,0:T(8,128)(2,1)S(1)}, u32[]{:S(2)}, u32[]{:S(2)}) collective-permute-start(bf16[64,256]{1,0:T(8,128)(2,1)S(1)} %collective-permute-done.12.map_seen), channel_id=1, source_target_pairs={{0,1},{1,0},{2,3},{3,2},{4,5},{5,4},{6,7},{7,6},{8,9},{9,8},{10,11... | collective-permute-start | bytes 98312 | tf_op jit(solution)/shard_map/ppermute | solution.py:476
  36.2 1.3 %collective-permute-start.15 = (bf16[128,256]{1,0:T(8,128)(2,1)S(1)}, bf16[128,256]{1,0:T(8,128)(2,1)S(1)}, u32[]{:S(2)}, u32[]{:S(2)}) collective-permute-start(bf16[128,256]{1,0:T(8,128)(2,1)S(1)} %shard_map.55.own), channel_id=1, source_target_pairs={{0,1},{1,0},{2,3},{3,2},{4,5},{5,4},{6,7},{7,6},{8,9},{9,8},{10,11... | collective-permute-start | bytes 196616 | tf_op jit(solution)/shard_map/ppermute | solution.py:476

commit v5 on v4

--- a/solution.py
+++ b/solution.py
@@ -224,12 +224,27 @@
     form_slab(forms, k, (f[0], f[1]), (f[2], f[3]), (l[2], l[3]), (l[0], l[1]), (f[4], l[4]))
 
 
-def solve_kernel(
-    later, _, *refs
-):
-    packed, given = refs[: 2 * len(later)], refs[2 * len(later) : 2 * len(later) + GROUP]
-    forms, send, send_map, leaving, entering, pi, sigma, response, shift, vectors, states, backs = refs[
-        2 * len(later) + GROUP :
+def more_kernel(later, _, *refs):
+    packed, forms = refs[:-1], refs[-1]
+    row = lax.axis_index("row")
+
+    def fill(first_is_own):
+        for n, k in enumerate(later):
+            form_packed(forms, k, packed[2 * n], packed[2 * n + 1], first_is_own)
+
+    @pl.when(row == 0)
+    def _():
+        fill(True)
+
+    @pl.when(row == 1)
+    def _():
+        fill(False)
+
+
+def solve_kernel(forms, *refs):
+    given = refs[:GROUP]
+    send, send_map, leaving, entering, pi, sigma, response, shift, vectors, states, backs = refs[
+        GROUP:
     ]
     row = lax.axis_index("row")
     slab = lax.axis_index("slab")
@@ -237,18 +252,6 @@
     member = slab % GROUP
     size = shift.shape[0]
     half = vectors.shape[1] // 2
-
-    def fill(first_is_own):
-        for n, k in enumerate(later):
-            form_packed(forms, k, packed[2 * n], packed[2 * n + 1], first_is_own)
-
-    @pl.when(row == 0)
-    def _():
-        fill(True)
-
-    @pl.when(row == 1)
-    def _():
-        fill(False)
 
     for k, v in enumerate(given):
         vectors[member ^ k] = v[...]
@@ -544,10 +547,19 @@
         couple_near,
         *(x for k in sooner for x in (packs[k], swapped[k])),
     )
-    forms, send, send_map, leaving, entering, pi, sigma, response, shift = call(
-        functools.partial(solve_kernel, later),
-        [V] * (1 + 2 * len(later) + GROUP),
-        [forms_shape, ((columns, 2 * surface), BF16), (thin, BF16)]
+    (forms,) = call(
+        functools.partial(more_kernel, later),
+        [V] * (1 + 2 * len(later)),
+        [forms_shape],
+        [],
+        forms,
+        *(x for k in later for x in (packs[k], swapped[k])),
+        aliases={0: 0},
+    )
+    send, send_map, leaving, entering, pi, sigma, response, shift = call(
+        solve_kernel,
+        [V] * (1 + GROUP),
+        [((columns, 2 * surface), BF16), (thin, BF16)]
         + [(joint, F32)] * 2
         + [(thin, F32)] * 2
         + [(joint, F32), (square, F32)],
@@ -557,10 +569,8 @@
             ((GROUP + 1,) + joint, F32),
         ],
         forms,
-        *(x for k in later for x in (packs[k], swapped[k])),
         vectors,
         *gathered,
-        aliases={0: 0},
     )
     gamma, back_whole = call(
         gamma_kernel, [V], [(square, F32), (square, F32)], [((GROUP + 1,) + square, F32)], forms

time: 38.7 us -> 38.2 us (0.987)
  waiting for transfers between devices: 16.8 us -> 15.7 us
  starting transfers between devices: 11.3 us -> 11.9 us
    ppermute x8, waiting for transfers between devices: 16 us -> 14.9 us  [partner(): return lax.ppermute(x, 'slab', [(i, i ^ bit) for i in range(slabs)])]
    ppermute x8, starting transfers between devices: 0.66 us -> 1.15 us  [across(): return lax.ppermute(x, 'row', [(0, 1), (1, 0)])]
    pallas_call x11 -> x12, Pallas kernels: 9.66 us -> 9.69 us  [call(): pl.pallas_call(kernel, in_specs=specs, out_specs=[V] * len(outs), out_sha...]
  transfers between devices with their start and end apart: 16 -> 16, of which waited for: 9 -> 7; matrix products, arithmetic and copies ran while one was open for 0% -> 0% of each run, Pallas kernels for 10% -> 11%
where the time goes in v5:
time: 38.2 us; the launch traced here: 38 us
  waiting for transfers between devices  15.7 us (41%)
  starting transfers between devices  11.9 us (31%)
  Pallas kernels  9.69 us (25%)
  between operations  0.8 us (2%)
    ppermute x8, waiting for transfers between devices, partner(): return lax.ppermute(x, 'slab', [(i, i ^ bit) for i in range(slabs)])  14.9 us
    ppermute x8, starting transfers between devices, partner(): return lax.ppermute(x, 'slab', [(i, i ^ bit) for i in range(slabs)])  10.7 us
    pallas_call x12, Pallas kernels, call(): pl.pallas_call(kernel, in_specs=specs, out_specs=[V] * len(outs), out_sha...  9.69 us
    ppermute x8, starting transfers between devices, across(): return lax.ppermute(x, 'row', [(0, 1), (1, 0)])  1.15 us
  transfers between devices with their start and end apart: 16, of which 7 were waited for; matrix products, arithmetic and copies ran while one was open for 0% of the time, Pallas kernels for 11%

profile of v5, /device:TPU:0, one launch (start us, length us, event | category | flops | bytes accessed | tf_op | source)
XLA Modules:
  0.0 38.0 jit_solution(10487650157119198424)
XLA Ops:
  0.0 0.9 %shard_map.46.pack = bf16[5,128,128]{2,1,0:T(8,128)(2,1)S(1)} custom-call(bf16[2,384,768]{2,1,0:T(8,128)(2,1)} %green.7, bf16[2,128,128]{2,1,0:T(8,128)(2,1)} %coupling.3), custom_call_target="tpu_custom_call" | custom-call | tf_op jit(solution)/shard_map/pallas_call | solution.py:447
  0.9 1.1 %shard_map.47 = (bf16[2,128,768]{2,1,0:T(8,128)(2,1)S(1)}, bf16[2,384,128]{2,1,0:T(8,128)(2,1)S(1)}, bf16[2,128,128]{2,1,0:T(8,128)(2,1)S(1)}) custom-call(bf16[2,384,768]{2,1,0:T(8,128)(2,1)} %green.7, bf16[2,128,128]{2,1,0:T(8,128)(2,1)} %coupling.3, bf16[2,384,128]{2,1,0:T(8,128)(2,1)} %source.1, bf16[5,128,128]{2,1,0:T(8,128)(2,1)S(1)} %shard_map.46.pack), custom_call_target="tpu_custom_call" | custom-call | tf_op jit(solution)/shard_map/pallas_call | solution.py:447
  2.0 0.6 %collective-permute-start.1 = (bf16[2,128,768]{2,1,0:T(8,128)(2,1)S(1)}, bf16[2,128,768]{2,1,0:T(8,128)(2,1)S(1)}, u32[]{:S(2)}, u32[]{:S(2)}) collective-permute-start(bf16[2,128,768]{2,1,0:T(8,128)(2,1)S(1)} %get-tuple-element.21.edge.refs_0_), channel_id=1, source_target_pairs={{0,1},{1,0},{2,3},{3,2},{4,5},{5,4},{6,7},{7,6},{8,9},{9,8},{10,11... | collective-permute-start | bytes 1179656 | tf_op jit(solution)/shard_map/ppermute | solution.py:479
  2.6 3.6 %collective-permute-start.2 = (bf16[5,128,128]{2,1,0:T(8,128)(2,1)S(1)}, bf16[5,128,128]{2,1,0:T(8,128)(2,1)S(1)}, u32[]{:S(2)}, u32[]{:S(2)}) collective-permute-start(bf16[5,128,128]{2,1,0:T(8,128)(2,1)S(1)} %shard_map.46.pack), channel_id=1, source_target_pairs={{0,6},{2,4},{4,2},{6,0},{8,14},{10,12},{12,10},{14,8},{1,7},{3,5},... | collective-permute-start | bytes 491528 | tf_op jit(solution)/shard_map/ppermute | solution.py:482
  6.8 4.4 %collective-permute-done.2.refs_3_ = bf16[5,128,128]{2,1,0:T(8,128)(2,1)S(1)} collective-permute-done((bf16[5,128,128]{2,1,0:T(8,128)(2,1)S(1)}, bf16[5,128,128]{2,1,0:T(8,128)(2,1)S(1)}, u32[]{:S(2)}, u32[]{:S(2)}) %collective-permute-start.2) | collective-permute-done | bytes 163872 | tf_op jit(solution)/shard_map/ppermute | solution.py:482
  11.2 3.4 %collective-permute-done.4.refs_5_ = bf16[5,128,128]{2,1,0:T(8,128)(2,1)S(1)} collective-permute-done((bf16[5,128,128]{2,1,0:T(8,128)(2,1)S(1)}, bf16[5,128,128]{2,1,0:T(8,128)(2,1)S(1)}, u32[]{:S(2)}, u32[]{:S(2)}) %collective-permute-start.4) | collective-permute-done | bytes 163872 | tf_op jit(solution)/shard_map/ppermute | solution.py:482
  14.7 0.5 %collective-permute-start.7 = (bf16[5,128,128]{2,1,0:T(8,128)(2,1)S(1)}, bf16[5,128,128]{2,1,0:T(8,128)(2,1)S(1)}, u32[]{:S(2)}, u32[]{:S(2)}) collective-permute-start(bf16[5,128,128]{2,1,0:T(8,128)(2,1)S(1)} %collective-permute-done.6.refs_0_), channel_id=1, source_target_pairs={{0,1},{1,0},{2,3},{3,2},{4,5},{5,4},{6,7},{7,6},{8,9},{9,8},{10,11... | collective-permute-start | bytes 491528 | tf_op jit(solution)/shard_map/ppermute | solution.py:479
  15.9 0.5 %shard_map.48.surfaces.refs_0_ = bf16[128,256]{1,0:T(8,128)(2,1)S(1)} custom-call(s32[8,128]{1,0:T(8,128)S(1)} %broadcast_in_dim.8.count, bf16[2,128,768]{2,1,0:T(8,128)(2,1)S(1)} %get-tuple-element.21.edge.refs_0_, bf16[2,128,768]{2,1,0:T(8,128)(2,1)S(1)} %collective-permute-done.1.edge_other.refs_1_, ...), custom_call_target="tpu_custom_call" | custom-call | tf_op jit(solution)/shard_map/pallas_call | solution.py:447
  16.4 1.0 %collective-permute-start.8 = (bf16[128,256]{1,0:T(8,128)(2,1)S(1)}, bf16[128,256]{1,0:T(8,128)(2,1)S(1)}, u32[]{:S(2)}, u32[]{:S(2)}) collective-permute-start(bf16[128,256]{1,0:T(8,128)(2,1)S(1)} %shard_map.48.surfaces.refs_0_), channel_id=1, source_target_pairs={{0,2},{2,0},{4,6},{6,4},{8,10},{10,8},{12,14},{14,12},{1,3},{3,1},... | collective-permute-start | bytes 196616 | tf_op jit(solution)/shard_map/ppermute | solution.py:482
  17.4 1.6 %collective-permute-start.9 = (bf16[128,256]{1,0:T(8,128)(2,1)S(1)}, bf16[128,256]{1,0:T(8,128)(2,1)S(1)}, u32[]{:S(2)}, u32[]{:S(2)}) collective-permute-start(bf16[128,256]{1,0:T(8,128)(2,1)S(1)} %shard_map.48.surfaces.refs_0_), channel_id=1, source_target_pairs={{0,4},{2,6},{4,0},{6,2},{8,12},{10,14},{12,8},{14,10},{1,5},{3,7},... | collective-permute-start | bytes 196616 | tf_op jit(solution)/shard_map/ppermute | solution.py:482
  18.9 1.0 %collective-permute-start.10 = (bf16[128,256]{1,0:T(8,128)(2,1)S(1)}, bf16[128,256]{1,0:T(8,128)(2,1)S(1)}, u32[]{:S(2)}, u32[]{:S(2)}) collective-permute-start(bf16[128,256]{1,0:T(8,128)(2,1)S(1)} %shard_map.48.surfaces.refs_0_), channel_id=1, source_target_pairs={{0,6},{2,4},{4,2},{6,0},{8,14},{10,12},{12,10},{14,8},{1,7},{3,5},... | collective-permute-start | bytes 196616 | tf_op jit(solution)/shard_map/ppermute | solution.py:482
  19.9 0.7 %shard_map.50._ = bf16[4,8,256,256]{3,2,1,0:T(8,128)(2,1)S(1)} custom-call(bf16[2,128,768]{2,1,0:T(8,128)(2,1)S(1)} %get-tuple-element.21.edge.refs_0_, bf16[2,128,768]{2,1,0:T(8,128)(2,1)S(1)} %collective-permute-done.1.edge_other.refs_1_, bf16[2,128,128]{2,1,0:T(8,128)(2,1)S(1)} %get-tuple-element.22.refs_2_.coupling, ...), custom_call_target="tpu_custom_call" | custom-call | tf_op jit(solution)/shard_map/pallas_call | solution.py:447
  20.7 0.5 %shard_map.51.forms = bf16[4,8,256,256]{3,2,1,0:T(8,128)(2,1)S(1)} custom-call(bf16[4,8,256,256]{3,2,1,0:T(8,128)(2,1)S(1)} %shard_map.50._, bf16[5,128,128]{2,1,0:T(8,128)(2,1)S(1)} %collective-permute-done.6.refs_0_, bf16[5,128,128]{2,1,0:T(8,128)(2,1)S(1)} %collective-permute-done.7.refs_1_), custom_call_target="tpu_custom_call", output_to_operand_aliasing={{}: (0, {})} | custom-call | tf_op jit(solution)/shard_map/pallas_call | solution.py:447
  21.2 0.6 %collective-permute-done.9.refs_2_ = bf16[128,256]{1,0:T(8,128)(2,1)S(1)} collective-permute-done((bf16[128,256]{1,0:T(8,128)(2,1)S(1)}, bf16[128,256]{1,0:T(8,128)(2,1)S(1)}, u32[]{:S(2)}, u32[]{:S(2)}) %collective-permute-start.9) | collective-permute-done | bytes 65568 | tf_op jit(solution)/shard_map/ppermute | solution.py:482
  21.8 2.4 %collective-permute-done.10.refs_3_ = bf16[128,256]{1,0:T(8,128)(2,1)S(1)} collective-permute-done((bf16[128,256]{1,0:T(8,128)(2,1)S(1)}, bf16[128,256]{1,0:T(8,128)(2,1)S(1)}, u32[]{:S(2)}, u32[]{:S(2)}) %collective-permute-start.10) | collective-permute-done | bytes 65568 | tf_op jit(solution)/shard_map/ppermute | solution.py:482
  24.1 2.1 %shard_map.52 = (bf16[128,256]{1,0:T(8,128)(2,1)S(1)}, bf16[64,256]{1,0:T(8,128)(2,1)S(1)}, f32[128,256]{1,0:T(8,128)S(1)}, f32[128,256]{1,0:T(8,128)}, f32[64,2...) custom-call(bf16[4,8,256,256]{3,2,1,0:T(8,128)(2,1)S(1)} %shard_map.51.forms, ...), custom_call_target="tpu_custom_call" | custom-call | tf_op jit(solution)/shard_map/pallas_call | solution.py:447
  26.2 2.6 %collective-permute-start.12 = (bf16[64,256]{1,0:T(8,128)(2,1)S(1)}, bf16[64,256]{1,0:T(8,128)(2,1)S(1)}, u32[]{:S(2)}, u32[]{:S(2)}) collective-permute-start(bf16[64,256]{1,0:T(8,128)(2,1)S(1)} %get-tuple-element.32), channel_id=1, source_target_pairs={{0,8},{2,10},{4,12},{6,14},{8,0},{10,2},{12,4},{14,6},{1,9},{3,11}... | collective-permute-start | bytes 98312 | tf_op jit(solution)/shard_map/ppermute | solution.py:482
  29.1 2.5 %collective-permute-done.12.map_seen = bf16[64,256]{1,0:T(8,128)(2,1)S(1)} collective-permute-done((bf16[64,256]{1,0:T(8,128)(2,1)S(1)}, bf16[64,256]{1,0:T(8,128)(2,1)S(1)}, u32[]{:S(2)}, u32[]{:S(2)}) %collective-permute-start.12) | collective-permute-done | bytes 32800 | tf_op jit(solution)/shard_map/ppermute | solution.py:482
  31.6 1.3 %shard_map.53 = (f32[128,256]{1,0:T(8,128)S(1)}, f32[128,256]{1,0:T(8,128)}) custom-call(bf16[4,8,256,256]{3,2,1,0:T(8,128)(2,1)S(1)} %shard_map.51.forms), custom_call_target="tpu_custom_call" | custom-call | tf_op jit(solution)/shard_map/pallas_call | solution.py:447
  33.2 0.5 %shard_map.55 = (f32[2,64,256]{2,1,0:T(8,128)S(1)}, bf16[2,256,256]{2,1,0:T(8,128)(2,1)S(1)}) custom-call(bf16[4,256,256]{2,1,0:T(8,128)(2,1)S(1)} %get-tuple-element.27.hand, f32[64,256]{1,0:T(8,128)S(1)} %get-tuple-element.28.base, f32[64,256]{1,0:T(8,128)S(1)} %get-tuple-element.29.pi, f32[128,256]{1,0:T(8,128)S(1)} %get-tuple-element.30.leaving, ...), custom_call_target="tpu_custom_call" | custom-call | tf_op jit(solution)/shard_map/pallas_call | solution.py:447
  33.7 1.6 %collective-permute-done.14.seen = bf16[128,256]{1,0:T(8,128)(2,1)S(1)} collective-permute-done((bf16[128,256]{1,0:T(8,128)(2,1)S(1)}, bf16[128,256]{1,0:T(8,128)(2,1)S(1)}, u32[]{:S(2)}, u32[]{:S(2)}) %collective-permute-start.14) | collective-permute-done | bytes 65568 | tf_op jit(solution)/shard_map/ppermute | solution.py:482
  35.7 0.5 %shard_map.49.direct = f32[384,256]{1,0:T(8,128)S(1)} custom-call(s32[8,128]{1,0:T(8,128)S(1)} %broadcast_in_dim.8.count, bf16[2,384,768]{2,1,0:T(8,128)(2,1)S(1)} %copy-done, bf16[2,384,128]{2,1,0:T(8,128)(2,1)S(1)} %get-tuple-element.20.source_own, bf16[2,384,128]{2,1,0:T(8,128)(2,1)S(1)} %collective-permute-done.source_other, ...), custom_call_target="tpu_custom_call" | custom-call | tf_op jit(solution)/shard_map/pallas_call | solution.py:447
  36.2 0.7 %collective-permute-done.15.other = bf16[128,256]{1,0:T(8,128)(2,1)S(1)} collective-permute-done((bf16[128,256]{1,0:T(8,128)(2,1)S(1)}, bf16[128,256]{1,0:T(8,128)(2,1)S(1)}, u32[]{:S(2)}, u32[]{:S(2)}) %collective-permute-start.15) | collective-permute-done | bytes 65568 | tf_op jit(solution)/shard_map/ppermute | solution.py:479
  37.0 1.1 %shard_map.57 = f32[2,384,128]{2,1,0:T(8,128)} custom-call(s32[8,128]{1,0:T(8,128)S(1)} %broadcast_in_dim.8.count, bf16[2,384,768]{2,1,0:T(8,128)(2,1)S(1)} %copy-done, f32[384,256]{1,0:T(8,128)S(1)} %shard_map.49.direct, bf16[128,256]{1,0:T(8,128)(2,1)S(1)} %shard_map.56.own, bf16[128,256]{1,0:T(8,128)(2,1)S(1)} %collective-permute-done.15.other), custom_call_target="tpu_custom_call" | custom-call | tf_op jit(solution)/shard_map/pallas_call | solution.py:447
  (24 shorter events, 1.7 us)
Async XLA Ops:
  2.0 13.8 %collective-permute-start.1 = (bf16[2,128,768]{2,1,0:T(8,128)(2,1)S(1)}, bf16[2,128,768]{2,1,0:T(8,128)(2,1)S(1)}, u32[]{:S(2)}, u32[]{:S(2)}) collective-permute-start(bf16[2,128,768]{2,1,0:T(8,128)(2,1)S(1)} %get-tuple-element.21.edge.refs_0_), channel_id=1, source_target_pairs={{0,1},{1,0},{2,3},{3,2},{4,5},{5,4},{6,7},{7,6},{8,9},{9,8},{10,11... | collective-permute-start | bytes 1179656 | tf_op jit(solution)/shard_map/ppermute | solution.py:479
  2.6 8.7 %collective-permute-start.2 = (bf16[5,128,128]{2,1,0:T(8,128)(2,1)S(1)}, bf16[5,128,128]{2,1,0:T(8,128)(2,1)S(1)}, u32[]{:S(2)}, u32[]{:S(2)}) collective-permute-start(bf16[5,128,128]{2,1,0:T(8,128)(2,1)S(1)} %shard_map.46.pack), channel_id=1, source_target_pairs={{0,6},{2,4},{4,2},{6,0},{8,14},{10,12},{12,10},{14,8},{1,7},{3,5},... | collective-permute-start | bytes 491528 | tf_op jit(solution)/shard_map/ppermute | solution.py:482
  6.2 8.5 %collective-permute-start.4 = (bf16[5,128,128]{2,1,0:T(8,128)(2,1)S(1)}, bf16[5,128,128]{2,1,0:T(8,128)(2,1)S(1)}, u32[]{:S(2)}, u32[]{:S(2)}) collective-permute-start(bf16[5,128,128]{2,1,0:T(8,128)(2,1)S(1)} %shard_map.46.pack), channel_id=1, source_target_pairs={{0,4},{2,6},{4,0},{6,2},{8,12},{10,14},{12,8},{14,10},{1,5},{3,7},... | collective-permute-start | bytes 491528 | tf_op jit(solution)/shard_map/ppermute | solution.py:482
  6.6 8.1 %collective-permute-start.6 = (bf16[5,128,128]{2,1,0:T(8,128)(2,1)S(1)}, bf16[5,128,128]{2,1,0:T(8,128)(2,1)S(1)}, u32[]{:S(2)}, u32[]{:S(2)}) collective-permute-start(bf16[5,128,128]{2,1,0:T(8,128)(2,1)S(1)} %shard_map.46.pack), channel_id=1, source_target_pairs={{0,2},{2,0},{4,6},{6,4},{8,10},{10,8},{12,14},{14,12},{1,3},{3,1},... | collective-permute-start | bytes 491528 | tf_op jit(solution)/shard_map/ppermute | solution.py:482
  6.8 9.0 %collective-permute-start = (bf16[2,384,128]{2,1,0:T(8,128)(2,1)}, bf16[2,384,128]{2,1,0:T(8,128)(2,1)S(1)}, u32[]{:S(2)}, u32[]{:S(2)}) collective-permute-start(bf16[2,384,128]{2,1,0:T(8,128)(2,1)} %source.1), channel_id=1, source_target_pairs={{0,1},{1,0},{2,3},{3,2},{4,5},{5,4},{6,7},{7,6},{8,9},{9,8},{10,11... | collective-permute-start | bytes 589832 | tf_op jit(solution)/shard_map/ppermute | solution.py:479
  11.2 7.7 %collective-permute-start.3 = (bf16[5,128,128]{2,1,0:T(8,128)(2,1)S(1)}, bf16[5,128,128]{2,1,0:T(8,128)(2,1)S(1)}, u32[]{:S(2)}, u32[]{:S(2)}) collective-permute-start(bf16[5,128,128]{2,1,0:T(8,128)(2,1)S(1)} %collective-permute-done.2.refs_3_), channel_id=1, source_target_pairs={{0,1},{1,0},{2,3},{3,2},{4,5},{5,4},{6,7},{7,6},{8,9},{9,8},{10,11... | collective-permute-start | bytes 491528 | tf_op jit(solution)/shard_map/ppermute | solution.py:479
  14.7 5.3 %collective-permute-start.5 = (bf16[5,128,128]{2,1,0:T(8,128)(2,1)S(1)}, bf16[5,128,128]{2,1,0:T(8,128)(2,1)S(1)}, u32[]{:S(2)}, u32[]{:S(2)}) collective-permute-start(bf16[5,128,128]{2,1,0:T(8,128)(2,1)S(1)} %collective-permute-done.4.refs_5_), channel_id=1, source_target_pairs={{0,1},{1,0},{2,3},{3,2},{4,5},{5,4},{6,7},{7,6},{8,9},{9,8},{10,11... | collective-permute-start | bytes 491528 | tf_op jit(solution)/shard_map/ppermute | solution.py:479
  14.7 6.0 %collective-permute-start.7 = (bf16[5,128,128]{2,1,0:T(8,128)(2,1)S(1)}, bf16[5,128,128]{2,1,0:T(8,128)(2,1)S(1)}, u32[]{:S(2)}, u32[]{:S(2)}) collective-permute-start(bf16[5,128,128]{2,1,0:T(8,128)(2,1)S(1)} %collective-permute-done.6.refs_0_), channel_id=1, source_target_pairs={{0,1},{1,0},{2,3},{3,2},{4,5},{5,4},{6,7},{7,6},{8,9},{9,8},{10,11... | collective-permute-start | bytes 491528 | tf_op jit(solution)/shard_map/ppermute | solution.py:479
  16.4 4.8 %collective-permute-start.8 = (bf16[128,256]{1,0:T(8,128)(2,1)S(1)}, bf16[128,256]{1,0:T(8,128)(2,1)S(1)}, u32[]{:S(2)}, u32[]{:S(2)}) collective-permute-start(bf16[128,256]{1,0:T(8,128)(2,1)S(1)} %shard_map.48.surfaces.refs_0_), channel_id=1, source_target_pairs={{0,2},{2,0},{4,6},{6,4},{8,10},{10,8},{12,14},{14,12},{1,3},{3,1},... | collective-permute-start | bytes 196616 | tf_op jit(solution)/shard_map/ppermute | solution.py:482
  17.4 4.4 %collective-permute-start.9 = (bf16[128,256]{1,0:T(8,128)(2,1)S(1)}, bf16[128,256]{1,0:T(8,128)(2,1)S(1)}, u32[]{:S(2)}, u32[]{:S(2)}) collective-permute-start(bf16[128,256]{1,0:T(8,128)(2,1)S(1)} %shard_map.48.surfaces.refs_0_), channel_id=1, source_target_pairs={{0,4},{2,6},{4,0},{6,2},{8,12},{10,14},{12,8},{14,10},{1,5},{3,7},... | collective-permute-start | bytes 196616 | tf_op jit(solution)/shard_map/ppermute | solution.py:482
  18.9 5.2 %collective-permute-start.10 = (bf16[128,256]{1,0:T(8,128)(2,1)S(1)}, bf16[128,256]{1,0:T(8,128)(2,1)S(1)}, u32[]{:S(2)}, u32[]{:S(2)}) collective-permute-start(bf16[128,256]{1,0:T(8,128)(2,1)S(1)} %shard_map.48.surfaces.refs_0_), channel_id=1, source_target_pairs={{0,6},{2,4},{4,2},{6,0},{8,14},{10,12},{12,10},{14,8},{1,7},{3,5},... | collective-permute-start | bytes 196616 | tf_op jit(solution)/shard_map/ppermute | solution.py:482
  26.2 9.6 %copy-start = (bf16[2,384,768]{2,1,0:T(8,128)(2,1)S(1)}, bf16[2,384,768]{2,1,0:T(8,128)(2,1)}, u32[]{:S(2)}) copy-start(bf16[2,384,768]{2,1,0:T(8,128)(2,1)} %green.7) | copy-start | bytes 3538948
  26.2 6.7 %collective-permute-start.11 = (f32[128,256]{1,0:T(8,128)S(1)}, f32[128,256]{1,0:T(8,128)S(1)}, u32[]{:S(2)}, u32[]{:S(2)}) collective-permute-start(f32[128,256]{1,0:T(8,128)S(1)} %get-tuple-element.24.response), channel_id=1, source_target_pairs={{0,1},{1,0},{2,3},{3,2},{4,5},{5,4},{6,7},{7,6},{8,9},{9,8},{10,11... | collective-permute-start | bytes 393224 | tf_op jit(solution)/shard_map/ppermute | solution.py:479
  26.2 5.4 %collective-permute-start.12 = (bf16[64,256]{1,0:T(8,128)(2,1)S(1)}, bf16[64,256]{1,0:T(8,128)(2,1)S(1)}, u32[]{:S(2)}, u32[]{:S(2)}) collective-permute-start(bf16[64,256]{1,0:T(8,128)(2,1)S(1)} %get-tuple-element.32), channel_id=1, source_target_pairs={{0,8},{2,10},{4,12},{6,14},{8,0},{10,2},{12,4},{14,6},{1,9},{3,11}... | collective-permute-start | bytes 98312 | tf_op jit(solution)/shard_map/ppermute | solution.py:482
  28.8 6.5 %collective-permute-start.14 = (bf16[128,256]{1,0:T(8,128)(2,1)S(1)}, bf16[128,256]{1,0:T(8,128)(2,1)S(1)}, u32[]{:S(2)}, u32[]{:S(2)}) collective-permute-start(bf16[128,256]{1,0:T(8,128)(2,1)S(1)} %get-tuple-element.31), channel_id=1, source_target_pairs={{0,8},{2,10},{4,12},{6,14},{8,0},{10,2},{12,4},{14,6},{1,9},{3,11}... | collective-permute-start | bytes 196616 | tf_op jit(solution)/shard_map/ppermute | solution.py:482
  31.6 1.6 %collective-permute-start.13 = (bf16[64,256]{1,0:T(8,128)(2,1)S(1)}, bf16[64,256]{1,0:T(8,128)(2,1)S(1)}, u32[]{:S(2)}, u32[]{:S(2)}) collective-permute-start(bf16[64,256]{1,0:T(8,128)(2,1)S(1)} %collective-permute-done.12.map_seen), channel_id=1, source_target_pairs={{0,1},{1,0},{2,3},{3,2},{4,5},{5,4},{6,7},{7,6},{8,9},{9,8},{10,11... | collective-permute-start | bytes 98312 | tf_op jit(solution)/shard_map/ppermute | solution.py:479
  35.6 1.3 %collective-permute-start.15 = (bf16[128,256]{1,0:T(8,128)(2,1)S(1)}, bf16[128,256]{1,0:T(8,128)(2,1)S(1)}, u32[]{:S(2)}, u32[]{:S(2)}) collective-permute-start(bf16[128,256]{1,0:T(8,128)(2,1)S(1)} %shard_map.56.own), channel_id=1, source_target_pairs={{0,1},{1,0},{2,3},{3,2},{4,5},{5,4},{6,7},{7,6},{8,9},{9,8},{10,11... | collective-permute-start | bytes 196616 | tf_op jit(solution)/shard_map/ppermute | solution.py:479
